TPU v7x, 32 devices: a whole 2x2x4 slice. The times are simulated.
32 devices in a mesh: seq: 2 (over y), head: 4 (over x, core), ctx: 4 (over z).
Axes of the slice: x: 2, y: 2, z: 4, core: 2. Of those that a mesh axis runs over, the one named last changes fastest.
Arguments:
- tokens: bfloat16 [16384, 768], P(('seq', 'head', 'ctx')), may hold values from -6 to 6
- segment_ids: int32 [16384], P(('seq', 'head', 'ctx')), may hold values from -1 to 3, as said below
- w_qkv: bfloat16 [768, 2304], P(('seq', 'head', 'ctx')), may hold values from -0.21875 to 0.21875
- w_out: bfloat16 [768, 768], P(('seq', 'head', 'ctx')), may hold values from -6 to 6
- w_up: bfloat16 [768, 3072], P(('seq', 'head', 'ctx')), may hold values from -0.21875 to 0.21875
- w_down: bfloat16 [3072, 768], P(('seq', 'head', 'ctx')), may hold values from -0.109375 to 0.109375
- gain_one: bfloat16 [768], P(('seq', 'head', 'ctx')), may hold values from 0.5 to 1.5
- bias_one: bfloat16 [768], P(('seq', 'head', 'ctx')), may hold values from -3 to 3
- gain_two: bfloat16 [768], P(('seq', 'head', 'ctx')), may hold values from 0.5 to 1.5
- bias_two: bfloat16 [768], P(('seq', 'head', 'ctx')), may hold values from -3 to 3
- cotangent: bfloat16 [16384, 768], P(('seq', 'head', 'ctx')), may hold values from -6 to 6
Outputs:
- output: bfloat16 [16384, 768], P(('seq', 'head', 'ctx'))
- grad_tokens: bfloat16 [16384, 768], P(('seq', 'head', 'ctx'))
- grad_w_qkv: float32 [768, 2304], P(('seq', 'head', 'ctx'))
- grad_w_out: float32 [768, 768], P(('seq', 'head', 'ctx'))
- grad_w_up: float32 [768, 3072], P(('seq', 'head', 'ctx'))
- grad_w_down: float32 [3072, 768], P(('seq', 'head', 'ctx'))
- grad_gain_one: float32 [768], P(('seq', 'head', 'ctx'))
- grad_bias_one: float32 [768], P(('seq', 'head', 'ctx'))
- grad_gain_two: float32 [768], P(('seq', 'head', 'ctx'))
- grad_bias_two: float32 [768], P(('seq', 'head', 'ctx'))
Inputs may be any that keep to these rules, and one draw needn't show every extreme that they name: `segment_ids`: within each sequence of 8192 tokens the ids start at 0 and never fall before the trailing padding; a scene is made of whole views of 1024 tokens (the last one possibly cut by the padding) and has at most 5 views; the padding is a tail of 1 to min(512, 1023) tokens of each sequence.
All inputs are finite; a program needn't handle non-finite values.
Results may differ from a plain program's by a relative error of at most 0.023.
Values may be sent and summed in bfloat16 or wider, within the bound.
No kernel may reach another device: no remote copies, remote signals or barrier semaphores. Data moves between devices by JAX's collectives and lax.ppermute only.
A program may use at most 192 MiB of HBM per device.

v0:
```python
from functools import partial

import jax
import jax.numpy as jnp
from jax import lax
from jax.sharding import PartitionSpec as P

D = 768
HEADS = 12
HDIM = 64


EPSILON = 1e-05
MASKED = -1e30


def norm_rows(values, gain_vec, bias_vec):
    row_mean = jnp.mean(values, axis=-1, keepdims=True)
    centered = values - row_mean
    variance = jnp.mean(centered * centered, axis=-1, keepdims=True)
    inv_rows = lax.rsqrt(variance + EPSILON)
    unit_rows = centered * inv_rows
    return (
        unit_rows * gain_vec.astype(jnp.float32) + bias_vec.astype(jnp.float32),
        unit_rows,
        inv_rows,
    )


def norm_back(grad_norm, unit_rows, inv_rows, gain_vec):
    scaled = grad_norm * gain_vec.astype(jnp.float32)
    return inv_rows * (
        scaled
        - jnp.mean(scaled, axis=-1, keepdims=True)
        - unit_rows * jnp.mean(scaled * unit_rows, axis=-1, keepdims=True)
    )


def gelu_exact(values):
    return jax.nn.gelu(values, approximate=False)


def key_rows():
    return 512


def fold_keys(q_blocks, id_blocks, score_scale, state_now, key_piece, first_row):
    kv_piece, kid_piece = key_piece
    piece_rows = kv_piece.shape[0]
    per_group = q_blocks.shape[2]
    block_rows = key_rows()
    kv_blocks = kv_piece.reshape(piece_rows // block_rows, block_rows, per_group, 2, HDIM)
    kid_blocks = kid_piece.reshape(piece_rows // block_rows, block_rows)

    def fold_over_keys(state_in, key_block):
        kv_now, kid_now = key_block

        def fold_over_queries(query_item):
            queries, query_ids, row_max, row_sum, weighted = query_item
            scores = (
                jnp.einsum(
                    "qhd,khd->qhk", queries, kv_now[:, :, 0], preferred_element_type=jnp.float32
                )
                * score_scale
            )
            same_scene = (query_ids[:, None] == kid_now[None, :])[:, None, :]
            new_max = jnp.maximum(row_max, jnp.max(jnp.where(same_scene, scores, MASKED), axis=-1))
            weights = jnp.where(same_scene, jnp.exp(scores - new_max[..., None]), 0.0)
            shrink = jnp.exp(row_max - new_max)
            row_sum = row_sum * shrink + jnp.sum(weights, axis=-1)
            weighted = weighted * shrink[..., None] + jnp.einsum(
                "qhk,khd->qhd",
                weights.astype(jnp.bfloat16),
                kv_now[:, :, 1],
                preferred_element_type=jnp.float32,
            )
            return (new_max, row_sum, weighted)

        return (lax.map(fold_over_queries, (q_blocks, id_blocks) + state_in), None)

    state_out, ignored = lax.scan(fold_over_keys, state_now, (kv_blocks, kid_blocks))
    return state_out


def attend_back(
    q_blocks, id_blocks, grad_blocks, lse_blocks, delta_blocks, keys_all, kid_all, score_scale
):
    piece_rows = keys_all.shape[0]
    per_group = q_blocks.shape[2]
    block_rows = key_rows()
    kv_blocks = keys_all.reshape(piece_rows // block_rows, block_rows, per_group, 2, HDIM)
    kid_blocks = kid_all.reshape(piece_rows // block_rows, block_rows)

    def attend_over_keys(grad_query, key_block):
        kv_now, kid_now = key_block
        keys_now = kv_now[:, :, 0]
        values_now = kv_now[:, :, 1]

        def attend_over_queries(grad_pair, query_item):
            grad_key, grad_value = grad_pair
            queries, query_ids, grad_attn, log_total, delta_rows = query_item
            scores = (
                jnp.einsum("qhd,khd->qhk", queries, keys_now, preferred_element_type=jnp.float32)
                * score_scale
            )
            same_scene = (query_ids[:, None] == kid_now[None, :])[:, None, :]
            probs_now = jnp.where(same_scene, jnp.exp(scores - log_total[..., None]), 0.0)
            grad_value = grad_value + jnp.einsum(
                "qhk,qhd->khd",
                probs_now.astype(jnp.bfloat16),
                grad_attn,
                preferred_element_type=jnp.float32,
            )
            grad_prob = jnp.einsum(
                "qhd,khd->qhk", grad_attn, values_now, preferred_element_type=jnp.float32
            )
            grad_score = (probs_now * (grad_prob - delta_rows[..., None])).astype(jnp.bfloat16)
            query_part = (
                jnp.einsum("qhk,khd->qhd", grad_score, keys_now, preferred_element_type=jnp.float32)
                * score_scale
            )
            grad_key = (
                grad_key
                + jnp.einsum(
                    "qhk,qhd->khd", grad_score, queries, preferred_element_type=jnp.float32
                )
                * score_scale
            )
            return ((grad_key, grad_value), query_part)

        zero_keys = jnp.zeros(keys_now.shape, jnp.float32)
        key_pair, query_parts = lax.scan(
            attend_over_queries,
            (zero_keys, zero_keys),
            (q_blocks, id_blocks, grad_blocks, lse_blocks, delta_blocks),
        )
        return (grad_query + query_parts, jnp.stack([key_pair[0], key_pair[1]], axis=2))

    grad_query, grad_kv = lax.scan(
        attend_over_keys, jnp.zeros(q_blocks.shape, jnp.float32), (kv_blocks, kid_blocks)
    )
    return (grad_query, grad_kv.reshape(piece_rows, per_group * 2 * HDIM))


def body(
    tokens,
    segment_ids,
    w_qkv,
    w_out,
    w_up,
    w_down,
    gain_one,
    bias_one,
    gain_two,
    bias_two,
    cotangent,
):
    heads_ax = lax.axis_size("head")
    tok_rows = tokens.shape[0]
    per_group = HEADS // heads_ax
    score_scale = HDIM ** (-0.5)
    gathered = (
        lax.all_gather(w_qkv, ("seq", "head", "ctx"), axis=0, tiled=True),
        lax.all_gather(w_out, ("seq", "head", "ctx"), axis=0, tiled=True),
        lax.all_gather(w_up, ("seq", "head", "ctx"), axis=0, tiled=True),
        lax.all_gather(w_down, ("seq", "head", "ctx"), axis=0, tiled=True),
        lax.all_gather(gain_one, ("seq", "head", "ctx"), axis=0, tiled=True),
        lax.all_gather(bias_one, ("seq", "head", "ctx"), axis=0, tiled=True),
        lax.all_gather(gain_two, ("seq", "head", "ctx"), axis=0, tiled=True),
        lax.all_gather(bias_two, ("seq", "head", "ctx"), axis=0, tiled=True),
    )
    (
        full_qkv,
        full_out,
        full_up,
        full_down,
        full_gain_one,
        full_bias_one,
        full_gain_two,
        full_bias_two,
    ) = gathered
    inputs = tokens.astype(jnp.float32)
    normed_one, unit_one, inv_one = norm_rows(inputs, full_gain_one, full_bias_one)
    h_one = normed_one.astype(jnp.bfloat16)
    qkv = jnp.dot(h_one, full_qkv, preferred_element_type=jnp.float32).astype(jnp.bfloat16)
    head_local = lax.all_to_all(
        qkv.reshape(tok_rows, heads_ax, per_group * 3 * HDIM),
        "head",
        split_axis=1,
        concat_axis=0,
        tiled=True,
    )
    head_rows = head_local.shape[0]
    head_local = head_local.reshape(head_rows, per_group, 3, HDIM)
    queries = head_local[:, :, 0]
    key_vals = head_local[:, :, 1:].reshape(head_rows, per_group * 2 * HDIM)
    query_ids = lax.all_gather(segment_ids, "head", axis=0, tiled=True)
    query_rows = min(512, head_rows)
    query_count = head_rows // query_rows
    q_blocks = queries.reshape(query_count, query_rows, per_group, HDIM)
    id_blocks = query_ids.reshape(query_count, query_rows)
    start_state = (
        jnp.full((query_count, query_rows, per_group), MASKED, jnp.float32),
        jnp.zeros((query_count, query_rows, per_group), jnp.float32),
        jnp.zeros((query_count, query_rows, per_group, HDIM), jnp.float32),
    )
    fold_fn = partial(fold_keys, q_blocks, id_blocks, score_scale)
    state_end = fold_fn(
        start_state,
        (
            lax.all_gather(key_vals, "ctx", axis=0, tiled=True),
            lax.all_gather(query_ids, "ctx", axis=0, tiled=True),
        ),
        jnp.int32(0),
    )
    row_max, row_sum, weighted = state_end
    attended = (weighted / row_sum[..., None]).reshape(head_rows, per_group, HDIM)
    log_total = row_max + jnp.log(row_sum)
    merged = lax.all_to_all(
        attended.astype(jnp.bfloat16).reshape(heads_ax, tok_rows, per_group * HDIM),
        "head",
        split_axis=0,
        concat_axis=2,
        tiled=True,
    ).reshape(tok_rows, D)
    y_one = inputs + jnp.dot(merged, full_out, preferred_element_type=jnp.float32)
    normed_two, unit_two, inv_two = norm_rows(y_one, full_gain_two, full_bias_two)
    h_two = normed_two.astype(jnp.bfloat16)
    up_proj = jnp.dot(h_two, full_up, preferred_element_type=jnp.float32)
    hidden = gelu_exact(up_proj).astype(jnp.bfloat16)
    output = (y_one + jnp.dot(hidden, full_down, preferred_element_type=jnp.float32)).astype(
        jnp.bfloat16
    )
    grad_w_down = jnp.einsum("tf,td->fd", hidden, cotangent, preferred_element_type=jnp.float32)
    grad_hidden = jnp.einsum("td,fd->tf", cotangent, full_down, preferred_element_type=jnp.float32)
    grad_up = jax.vjp(gelu_exact, up_proj)[1](grad_hidden)[0].astype(jnp.bfloat16)
    grad_w_up = jnp.einsum("td,tf->df", h_two, grad_up, preferred_element_type=jnp.float32)
    grad_h_two = jnp.einsum("tf,df->td", grad_up, full_up, preferred_element_type=jnp.float32)
    grad_gain_two = jnp.sum(grad_h_two * unit_two, axis=0)
    grad_bias_two = jnp.sum(grad_h_two, axis=0)
    grad_y_one = cotangent.astype(jnp.float32) + norm_back(
        grad_h_two, unit_two, inv_two, full_gain_two
    )
    grad_z = grad_y_one.astype(jnp.bfloat16)
    grad_w_out = jnp.einsum("ta,td->ad", merged, grad_z, preferred_element_type=jnp.float32)
    grad_merged = jnp.einsum(
        "td,ad->ta", grad_z, full_out, preferred_element_type=jnp.float32
    ).astype(jnp.bfloat16)
    grad_local = lax.all_to_all(
        grad_merged.reshape(tok_rows, heads_ax, per_group * HDIM),
        "head",
        split_axis=1,
        concat_axis=0,
        tiled=True,
    ).reshape(head_rows, per_group, HDIM)
    delta_rows = jnp.sum(grad_local.astype(jnp.float32) * attended, axis=-1)
    keys_back = (
        lax.all_gather(key_vals, "ctx", axis=0, tiled=True),
        lax.all_gather(query_ids, "ctx", axis=0, tiled=True),
    )
    grad_blocks = grad_local.reshape(query_count, query_rows, per_group, HDIM)
    delta_blocks = delta_rows.reshape(query_count, query_rows, per_group)
    grad_query, grad_kv = attend_back(
        q_blocks,
        id_blocks,
        grad_blocks,
        log_total,
        delta_blocks,
        keys_back[0],
        keys_back[1],
        score_scale,
    )
    grad_kv_own = lax.psum_scatter(
        grad_kv.astype(jnp.bfloat16), "ctx", scatter_dimension=0, tiled=True
    ).astype(jnp.float32)
    grad_local_qkv = jnp.concatenate(
        [
            grad_query.reshape(head_rows, per_group, 1, HDIM),
            grad_kv_own.reshape(head_rows, per_group, 2, HDIM),
        ],
        axis=2,
    )
    grad_local_qkv = grad_local_qkv.astype(jnp.bfloat16)
    grad_qkv = lax.all_to_all(
        grad_local_qkv.reshape(heads_ax, tok_rows, per_group * 3 * HDIM),
        "head",
        split_axis=0,
        concat_axis=2,
        tiled=True,
    ).reshape(tok_rows, 3 * D)
    grad_w_qkv = jnp.einsum("td,tc->dc", h_one, grad_qkv, preferred_element_type=jnp.float32)
    grad_h_one = jnp.einsum("tc,dc->td", grad_qkv, full_qkv, preferred_element_type=jnp.float32)
    grad_gain_one = jnp.sum(grad_h_one * unit_one, axis=0)
    grad_bias_one = jnp.sum(grad_h_one, axis=0)
    grad_tokens = (grad_y_one + norm_back(grad_h_one, unit_one, inv_one, full_gain_one)).astype(
        jnp.bfloat16
    )
    summed = (
        lax.psum_scatter(grad_w_qkv, ("seq", "head", "ctx"), scatter_dimension=0, tiled=True),
        lax.psum_scatter(grad_w_out, ("seq", "head", "ctx"), scatter_dimension=0, tiled=True),
        lax.psum_scatter(grad_w_up, ("seq", "head", "ctx"), scatter_dimension=0, tiled=True),
        lax.psum_scatter(grad_w_down, ("seq", "head", "ctx"), scatter_dimension=0, tiled=True),
        lax.psum_scatter(grad_gain_one, ("seq", "head", "ctx"), scatter_dimension=0, tiled=True),
        lax.psum_scatter(grad_bias_one, ("seq", "head", "ctx"), scatter_dimension=0, tiled=True),
        lax.psum_scatter(grad_gain_two, ("seq", "head", "ctx"), scatter_dimension=0, tiled=True),
        lax.psum_scatter(grad_bias_two, ("seq", "head", "ctx"), scatter_dimension=0, tiled=True),
    )
    return (
        output,
        grad_tokens,
        summed[0],
        summed[1],
        summed[2],
        summed[3],
        summed[4],
        summed[5],
        summed[6],
        summed[7],
    )


def solution(mesh):
    placed = (
        P(("seq", "head", "ctx"), None),
        P(("seq", "head", "ctx")),
        P(("seq", "head", "ctx"), None),
        P(("seq", "head", "ctx"), None),
        P(("seq", "head", "ctx"), None),
        P(("seq", "head", "ctx"), None),
        P(("seq", "head", "ctx")),
        P(("seq", "head", "ctx")),
        P(("seq", "head", "ctx")),
        P(("seq", "head", "ctx")),
        P(("seq", "head", "ctx"), None),
    )
    return jax.shard_map(
        body,
        mesh=mesh,
        in_specs=placed,
        out_specs=(
            P(("seq", "head", "ctx"), None),
            P(("seq", "head", "ctx"), None),
            P(("seq", "head", "ctx"), None),
            P(("seq", "head", "ctx"), None),
            P(("seq", "head", "ctx"), None),
            P(("seq", "head", "ctx"), None),
            P(("seq", "head", "ctx")),
            P(("seq", "head", "ctx")),
            P(("seq", "head", "ctx")),
            P(("seq", "head", "ctx")),
        ),
        check_vma=False,
    )
```

profile of v0, /device:TPU:0, one launch (start us, length us, event | category | flops | bytes accessed | tf_op | source)
XLA Modules:
  0.0 1802.7 jit_solution(5511258278516865616)
XLA Ops:
  11.3 42.2 %all-reduce.9 = (bf16[768]{0:T(1024)(128)(2,1)S(1)}, bf16[768]{0:T(1024)(128)(2,1)S(1)}, bf16[768]{0:T(1024)(128)(2,1)S(1)}, bf16[768]{0:T(1024)(128)(2,1)S(1)}) all-reduce(bf16[768]{0:T(1024)(128)(2,1)S(1)} %dynamic-update-slice.1, ...), channel_id=1, replica_groups=mesh['seq'=2,'head'=4,'ctx'=4] {'seq','head','ctx'}, use_global_device_ids=true, to_apply=%add.1 | all-reduce | flops 3072 | bytes 12288
  146.4 91.1 %all-gather.9.cloned.1.call-done = bf16[8192,384]{0,1:T(8,128)(2,1)} async-done(((bf16[2048,384]{0,1:T(8,128)(2,1)}), bf16[8192,384]{0,1:T(8,128)(2,1)}) %all-gather.9.cloned.1.call-update) | async-done | bytes 6291472 | tf_op jit(solution)/shard_map/all_gather | solution.py:211
  249.7 187.3 %while.65 = (s32[]{:T(128)}, f32[4,512,3]{1,2,0:T(4,128)S(1)}, f32[4,512,3]{1,2,0:T(4,128)S(1)}, f32[4,512,3,64]{1,3,2,0:T(8,128)S(1)}, bf16[16,512,3,2,64]{1,4,...) while((s32[]{:T(128)}, f32[4,512,3]{1,2,0:T(4,128)S(1)}, ...), condition=%wide.region_7.8_spmd.clone, body=%wide.region_2.7_spmd.sunk.clone | while | flops 210442240 | bytes 13556034 | solution.py:81
  510.9 645.9 %while.67 = (s32[]{:T(128)}, f32[4,512,3,64]{1,3,2,0:T(8,128)}, bf16[16,512,3,2,64]{1,4,2,3,0:T(8,128)(2,1)}, bf16[16,512,3,2,64]{1,4,2,3,0:T(8,128)(2,1)}, s32[...) while((s32[]{:T(128)}, f32[4,512,3,64]{1,3,2,0:T(8,128)}, ...), condition=%wide.region_16.17_spmd.clone.clone, body=%wide.region_13.16_spmd.clone.sunk.clone | while | flops 513605632 | bytes 39967228 | solution.py:139
  512.0 35.0 %while.66 = (s32[]{:T(128)}, f32[512,3,64]{0,2,1:T(8,128)S(1)}, f32[512,3,64]{0,2,1:T(8,128)}, f32[4,512,3,64]{1,3,2,0:T(8,128)}, bf16[4,512,3,64]{1,3,2,0:T(8,1...) while((s32[]{:T(128)}, f32[512,3,64]{0,2,1:T(8,128)S(1)}, ...), condition=%wide.region_15.15_spmd.clone, body=%wide.region_14.14_spmd.clone.sunk | while | flops 512032768 | bytes 30918864 | solution.py:132
  592.3 35.0 %while.66 = (s32[]{:T(128)}, f32[512,3,64]{0,2,1:T(8,128)S(1)}, f32[512,3,64]{0,2,1:T(8,128)}, f32[4,512,3,64]{1,3,2,0:T(8,128)}, bf16[4,512,3,64]{1,3,2,0:T(8,1...) while((s32[]{:T(128)}, f32[512,3,64]{0,2,1:T(8,128)S(1)}, ...), condition=%wide.region_15.15_spmd.clone, body=%wide.region_14.14_spmd.clone.sunk | while | flops 512032768 | bytes 30918864 | solution.py:132
  632.7 35.0 %while.66 = (s32[]{:T(128)}, f32[512,3,64]{0,2,1:T(8,128)S(1)}, f32[512,3,64]{0,2,1:T(8,128)}, f32[4,512,3,64]{1,3,2,0:T(8,128)}, bf16[4,512,3,64]{1,3,2,0:T(8,1...) while((s32[]{:T(128)}, f32[512,3,64]{0,2,1:T(8,128)S(1)}, ...), condition=%wide.region_15.15_spmd.clone, body=%wide.region_14.14_spmd.clone.sunk | while | flops 512032768 | bytes 30918864 | solution.py:132
  673.0 35.0 %while.66 = (s32[]{:T(128)}, f32[512,3,64]{0,2,1:T(8,128)S(1)}, f32[512,3,64]{0,2,1:T(8,128)}, f32[4,512,3,64]{1,3,2,0:T(8,128)}, bf16[4,512,3,64]{1,3,2,0:T(8,1...) while((s32[]{:T(128)}, f32[512,3,64]{0,2,1:T(8,128)S(1)}, ...), condition=%wide.region_15.15_spmd.clone, body=%wide.region_14.14_spmd.clone.sunk | while | flops 512032768 | bytes 30918864 | solution.py:132
  713.4 35.0 %while.66 = (s32[]{:T(128)}, f32[512,3,64]{0,2,1:T(8,128)S(1)}, f32[512,3,64]{0,2,1:T(8,128)}, f32[4,512,3,64]{1,3,2,0:T(8,128)}, bf16[4,512,3,64]{1,3,2,0:T(8,1...) while((s32[]{:T(128)}, f32[512,3,64]{0,2,1:T(8,128)S(1)}, ...), condition=%wide.region_15.15_spmd.clone, body=%wide.region_14.14_spmd.clone.sunk | while | flops 512032768 | bytes 30918864 | solution.py:132
  753.8 35.0 %while.66 = (s32[]{:T(128)}, f32[512,3,64]{0,2,1:T(8,128)S(1)}, f32[512,3,64]{0,2,1:T(8,128)}, f32[4,512,3,64]{1,3,2,0:T(8,128)}, bf16[4,512,3,64]{1,3,2,0:T(8,1...) while((s32[]{:T(128)}, f32[512,3,64]{0,2,1:T(8,128)S(1)}, ...), condition=%wide.region_15.15_spmd.clone, body=%wide.region_14.14_spmd.clone.sunk | while | flops 512032768 | bytes 30918864 | solution.py:132
  794.2 35.0 %while.66 = (s32[]{:T(128)}, f32[512,3,64]{0,2,1:T(8,128)S(1)}, f32[512,3,64]{0,2,1:T(8,128)}, f32[4,512,3,64]{1,3,2,0:T(8,128)}, bf16[4,512,3,64]{1,3,2,0:T(8,1...) while((s32[]{:T(128)}, f32[512,3,64]{0,2,1:T(8,128)S(1)}, ...), condition=%wide.region_15.15_spmd.clone, body=%wide.region_14.14_spmd.clone.sunk | while | flops 512032768 | bytes 30918864 | solution.py:132
  834.6 35.0 %while.66 = (s32[]{:T(128)}, f32[512,3,64]{0,2,1:T(8,128)S(1)}, f32[512,3,64]{0,2,1:T(8,128)}, f32[4,512,3,64]{1,3,2,0:T(8,128)}, bf16[4,512,3,64]{1,3,2,0:T(8,1...) while((s32[]{:T(128)}, f32[512,3,64]{0,2,1:T(8,128)S(1)}, ...), condition=%wide.region_15.15_spmd.clone, body=%wide.region_14.14_spmd.clone.sunk | while | flops 512032768 | bytes 30918864 | solution.py:132
  875.0 35.0 %while.66 = (s32[]{:T(128)}, f32[512,3,64]{0,2,1:T(8,128)S(1)}, f32[512,3,64]{0,2,1:T(8,128)}, f32[4,512,3,64]{1,3,2,0:T(8,128)}, bf16[4,512,3,64]{1,3,2,0:T(8,1...) while((s32[]{:T(128)}, f32[512,3,64]{0,2,1:T(8,128)S(1)}, ...), condition=%wide.region_15.15_spmd.clone, body=%wide.region_14.14_spmd.clone.sunk | while | flops 512032768 | bytes 30918864 | solution.py:132
  915.4 35.0 %while.66 = (s32[]{:T(128)}, f32[512,3,64]{0,2,1:T(8,128)S(1)}, f32[512,3,64]{0,2,1:T(8,128)}, f32[4,512,3,64]{1,3,2,0:T(8,128)}, bf16[4,512,3,64]{1,3,2,0:T(8,1...) while((s32[]{:T(128)}, f32[512,3,64]{0,2,1:T(8,128)S(1)}, ...), condition=%wide.region_15.15_spmd.clone, body=%wide.region_14.14_spmd.clone.sunk | while | flops 512032768 | bytes 30918864 | solution.py:132
  955.8 35.0 %while.66 = (s32[]{:T(128)}, f32[512,3,64]{0,2,1:T(8,128)S(1)}, f32[512,3,64]{0,2,1:T(8,128)}, f32[4,512,3,64]{1,3,2,0:T(8,128)}, bf16[4,512,3,64]{1,3,2,0:T(8,1...) while((s32[]{:T(128)}, f32[512,3,64]{0,2,1:T(8,128)S(1)}, ...), condition=%wide.region_15.15_spmd.clone, body=%wide.region_14.14_spmd.clone.sunk | while | flops 512032768 | bytes 30918864 | solution.py:132
  996.1 35.0 %while.66 = (s32[]{:T(128)}, f32[512,3,64]{0,2,1:T(8,128)S(1)}, f32[512,3,64]{0,2,1:T(8,128)}, f32[4,512,3,64]{1,3,2,0:T(8,128)}, bf16[4,512,3,64]{1,3,2,0:T(8,1...) while((s32[]{:T(128)}, f32[512,3,64]{0,2,1:T(8,128)S(1)}, ...), condition=%wide.region_15.15_spmd.clone, body=%wide.region_14.14_spmd.clone.sunk | while | flops 512032768 | bytes 30918864 | solution.py:132
  1036.5 35.0 %while.66 = (s32[]{:T(128)}, f32[512,3,64]{0,2,1:T(8,128)S(1)}, f32[512,3,64]{0,2,1:T(8,128)}, f32[4,512,3,64]{1,3,2,0:T(8,128)}, bf16[4,512,3,64]{1,3,2,0:T(8,1...) while((s32[]{:T(128)}, f32[512,3,64]{0,2,1:T(8,128)S(1)}, ...), condition=%wide.region_15.15_spmd.clone, body=%wide.region_14.14_spmd.clone.sunk | while | flops 512032768 | bytes 30918864 | solution.py:132
  1076.9 35.0 %while.66 = (s32[]{:T(128)}, f32[512,3,64]{0,2,1:T(8,128)S(1)}, f32[512,3,64]{0,2,1:T(8,128)}, f32[4,512,3,64]{1,3,2,0:T(8,128)}, bf16[4,512,3,64]{1,3,2,0:T(8,1...) while((s32[]{:T(128)}, f32[512,3,64]{0,2,1:T(8,128)S(1)}, ...), condition=%wide.region_15.15_spmd.clone, body=%wide.region_14.14_spmd.clone.sunk | while | flops 512032768 | bytes 30918864 | solution.py:132
  1117.3 35.0 %while.66 = (s32[]{:T(128)}, f32[512,3,64]{0,2,1:T(8,128)S(1)}, f32[512,3,64]{0,2,1:T(8,128)}, f32[4,512,3,64]{1,3,2,0:T(8,128)}, bf16[4,512,3,64]{1,3,2,0:T(8,1...) while((s32[]{:T(128)}, f32[512,3,64]{0,2,1:T(8,128)S(1)}, ...), condition=%wide.region_15.15_spmd.clone, body=%wide.region_14.14_spmd.clone.sunk | while | flops 512032768 | bytes 30918864 | solution.py:132
  1201.4 80.3 %reduce-scatter.6.cloned.1.call-done = bf16[2048,384]{0,1:T(8,128)(2,1)} async-done(((bf16[8192,384]{0,1:T(8,128)(2,1)}), bf16[2048,384]{0,1:T(8,128)(2,1)}) %reduce-scatter.6.cloned.1.call-update) | async-done | bytes 1572880 | tf_op jit(solution)/shard_map/reduce_scatter | solution.py:273
  1342.1 40.2 %all-reduce.8 = (f32[768]{0:T(1024)S(1)}, f32[768]{0:T(1024)S(1)}, f32[768]{0:T(1024)S(1)}, f32[768]{0:T(1024)S(1)}) all-reduce(f32[768]{0:T(1024)S(1)} %get-tuple-element.381, f32[768]{0:T(1024)S(1)} %get-tuple-element.386, f32[768]{0:T(1024)S(1)} %copy-done.31, ...), channel_id=7, replica_groups=mesh['seq'=2,'head'=4,'ctx'=4] {'seq','head','ctx'}, use_global_device_ids=true, to_apply=%region_25.26.clone | all-reduce | flops 3072 | bytes 24576
  1387.6 141.8 %reduce-scatter.12.cloned.1.call-done = f32[24,3072]{1,0:T(8,128)} async-done(((f32[768,3072]{1,0:T(8,128)}), f32[24,3072]{1,0:T(8,128)}) %reduce-scatter.12.cloned.1.call-update) | async-done | bytes 294928 | tf_op jit(solution)/shard_map/reduce_scatter | solution.py:301
  1529.4 141.1 %reduce-scatter.14.cloned.1.call-done = f32[96,768]{1,0:T(8,128)} async-done(((f32[3072,768]{1,0:T(8,128)}), f32[96,768]{1,0:T(8,128)}) %reduce-scatter.14.cloned.1.call-update) | async-done | bytes 294928 | tf_op jit(solution)/shard_map/reduce_scatter | solution.py:302
  1670.4 125.0 %reduce-scatter.8.cloned.1.call-done = f32[24,2304]{1,0:T(8,128)} async-done(((f32[768,2304]{1,0:T(8,128)}), f32[24,2304]{1,0:T(8,128)}) %reduce-scatter.8.cloned.1.call-update) | async-done | bytes 221200 | tf_op jit(solution)/shard_map/reduce_scatter | solution.py:299
  (1535 shorter events, 1322.1 us)
Async XLA Ops:
  7.2 66.6 %all-gather.7.cloned.1.call-start = ((), (), s32[]{:S(2)}) async-start(), calls=%async_computation.9 | async-start | bytes 3649536 | tf_op jit(solution)/shard_map/all_gather | solution.py:163
  7.9 229.6 %all-gather.9.cloned.1.call-start = ((), (), s32[]{:S(2)}) async-start(), calls=%async_computation.10 | async-start | bytes 7864320 | tf_op jit(solution)/shard_map/all_gather | solution.py:211
  53.5 20.3 %copy-start.27 = (f32[768]{0:T(1024)}, f32[768]{0:T(1024)S(1)}, u32[]{:S(2)}) copy-start(f32[768]{0:T(1024)S(1)} %convert_element_type.81) | copy-start | bytes 9220
  53.5 20.3 %copy-start.21 = (f32[768]{0:T(1024)}, f32[768]{0:T(1024)S(1)}, u32[]{:S(2)}) copy-start(f32[768]{0:T(1024)S(1)} %convert_element_type.80) | copy-start | bytes 9220
  122.8 320.1 %all-gather.11.cloned.1.call-start = ((), (), s32[]{:S(2)}) async-start(), calls=%async_computation.11 | async-start | bytes 1216512 | tf_op jit(solution)/shard_map/all_gather | solution.py:164
  123.6 334.9 %all-gather.13.cloned.1.call-start = ((), (), s32[]{:S(2)}) async-start(), calls=%async_computation.12 | async-start | bytes 4866048 | tf_op jit(solution)/shard_map/all_gather | solution.py:165
  124.1 342.6 %all-gather.15.cloned.1.call-start = ((), (), s32[]{:S(2)}) async-start(), calls=%async_computation.13 | async-start | bytes 4866048 | tf_op jit(solution)/shard_map/all_gather | solution.py:166
  438.2 16.4 all-to-all-start.1
  442.8 23.9 %copy-start.29 = (f32[768]{0:T(1024)}, f32[768]{0:T(1024)S(1)}, u32[]{:S(2)}) copy-start(f32[768]{0:T(1024)S(1)} %convert_element_type.87) | copy-start | bytes 9220
  442.9 46.9 %copy-start.19 = (f32[768]{0:T(1024)}, f32[768]{0:T(1024)S(1)}, u32[]{:S(2)}) copy-start(f32[768]{0:T(1024)S(1)} %convert_element_type.86) | copy-start | bytes 9220
  457.0 32.8 %copy-start.17 = (f32[512]{0:T(512)}, f32[512]{0:T(512)S(1)}, u32[]{:S(2)}) copy-start(f32[512]{0:T(512)S(1)} %broadcast_multiply_fusion.4) | copy-start | bytes 6148
  458.4 31.3 %copy-start.25 = (f32[512]{0:T(512)}, f32[512]{0:T(512)S(1)}, u32[]{:S(2)}) copy-start(f32[512]{0:T(512)S(1)} %add_rsqrt_fusion) | copy-start | bytes 6148
  466.8 19.4 %copy-start.8 = (f32[512,768]{1,0:T(8,128)S(1)}, f32[512,768]{1,0:T(8,128)}, u32[]{:S(2)}) copy-start(f32[512,768]{1,0:T(8,128)} %copy-done.7) | copy-start | bytes 4718596
  493.5 15.9 all-to-all-start.2
  497.7 783.9 %reduce-scatter.6.cloned.1.call-start = ((), (), s32[]{:S(2)}) async-start(), calls=%async_computation.14 | async-start | bytes 7864320 | tf_op jit(solution)/shard_map/reduce_scatter | solution.py:273
  1173.5 214.1 %reduce-scatter.10.cloned.1.call-start = ((), (), s32[]{:S(2)}) async-start(), calls=%async_computation.16 | async-start | bytes 2433024 | tf_op jit(solution)/shard_map/reduce_scatter | solution.py:300
  1178.2 351.2 %reduce-scatter.12.cloned.1.call-start = ((), (), s32[]{:S(2)}) async-start(), calls=%async_computation.17 | async-start | bytes 9732096 | tf_op jit(solution)/shard_map/reduce_scatter | solution.py:301
  1185.6 484.9 %reduce-scatter.14.cloned.1.call-start = ((), (), s32[]{:S(2)}) async-start(), calls=%async_computation.18 | async-start | bytes 9732096 | tf_op jit(solution)/shard_map/reduce_scatter | solution.py:302
  1198.7 596.7 %reduce-scatter.8.cloned.1.call-start = ((), (), s32[]{:S(2)}) async-start(), calls=%async_computation.15 | async-start | bytes 7299072 | tf_op jit(solution)/shard_map/reduce_scatter | solution.py:299
  1293.0 32.9 %copy-start.6 = (bf16[512,768]{1,0:T(8,128)(2,1)S(1)}, bf16[512,768]{1,0:T(8,128)(2,1)}, u32[]{:S(2)}) copy-start(bf16[512,768]{1,0:T(8,128)(2,1)} %param.19) | copy-start | bytes 2359300
  1293.0 32.9 %copy-start.16 = (f32[512]{0:T(512)S(1)}, f32[512]{0:T(512)}, u32[]{:S(2)}) copy-start(f32[512]{0:T(512)} %copy-done.15) | copy-start | bytes 6148
  1293.0 32.9 %copy-start.22 = (f32[768]{0:T(1024)S(1)}, f32[768]{0:T(1024)}, u32[]{:S(2)}) copy-start(f32[768]{0:T(1024)} %copy-done.21) | copy-start | bytes 9220
  1293.0 32.8 %copy-start.24 = (f32[512]{0:T(512)S(1)}, f32[512]{0:T(512)}, u32[]{:S(2)}) copy-start(f32[512]{0:T(512)} %copy-done.23) | copy-start | bytes 6148
  1293.0 32.8 %copy-start.28 = (f32[768]{0:T(1024)S(1)}, f32[768]{0:T(1024)}, u32[]{:S(2)}) copy-start(f32[768]{0:T(1024)} %copy-done.27) | copy-start | bytes 9220
  (104 other events, 378.2 us)
Sparse Core Ops, SparseCore 0:
  10.8 62.9 all-gather.6
  122.9 114.5 all-gather.8
  240.3 52.2 all-gather.10
  295.2 62.4 all-gather.12
  360.4 62.3 all-gather.14
  1173.5 108.0 reduce-scatter.5
  1287.5 99.6 reduce-scatter.9
  1394.7 134.6 reduce-scatter.11
  1535.8 134.5 reduce-scatter.13
  1677.5 117.8 reduce-scatter.7
where the time goes:
time: 1810 us; the launch traced here: 1800 us
  matrix products  715 us (40%)
  waiting for transfers between devices  622 us (34%)
  blocking collectives  166 us (9%)
  other arithmetic  161 us (9%)
  local copies, waits for them, and re-layouts  104 us (6%)
    dot_general x64, matrix products, attend_over_queries(): jnp.einsum('qhk,qhd->khd', probs_now.astype(jnp.bfloat16), grad_attn, pre...  234 us
    dot_general x64, matrix products, attend_over_queries(): jnp.einsum('qhd,khd->qhk', grad_attn, values_now, preferred_element_type=...  153 us
    reduce_scatter x1, waiting for transfers between devices, body(): lax.psum_scatter(grad_w_up, ('seq', 'head', 'ctx'), scatter_dimension=0,...  142 us
    reduce_scatter x1, waiting for transfers between devices, body(): lax.psum_scatter(grad_w_down, ('seq', 'head', 'ctx'), scatter_dimension=0...  141 us
    reduce_scatter x1, waiting for transfers between devices, body(): lax.psum_scatter(grad_w_qkv, ('seq', 'head', 'ctx'), scatter_dimension=0,...  125 us
    all_gather x1, waiting for transfers between devices, body(): lax.all_gather(key_vals, 'ctx', axis=0, tiled=True)  91.1 us
    dot_general x64, matrix products, attend_over_queries(): jnp.einsum('qhk,khd->qhd', grad_score, keys_now, preferred_element_type=j...  86.9 us
    unnamed x2, blocking collectives  82.4 us
  transfers between devices with their start and end apart: 12, of which 8 were waited for; matrix products, arithmetic and copies ran while one was open for 15% of the time, Pallas kernels for 0%

commit v1 on v0

v1 whole, which is shorter than its diff:
```python
from functools import partial

import jax
import jax.numpy as jnp
from jax import lax
from jax.experimental import pallas as pl
from jax.experimental.pallas import tpu as pltpu
from jax.sharding import PartitionSpec as P

D = 768
HEADS = 12
HDIM = 64
BLOCK = 512
LANES = 128
EPSILON = 1e-05
MASKED = -1e30
LOG2E = 1.4426950408889634
LN2 = 0.6931471805599453
ALL_AXES = ("seq", "head", "ctx")
BF16 = jnp.bfloat16
F32 = jnp.float32


def dot_on(left, right, left_dim, right_dim):
    return lax.dot_general(
        left, right, (((left_dim,), (right_dim,)), ((), ())), preferred_element_type=F32
    )


def norm_rows(values, gain_vec, bias_vec):
    row_mean = jnp.mean(values, axis=-1, keepdims=True)
    centered = values - row_mean
    variance = jnp.mean(centered * centered, axis=-1, keepdims=True)
    inv_rows = lax.rsqrt(variance + EPSILON)
    unit_rows = centered * inv_rows
    return (unit_rows * gain_vec + bias_vec, unit_rows, inv_rows)


def norm_back(grad_norm, unit_rows, inv_rows, gain_vec):
    scaled = grad_norm * gain_vec
    return inv_rows * (
        scaled
        - jnp.mean(scaled, axis=-1, keepdims=True)
        - unit_rows * jnp.mean(scaled * unit_rows, axis=-1, keepdims=True)
    )


def gelu_exact(values):
    return jax.nn.gelu(values, approximate=False)


def swap_head(value, mask):
    count = lax.axis_size("head")
    return lax.ppermute(value, "head", [(i, i ^ mask) for i in range(count)])


def ring_order(count):
    return [0, 1, 3, 2] if count == 4 else list(range(count))


def ring_pairs(count, step):
    order = ring_order(count)
    return [(order[i], order[(i + step) % count]) for i in range(count)]


def ring_send(value, step):
    return lax.ppermute(value, "ctx", ring_pairs(lax.axis_size("ctx"), step))


def plane_blocks(block):
    near = swap_head(block, 2)
    return [block, swap_head(block, 1), near, swap_head(near, 1)]


def split_three(values):
    high = values.astype(BF16)
    rest = values - high.astype(F32)
    middle = rest.astype(BF16)
    low = (rest - middle.astype(F32)).astype(BF16)
    return [high.astype(F32), middle.astype(F32), low.astype(F32)]


def key_marks(valid, lane):
    row = lax.broadcasted_iota(jnp.int32, (BLOCK, LANES), 0)
    real = row < valid
    marks = jnp.where((lane >= 64) & (lane < 67), 1.0, 0.0)
    marks = jnp.where((lane == 67) & jnp.logical_not(real), MASKED, marks)
    return jnp.where((lane == 68) & real, MASKED, marks)


def fill_keys(slots, kv_ref, valid_ref, keys_out, values_t=None, values_out=None):
    lane = lax.broadcasted_iota(jnp.int32, (BLOCK, LANES), 1)

    def fill(slot, carry):
        rows = pl.ds(pl.multiple_of(slot * BLOCK, BLOCK), BLOCK)
        marks = key_marks(valid_ref[slot], lane)
        for head in range(3):
            pair = kv_ref[rows, head * LANES : (head + 1) * LANES].astype(F32)
            keys_out[head, rows, :] = jnp.where(lane < 64, pair, marks).astype(BF16)
            if values_out is not None:
                ones = jnp.where(lane < 3, 1.0, 0.0)
                values_out[head, rows, :] = jnp.where(lane < 64, ones, pair).astype(BF16)
            if values_t is not None:
                turned = pair.T[64:128].astype(BF16)
                values_t[head, :, rows] = jnp.concatenate(
                    [turned, jnp.ones((16, BLOCK), BF16)], axis=0
                )
        return carry

    lax.fori_loop(0, slots, fill, 0)


def query_marks(valid, width):
    row = lax.broadcasted_iota(jnp.int32, (1, width), 1)
    real = jnp.where(row < valid, 1.0, 0.0)
    return [real, 1.0 - real]


def forward_kernel(
    slots, count_ref, list_ref, valid_ref, q_ref, kv_ref, out_ref, lse_ref, keys, values_t, q_ext, acc, top, total
):
    fill_keys(slots, kv_ref, valid_ref, keys, values_t=values_t)

    def over_queries(block, carry):
        q_rows = pl.ds(pl.multiple_of(block * BLOCK, BLOCK), BLOCK)
        lane = lax.broadcasted_iota(jnp.int32, (BLOCK, LANES), 1)
        row = lax.broadcasted_iota(jnp.int32, (BLOCK, LANES), 0)
        real = row < valid_ref[block]
        marks = jnp.where((lane == 67) & real, 1.0, 0.0)
        marks = jnp.where((lane == 68) & jnp.logical_not(real), 1.0, marks)
        for head in range(3):
            own = q_ref[q_rows, head * LANES : (head + 1) * LANES].astype(F32)
            q_ext[head] = jnp.where(lane < 64, own, marks).astype(BF16)
            acc[head] = jnp.zeros(acc.shape[1:], F32)

        def scores_of(slot, head):
            rows = pl.ds(pl.multiple_of(slot * BLOCK, BLOCK), BLOCK)
            return dot_on(keys[head, rows, :], q_ext[head], 1, 1)

        def over_keys(item, carry_in):
            slot = list_ref[block, item]
            rows = pl.ds(pl.multiple_of(slot * BLOCK, BLOCK), BLOCK)
            ready = [scores_of(slot, 0), scores_of(slot, 1)]
            for head in range(3):
                if head == 0:
                    ready.append(scores_of(slot, 2))
                weights = jnp.exp2(ready.pop(0)).astype(BF16)
                acc[head] += dot_on(values_t[head, :, rows], weights, 1, 0)
            return carry_in

        lax.fori_loop(0, count_ref[block], over_keys, 0)
        safe = jnp.bool_(True)
        for head in range(3):
            sums = acc[head, 64:65, :]
            good = (sums >= 2.0**-60) & (sums <= 2.0**100)
            safe = safe & (jnp.min(jnp.where(good, 1.0, 0.0)) > 0.5)
        for head in range(3):
            top[head] = jnp.zeros((1, BLOCK), F32)

        @pl.when(jnp.logical_not(safe))
        def _():
            for head in range(3):
                top[head] = jnp.full((1, BLOCK), MASKED, F32)
                acc[head] = jnp.zeros(acc.shape[1:], F32)

            def with_max(item, carry_in):
                slot = list_ref[block, item]
                rows = pl.ds(pl.multiple_of(slot * BLOCK, BLOCK), BLOCK)
                for head in range(3):
                    scores = scores_of(slot, head)
                    before = top[head]
                    after = jnp.maximum(before, jnp.max(scores, axis=0, keepdims=True))
                    weights = jnp.exp2(scores - after).astype(BF16)
                    top[head] = after
                    acc[head] = acc[head] * jnp.exp2(before - after) + dot_on(
                        values_t[head, :, rows], weights, 1, 0
                    )
                return carry_in

            lax.fori_loop(0, count_ref[block], with_max, 0)

        for head in range(3):
            sums = acc[head, 64:65, :]
            out_ref[head, :, q_rows] = (acc[head, 0:64, :] / sums).astype(BF16)
            lse_ref[head, :, q_rows] = top[head] + jnp.log2(sums)
        return carry

    lax.fori_loop(0, 4, over_queries, 0)


def attend_forward(counts, lists, valid, queries, key_vals):
    q_rows, kv_rows = queries.shape[0], key_vals.shape[0]
    slots = kv_rows // BLOCK
    smem = pl.BlockSpec(memory_space=pltpu.SMEM)
    vmem = pl.BlockSpec(memory_space=pltpu.VMEM)
    return pl.pallas_call(
        partial(forward_kernel, slots),
        out_shape=(
            jax.ShapeDtypeStruct((3, HDIM, q_rows), BF16),
            jax.ShapeDtypeStruct((3, 1, q_rows), F32),
        ),
        in_specs=[smem, smem, smem, vmem, vmem],
        out_specs=(vmem, vmem),
        scratch_shapes=[
            pltpu.VMEM((3, kv_rows, LANES), BF16),
            pltpu.VMEM((3, 80, kv_rows), BF16),
            pltpu.VMEM((3, BLOCK, LANES), BF16),
            pltpu.VMEM((3, 80, BLOCK), F32),
            pltpu.VMEM((3, 1, BLOCK), F32),
            pltpu.VMEM((3, 1, BLOCK), F32),
        ],
        compiler_params=pltpu.CompilerParams(vmem_limit_bytes=48 << 20),
        cost_estimate=pl.CostEstimate(
            flops=4 * 108 * BLOCK * BLOCK * 256, bytes_accessed=10 << 20, transcendentals=28 << 20
        ),
        name="attend_forward",
    )(counts, lists, valid, queries, key_vals)


def backward_kernel(
    slots,
    count_ref,
    list_ref,
    valid_ref,
    q_ref,
    kv_ref,
    out_ref,
    lse_ref,
    grad_ref,
    dq_ref,
    dkv_ref,
    keys,
    values,
    q_ext,
    g_ext,
    q_turned,
    dq_acc,
    dkv_acc,
):
    fill_keys(slots, kv_ref, valid_ref, keys, values_out=values)

    def clear(slot, carry):
        rows = pl.ds(pl.multiple_of(slot * BLOCK, BLOCK), BLOCK)
        for head in range(3):
            dkv_acc[head, :, rows] = jnp.zeros((LANES, BLOCK), F32)
        return carry

    lax.fori_loop(0, slots, clear, 0)

    def over_queries(block, carry):
        q_rows = pl.ds(pl.multiple_of(block * BLOCK, BLOCK), BLOCK)
        for head in range(3):
            turned = q_ref[q_rows, head * LANES : (head + 1) * LANES].astype(F32).T[0:64]
            grad_t = grad_ref[head, :, q_rows].astype(F32)
            delta = jnp.sum(grad_t * out_ref[head, :, q_rows].astype(F32), axis=0, keepdims=True)
            marks = split_three(-lse_ref[head, :, q_rows]) + query_marks(valid_ref[block], BLOCK)
            blank = jnp.zeros((64 - len(marks), BLOCK), F32)
            q_turned[head] = turned.astype(BF16)
            q_ext[head] = jnp.concatenate([turned] + marks + [blank], axis=0).T.astype(BF16)
            minus = split_three(-delta)
            blank = jnp.zeros((64 - len(minus), BLOCK), F32)
            g_ext[head] = jnp.concatenate(minus + [blank, grad_t], axis=0).T.astype(BF16)
            dq_acc[head] = jnp.zeros((BLOCK, LANES), F32)

        def over_keys(item, carry_in):
            slot = list_ref[block, item]
            rows = pl.ds(pl.multiple_of(slot * BLOCK, BLOCK), BLOCK)

            def products(head):
                return (
                    dot_on(q_ext[head], keys[head, rows, :], 1, 1),
                    dot_on(g_ext[head], values[head, rows, :], 1, 1),
                )

            ready = [products(0)]
            for head in range(3):
                if head < 2:
                    ready.append(products(head + 1))
                scores, grad_probs = ready.pop(0)
                probs = jnp.exp2(scores)
                grad_scores = (probs * grad_probs).astype(BF16)
                dkv_acc[head, 64:128, rows] += dot_on(
                    grad_ref[head, :, q_rows], probs.astype(BF16), 1, 0
                )
                dkv_acc[head, 0:64, rows] += dot_on(q_turned[head], grad_scores, 1, 0)
                dq_acc[head] += dot_on(grad_scores, keys[head, rows, :], 1, 0)
            return carry_in

        lax.fori_loop(0, count_ref[block], over_keys, 0)
        lane = lax.broadcasted_iota(jnp.int32, (BLOCK, LANES), 1)
        for head in range(3):
            dq_ref[q_rows, head * LANES : (head + 1) * LANES] = jnp.where(
                lane < 64, dq_acc[head] * HDIM ** (-0.5), 0.0
            ).astype(BF16)
        return carry

    lax.fori_loop(0, 4, over_queries, 0)

    def finish(slot, carry):
        rows = pl.ds(pl.multiple_of(slot * BLOCK, BLOCK), BLOCK)
        for head in range(3):
            dkv_ref[head, 0:64, rows] = (dkv_acc[head, 0:64, rows] * LN2).astype(BF16)
            dkv_ref[head, 64:128, rows] = dkv_acc[head, 64:128, rows].astype(BF16)
        return carry

    lax.fori_loop(0, slots, finish, 0)


def attend_backward(counts, lists, valid, queries, key_vals, attended, lse, grads):
    q_rows, kv_rows = queries.shape[0], key_vals.shape[0]
    slots = kv_rows // BLOCK
    smem = pl.BlockSpec(memory_space=pltpu.SMEM)
    vmem = pl.BlockSpec(memory_space=pltpu.VMEM)
    return pl.pallas_call(
        partial(backward_kernel, slots),
        out_shape=(
            jax.ShapeDtypeStruct((q_rows, 3 * LANES), BF16),
            jax.ShapeDtypeStruct((3, LANES, kv_rows), BF16),
        ),
        in_specs=[smem] * 3 + [vmem] * 5,
        out_specs=(vmem, vmem),
        scratch_shapes=[
            pltpu.VMEM((3, kv_rows, LANES), BF16),
            pltpu.VMEM((3, kv_rows, LANES), BF16),
            pltpu.VMEM((3, BLOCK, LANES), BF16),
            pltpu.VMEM((3, BLOCK, LANES), BF16),
            pltpu.VMEM((3, HDIM, BLOCK), BF16),
            pltpu.VMEM((3, BLOCK, LANES), F32),
            pltpu.VMEM((3, LANES, kv_rows), F32),
        ],
        compiler_params=pltpu.CompilerParams(vmem_limit_bytes=58 << 20),
        cost_estimate=pl.CostEstimate(
            flops=10 * 108 * BLOCK * BLOCK * 256, bytes_accessed=20 << 20, transcendentals=28 << 20
        ),
        name="attend_backward",
    )(counts, lists, valid, queries, key_vals, attended, lse, grads)


def scene_lists(segment_ids, slots_ids, slots_valid):
    same = slots_ids[:4, None] == slots_ids[None, :]
    counts = jnp.sum(same, axis=1).astype(jnp.int32)
    number = slots_ids.shape[0]
    earlier = jnp.arange(number)[None, :] < jnp.arange(number)[:, None]
    place = jnp.sum(same[:, None, :] & earlier[None], axis=2)
    hits = same[:, None, :] & (place[:, None, :] == jnp.arange(number)[None, :, None])
    lists = jnp.sum(jnp.where(hits, jnp.arange(number)[None, None, :], 0), axis=2)
    return counts, lists.astype(jnp.int32)


def body(
    tokens,
    segment_ids,
    w_qkv,
    w_out,
    w_up,
    w_down,
    gain_one,
    bias_one,
    gain_two,
    bias_two,
    cotangent,
):
    heads_ax = lax.axis_size("head")
    ctx_ax = lax.axis_size("ctx")
    me_head = lax.axis_index("head")
    tok_rows = tokens.shape[0]
    group = D // heads_ax
    shard = w_qkv.shape[0]

    ring = [tokens]
    for _ in range(ctx_ax - 1):
        ring.append(ring_send(ring[-1], 1))
    planes = [plane_blocks(block) for block in ring]

    norms = jnp.stack([gain_one, bias_one, gain_two, bias_two], axis=1)
    packed = jnp.concatenate([w_qkv, jnp.pad(norms, ((0, 0), (0, LANES - 4)))], axis=1)
    packed = lax.all_gather(packed, ALL_AXES, axis=0, tiled=True)
    full_qkv = packed[:, : 3 * D]
    g_one, b_one, g_two, b_two = [packed[:, 3 * D + i].astype(F32) for i in range(4)]
    full_out = lax.all_gather(w_out, ALL_AXES, axis=0, tiled=True)
    full_up = lax.all_gather(w_up, ALL_AXES, axis=0, tiled=True)
    full_down = lax.all_gather(w_down, ALL_AXES, axis=0, tiled=True)

    about = jnp.stack([segment_ids[0], jnp.sum(segment_ids >= 0).astype(jnp.int32)])
    about = jnp.broadcast_to(about[:, None], (2, LANES))
    ring_about = [about]
    for _ in range(ctx_ax - 1):
        ring_about.append(ring_send(ring_about[-1], 1))
    about_all = jnp.stack([b[:, 0] for r in ring_about for b in plane_blocks(r)])
    slot_ids, slot_valid = about_all[:, 0], about_all[:, 1]
    counts, lists = scene_lists(segment_ids, slot_ids, slot_valid)

    w_mine = lax.dynamic_slice_in_dim(full_qkv, me_head * 3 * group, 3 * group, axis=1)
    w_mine = w_mine.reshape(D, 3, 3, HDIM)
    w_kv = w_mine[:, :, 1:].reshape(D, 6 * HDIM)
    w_q = jnp.pad(w_mine[:, :, :1], ((0, 0), (0, 0), (0, 1), (0, 0))).reshape(D, 6 * HDIM)

    x_all = jnp.concatenate([b for plane in planes for b in plane], axis=0).astype(F32)
    normed, ignored, ignored_too = norm_rows(x_all, g_one, b_one)
    h_all = normed.astype(BF16)
    key_vals = jnp.dot(h_all, w_kv, preferred_element_type=F32).astype(BF16)
    h_plane = h_all[: heads_ax * tok_rows]
    queries = jnp.dot(h_plane, w_q, preferred_element_type=F32) * (HDIM ** (-0.5) * LOG2E)
    queries = queries.astype(BF16)

    attended, lse = attend_forward(counts, lists, slot_valid, queries, key_vals)

    parts = []
    for j in range(heads_ax):
        part = attended[:, :, j * tok_rows : (j + 1) * tok_rows].reshape(group, tok_rows)
        parts.append(swap_head(part, j) if j else part)
    merged_t = jnp.concatenate(parts, axis=0)
    order = [me_head ^ j for j in range(heads_ax)]
    out_groups = full_out.reshape(heads_ax, group, D)
    out_mine = jnp.concatenate(
        [lax.dynamic_index_in_dim(out_groups, o, 0, keepdims=False) for o in order], axis=0
    )

    inputs = tokens.astype(F32)
    y_one = inputs + jnp.einsum("at,ad->td", merged_t, out_mine, preferred_element_type=F32)
    normed_two, unit_two, inv_two = norm_rows(y_one, g_two, b_two)
    h_two = normed_two.astype(BF16)
    up_proj = jnp.dot(h_two, full_up, preferred_element_type=F32)
    hidden = gelu_exact(up_proj).astype(BF16)
    output = (y_one + jnp.dot(hidden, full_down, preferred_element_type=F32)).astype(BF16)
    grad_w_down = jnp.einsum("tf,td->fd", hidden, cotangent, preferred_element_type=F32)
    grad_hidden = jnp.einsum("td,fd->tf", cotangent, full_down, preferred_element_type=F32)
    grad_up = jax.vjp(gelu_exact, up_proj)[1](grad_hidden)[0].astype(BF16)
    grad_w_up = jnp.einsum("td,tf->df", h_two, grad_up, preferred_element_type=F32)
    grad_h_two = jnp.einsum("tf,df->td", grad_up, full_up, preferred_element_type=F32)
    grad_gain_two = jnp.sum(grad_h_two * unit_two, axis=0)
    grad_bias_two = jnp.sum(grad_h_two, axis=0)
    grad_y_one = cotangent.astype(F32) + norm_back(grad_h_two, unit_two, inv_two, g_two)
    grad_z = grad_y_one.astype(BF16)
    grad_w_out = jnp.einsum("at,td->ad", merged_t, grad_z, preferred_element_type=F32)
    grad_merged = jnp.einsum("td,ad->at", grad_z, out_mine, preferred_element_type=F32)
    grad_merged = grad_merged.astype(BF16)

    grad_parts = []
    for j in range(heads_ax):
        part = grad_merged[j * group : (j + 1) * group]
        grad_parts.append(swap_head(part, j) if j else part)
    grad_local = jnp.concatenate(grad_parts, axis=1).reshape(3, HDIM, heads_ax * tok_rows)

    d_query, d_kv = attend_backward(
        counts, lists, slot_valid, queries, key_vals, attended, lse, grad_local
    )
    d_kv = d_kv.reshape(6 * HDIM, heads_ax * ctx_ax * tok_rows)

    grad_h = jnp.einsum("ct,dc->td", d_kv, w_kv, preferred_element_type=F32)
    grad_h_q = jnp.einsum("tc,dc->td", d_query, w_q, preferred_element_type=F32)
    grad_h = grad_h.reshape(ctx_ax, heads_ax, tok_rows, D)
    grad_h_q = grad_h_q.reshape(heads_ax, tok_rows, D)
    traveling = None
    for r in reversed(range(ctx_ax)):
        term = grad_h[r]
        if r == 0:
            term = term + grad_h_q
        low = term.astype(BF16)
        by_x = [
            term[2 * i] + swap_head(low[2 * i + 1], 1).astype(F32) for i in range(2)
        ]
        own = by_x[0] + swap_head(by_x[1].astype(BF16), 2).astype(F32)
        if traveling is not None:
            own = own + ring_send(traveling.astype(BF16), -1).astype(F32)
        traveling = own
    grad_h_one = traveling

    grad_w_kv = jnp.einsum("td,ct->dc", h_all, d_kv, preferred_element_type=F32)
    grad_w_q = jnp.einsum("td,tc->dc", h_plane, d_query, preferred_element_type=F32)
    grad_w_mine = jnp.concatenate(
        [
            grad_w_q.reshape(D, 3, 2, HDIM)[:, :, :1],
            grad_w_kv.reshape(D, 3, 2, HDIM),
        ],
        axis=2,
    ).reshape(-1, heads_ax, ctx_ax, shard, 3 * group)
    grad_w_mine = jnp.swapaxes(grad_w_mine, 1, 2).reshape(D, 3 * group).astype(BF16)
    grad_w_mine = lax.psum_scatter(
        grad_w_mine, ("seq", "ctx"), scatter_dimension=0, tiled=True
    )
    grad_w_qkv = lax.all_to_all(
        grad_w_mine.reshape(heads_ax, shard, 3 * group),
        "head",
        split_axis=0,
        concat_axis=2,
        tiled=True,
    ).reshape(shard, 3 * D).astype(F32)

    normed_one, unit_one, inv_one = norm_rows(inputs, g_one, b_one)
    grad_gain_one = jnp.sum(grad_h_one * unit_one, axis=0)
    grad_bias_one = jnp.sum(grad_h_one, axis=0)
    grad_tokens = (grad_y_one + norm_back(grad_h_one, unit_one, inv_one, g_one)).astype(BF16)

    grad_out_groups = grad_w_out.reshape(heads_ax, group, D)
    grad_w_out = jnp.concatenate(
        [lax.dynamic_index_in_dim(grad_out_groups, o, 0, keepdims=False) for o in order], axis=0
    )
    scatter = partial(lax.psum_scatter, axis_name=ALL_AXES, scatter_dimension=0, tiled=True)
    return (
        output,
        grad_tokens,
        grad_w_qkv,
        scatter(grad_w_out.astype(BF16)).astype(F32),
        scatter(grad_w_up.astype(BF16)).astype(F32),
        scatter(grad_w_down.astype(BF16)).astype(F32),
        scatter(grad_gain_one),
        scatter(grad_bias_one),
        scatter(grad_gain_two),
        scatter(grad_bias_two),
    )


def solution(mesh):
    rows = P(ALL_AXES, None)
    vector = P(ALL_AXES)
    return jax.shard_map(
        body,
        mesh=mesh,
        in_specs=(rows, vector, rows, rows, rows, rows, vector, vector, vector, vector, rows),
        out_specs=(rows, rows, rows, rows, rows, rows, vector, vector, vector, vector),
        check_vma=False,
    )
```

time: 1810 us -> 819 us (0.45)
  matrix products: 715 us -> 104 us
  waiting for transfers between devices: 622 us -> 381 us
  blocking collectives: 166 us -> 40.4 us
  Pallas kernels: 0 us -> 111 us
  other arithmetic: 161 us -> 66.7 us
  local copies, waits for them, and re-layouts: 104 us -> 52.1 us
  starting transfers between devices: 9.49 us -> 38.6 us
    dot_general x460 -> x15, matrix products: 715 us -> 104 us  [the longest x1 19.6 us: body(): jnp.einsum('td,fd->tf', cotangent, full_down, preferred_element_type=F32)]
    reduce_scatter x5 -> x4, waiting for transfers between devices: 488 us -> 218 us  [the longest x1 110 us: body(): scatter(grad_w_down.astype(BF16)).astype(F32)]
    ppermute x0 -> x51, waiting for transfers between devices: none -> 134 us  [the longest x9 73 us: ring_send(): return lax.ppermute(value, 'ctx', ring_pairs(lax.axis_size('ctx'), step))]
    pallas_call x0 -> x2, Pallas kernels: none -> 111 us  [the longest x1 77.1 us: attend_backward(): pl.pallas_call(partial(backward_kernel, slots), out_shape=(jax.ShapeDtype...]
    all_gather x5 -> x4, waiting for transfers between devices: 109 us -> 27.8 us  [the longest x1 27.8 us: body(): full_down = lax.all_gather(w_down, ALL_AXES, axis=0, tiled=True)]
    all_to_all x2 -> x0, blocking collectives: 62.4 us -> none  [the longest x1 31.4 us: body(): lax.all_to_all(grad_local_qkv.reshape(heads_ax, tok_rows, per_group * 3 *...]
    add x18 -> x1, other arithmetic: 55.5 us -> 0.6 us  [body(): cotangent.astype(F32) + norm_back(grad_h_two, unit_two, inv_two, g_two)]
    unnamed x2 -> x1, blocking collectives: 82.4 us -> 40.4 us
  transfers between devices with their start and end apart: 12 -> 60, of which waited for: 8 -> 22; matrix products, arithmetic and copies ran while one was open for 15% -> 20% of each run, Pallas kernels for 0% -> 4%
where the time goes in v1:
time: 819 us; the launch traced here: 809 us
  waiting for transfers between devices  381 us (47%)
  Pallas kernels  111 us (14%)
  matrix products  104 us (13%)
  other arithmetic  66.7 us (8%)
  local copies, waits for them, and re-layouts  52.1 us (6%)
  blocking collectives  40.4 us (5%)
  starting transfers between devices  38.6 us (5%)
  between operations  15.2 us (2%)
    reduce_scatter x1, waiting for transfers between devices, body(): scatter(grad_w_down.astype(BF16)).astype(F32)  110 us
    pallas_call x1, Pallas kernels, attend_backward(): pl.pallas_call(partial(backward_kernel, slots), out_shape=(jax.ShapeDtype...  77.1 us
    ppermute x9, waiting for transfers between devices, ring_send(): return lax.ppermute(value, 'ctx', ring_pairs(lax.axis_size('ctx'), step))  73 us
    ppermute x42, waiting for transfers between devices, swap_head(): return lax.ppermute(value, 'head', [(i, i ^ mask) for i in range(count)])  61.2 us
    reduce_scatter x1, waiting for transfers between devices, body(): scatter(grad_w_up.astype(BF16)).astype(F32)  60 us
    reduce_scatter x1, waiting for transfers between devices, body(): scatter(grad_w_out.astype(BF16)).astype(F32)  47.6 us
    unnamed x1, blocking collectives  40.4 us
    pallas_call x1, Pallas kernels, attend_forward(): pl.pallas_call(partial(forward_kernel, slots), out_shape=(jax.ShapeDtypeS...  34 us
  transfers between devices with their start and end apart: 60, of which 22 were waited for; matrix products, arithmetic and copies ran while one was open for 20% of the time, Pallas kernels for 4%

profile of v1, /device:TPU:0, one launch (start us, length us, event | category | flops | bytes accessed | tf_op | source)
XLA Modules:
  0.0 808.9 jit_solution(12639662789226696922)
XLA Ops:
  28.8 22.0 %collective-permute-done.7 = s32[2,128]{0,1:T(8,128)S(1)} collective-permute-done((s32[2,128]{0,1:T(8,128)S(1)}, s32[2,128]{0,1:T(8,128)S(1)}, u32[]{:S(2)}, u32[]{:S(2)}) %collective-permute-start.7) | collective-permute-done | bytes 1056 | tf_op jit(solution)/shard_map/ppermute | solution.py:67
  68.3 23.5 %collective-permute-done.22 = bf16[512,768]{1,0:T(8,128)(2,1)S(1)} collective-permute-done((bf16[512,768]{1,0:T(8,128)(2,1)S(1)}, bf16[512,768]{1,0:T(8,128)(2,1)S(1)}, u32[]{:S(2)}, u32[]{:S(2)}) %collective-permute-start.22) | collective-permute-done | bytes 786464 | tf_op jit(solution)/shard_map/ppermute | solution.py:67
  96.3 16.8 %collective-permute-done.26 = bf16[512,768]{1,0:T(8,128)(2,1)S(1)} collective-permute-done((bf16[512,768]{1,0:T(8,128)(2,1)S(1)}, bf16[512,768]{1,0:T(8,128)(2,1)S(1)}, u32[]{:S(2)}, u32[]{:S(2)}) %collective-permute-start.26) | collective-permute-done | bytes 786464 | tf_op jit(solution)/shard_map/ppermute | solution.py:67
  121.5 12.6 %collective-permute-done.28 = bf16[512,768]{1,0:T(8,128)(2,1)S(1)} collective-permute-done((bf16[512,768]{1,0:T(8,128)(2,1)S(1)}, bf16[512,768]{1,0:T(8,128)(2,1)S(1)}, u32[]{:S(2)}, u32[]{:S(2)}) %collective-permute-start.28) | collective-permute-done | bytes 786464 | tf_op jit(solution)/shard_map/ppermute | solution.py:54
  140.8 6.3 convert_reduce_fusion
  147.2 8.2 %fusion.2 = f32[8192]{0:T(1024)S(1)} fusion(bf16[8192,768]{1,0:T(8,128)(2,1)} %constant_dynamic-update-slice_fusion, f32[8192]{0:T(1024)S(1)} %broadcast_multiply_fusion), kind=kLoop, calls=%fused_computation.4 | loop fusion | flops 25157632 | bytes 12648448 | tf_op jit(solution)/shard_map/reduce_sum | solution.py:33
  163.4 8.5 %fusion.5 = bf16[8192,768]{1,0:T(8,128)(2,1)S(1)} fusion(bf16[8192,768]{1,0:T(8,128)(2,1)} %constant_dynamic-update-slice_fusion, f32[768]{0:T(1024)S(1)} %get-tuple-element.20, f32[768]{0:T(1024)S(1)} %get-tuple-element.21, f32[8192]{0:T(1024)S(1)} %copy-done.33, f32[8192]{0:T(1024)S(1)} %copy-done.25), kind=kLoop, calls=%fused_computation.7 | loop fusion | flops 37748736 | bytes 25237504 | tf_op jit(solution)/shard_map/convert_element_type | solution.py:400
  176.6 12.0 %convolution_convert_fusion.kv_ref = bf16[8192,384]{1,0:T(8,128)(2,1)} fusion(bf16[8192,768]{1,0:T(8,128)(2,1)} %copy-done.8, bf16[768,384]{0,1:T(8,128)(2,1)S(1)} %bitcast.137), kind=kOutput, calls=%fused_computation.10 | convolution fusion | flops 4834983936 | bytes 19464192 | tf_op jit(solution)/shard_map/dot_general | solution.py:401
  188.5 34.0 %attend_forward.1 = (bf16[3,64,2048]{2,1,0:T(8,128)(2,1)S(1)}, f32[3,1,2048]{2,1,0:T(1,128)S(1)}) custom-call(s32[4]{0:T(128)S(1)} %get-tuple-element.37.count_ref, s32[4,16]{1,0:T(4,128)S(1)} %select_reduce_fusion.list_ref, s32[16]{0:T(128)S(1)} %get-tuple-element.68.valid_ref, bf16[2048,384]{1,0:T(8,128)(2,1)S(1)} %multiply_convert_fusion.1.q_ref, ...), custom_call_target="tpu_custom_call" | custom-call | flops 28991029248 | bytes 10485760 | tf_op jit(solution)/shard_map/attend_forward/pallas_call | solution.py:196
  238.6 7.3 fusion.64
  245.9 27.8 %all-gather.11.cloned.1.call-done = bf16[3072,768]{1,0:T(8,128)(2,1)} async-done(((bf16[96,768]{1,0:T(8,128)(2,1)}), bf16[3072,768]{1,0:T(8,128)(2,1)}) %all-gather.11.cloned.1.call-update) | async-done | bytes 4718608 | tf_op jit(solution)/shard_map/all_gather | solution.py:382
  273.7 19.6 %add_convert_fusion = (bf16[512,3072]{1,0:T(8,128)(2,1)S(1)}, f32[512,3072]{1,0:T(8,128)}) fusion(f32[512,3072]{1,0:T(8,128)} %fusion.64, bf16[512,768]{1,0:T(8,128)(2,1)S(1)} %copy-done.21, bf16[3072,768]{1,0:T(8,128)(2,1)} %all-gather.11.cloned.1.call-done), kind=kOutput, calls=%fused_computation.13 | convolution fusion | flops 2529165312 | bytes 21233664 | tf_op jit(solution)/shard_map/td,fd->tf/dot_general | solution.py:427
  311.6 77.1 %attend_backward.1 = (bf16[2048,384]{1,0:T(8,128)(2,1)}, bf16[3,128,8192]{2,1,0:T(8,128)(2,1)}) custom-call(s32[4]{0:T(128)} %copy-done.3, s32[4,16]{1,0:T(4,128)} %copy-done.1, s32[16]{0:T(128)} %copy-done.2, bf16[2048,384]{1,0:T(8,128)(2,1)} %copy-done.4, bf16[8192,384]{1,0:T(8,128)(2,1)} %convolution_convert_fusion.kv_ref, bf16[3,64,2048]{2,1,0:T(8,128)(2,1)} %copy-done, ...), custom_call_target="tpu_custom_call" | custom-call | flops 72477573120 | bytes 20971520 | tf_op jit(solution)/shard_map/attend_backward/pallas_call | solution.py:314
  388.7 11.2 %fusion.48 = bf16[768,3,2,64]{0,3,2,1:T(8,128)(2,1)S(1)} fusion(bf16[3,2,64,8192]{3,2,1,0:T(8,128)(2,1)} %bitcast.128, bf16[8192,768]{1,0:T(8,128)(2,1)} %copy-done.8), kind=kOutput, calls=%fused_computation.85 | convolution fusion | flops 4832133120 | bytes 19464192 | tf_op jit(solution)/shard_map/td,ct->dc/dot_general | solution.py:469
  412.1 6.5 convolution_convert_fusion.2
  419.7 18.2 %fusion.72 = (bf16[8192,768]{1,0:T(8,128)(2,1)}, f32[8192,768]{1,0:T(8,128)}) fusion(bf16[384,8192]{1,0:T(8,128)(2,1)} %bitcast.129, bf16[768,384]{0,1:T(8,128)(2,1)S(1)} %bitcast.138), kind=kOutput, calls=%fused_computation.182 | convolution fusion | flops 4838129664 | bytes 44630016 | tf_op jit(solution)/shard_map/ct,dc->td/dot_general | solution.py:450
  464.0 14.3 %collective-permute-done.47 = bf16[512,768]{1,0:T(8,128)(2,1)S(1)} collective-permute-done((bf16[512,768]{1,0:T(8,128)(2,1)S(1)}, bf16[512,768]{1,0:T(8,128)(2,1)S(1)}, u32[]{:S(2)}, u32[]{:S(2)}) %collective-permute-start.47) | collective-permute-done | bytes 786464 | tf_op jit(solution)/shard_map/ppermute | solution.py:54
  487.3 7.8 collective-permute-done.44
  512.1 6.6 collective-permute-done.49
  522.7 5.9 add_convert_fusion.1
  528.6 47.6 %reduce-scatter.7.cloned.1.call-done = bf16[24,768]{1,0:T(8,128)(2,1)} async-done(((bf16[768,768]{1,0:T(8,128)(2,1)}), bf16[24,768]{1,0:T(8,128)(2,1)}) %reduce-scatter.7.cloned.1.call-update) | async-done | bytes 36880 | tf_op jit(solution)/shard_map/reduce_scatter | solution.py:504
  583.0 40.4 %all-reduce.5 = (f32[768]{0:T(1024)S(1)}, f32[768]{0:T(1024)S(1)}, f32[768]{0:T(1024)S(1)}, f32[768]{0:T(1024)S(1)}) all-reduce(f32[768]{0:T(1024)S(1)} %get-tuple-element.24, f32[768]{0:T(1024)S(1)} %get-tuple-element.29, f32[768]{0:T(1024)S(1)} %copy-done.38, ...), channel_id=6, replica_groups=mesh['seq'=2,'head'=4,'ctx'=4] {'seq','head','ctx'}, use_global_device_ids=true, to_apply=%region_19.20.clone | all-reduce | flops 3072 | bytes 24576
  628.6 60.0 %reduce-scatter.9.cloned.1.call-done = bf16[24,3072]{1,0:T(8,128)(2,1)} async-done(((bf16[768,3072]{1,0:T(8,128)(2,1)}), bf16[24,3072]{1,0:T(8,128)(2,1)}) %reduce-scatter.9.cloned.1.call-update) | async-done | bytes 147472 | tf_op jit(solution)/shard_map/reduce_scatter | solution.py:505
  690.3 109.9 %reduce-scatter.11.cloned.1.call-done = bf16[96,768]{1,0:T(8,128)(2,1)} async-done(((bf16[3072,768]{1,0:T(8,128)(2,1)}), bf16[96,768]{1,0:T(8,128)(2,1)}) %reduce-scatter.11.cloned.1.call-update) | async-done | bytes 147472 | tf_op jit(solution)/shard_map/reduce_scatter | solution.py:506
  (336 shorter events, 189.6 us)
Async XLA Ops:
  7.2 148.8 %all-gather.5.cloned.1.call-start = ((), (), s32[]{:S(2)}) async-start(), calls=%async_computation.5 | async-start | bytes 3852288 | tf_op jit(solution)/shard_map/all_gather | solution.py:377
  9.6 216.6 %all-gather.7.cloned.1.call-start = ((), (), s32[]{:S(2)}) async-start(), calls=%async_computation.6 | async-start | bytes 1216512 | tf_op jit(solution)/shard_map/all_gather | solution.py:380
  10.4 228.2 %all-gather.9.cloned.1.call-start = ((), (), s32[]{:S(2)}) async-start(), calls=%async_computation.7 | async-start | bytes 4866048 | tf_op jit(solution)/shard_map/all_gather | solution.py:381
  11.1 262.6 %all-gather.11.cloned.1.call-start = ((), (), s32[]{:S(2)}) async-start(), calls=%async_computation.8 | async-start | bytes 4866048 | tf_op jit(solution)/shard_map/all_gather | solution.py:382
  19.6 48.6 %collective-permute-start.16 = (bf16[512,768]{1,0:T(8,128)(2,1)}, bf16[512,768]{1,0:T(8,128)(2,1)S(1)}, u32[]{:S(2)}, u32[]{:S(2)}) collective-permute-start(bf16[512,768]{1,0:T(8,128)(2,1)} %param.11), channel_id=1, source_target_pairs={{0,8},{4,12},{8,0},{12,4},{1,9},{5,13},{9,1},{13,5},{2,10},{6,14},... | collective-permute-start | bytes 2359304 | tf_op jit(solution)/shard_map/ppermute | solution.py:54
  20.1 71.8 %collective-permute-start.15 = (bf16[512,768]{1,0:T(8,128)(2,1)}, bf16[512,768]{1,0:T(8,128)(2,1)S(1)}, u32[]{:S(2)}, u32[]{:S(2)}) collective-permute-start(bf16[512,768]{1,0:T(8,128)(2,1)} %param.11), channel_id=1, source_target_pairs={{0,4},{4,0},{8,12},{12,8},{1,5},{5,1},{9,13},{13,9},{2,6},{6,2},{1... | collective-permute-start | bytes 2359304 | tf_op jit(solution)/shard_map/ppermute | solution.py:54
  20.3 485.9 %reduce-scatter.5.cloned.1.call-start = ((), (), s32[]{:S(2)}) async-start(), calls=%async_computation.9 | async-start | bytes 1105920 | tf_op jit(solution)/shard_map/reduce_scatter | solution.py:479
  24.0 40.5 %collective-permute-start.18 = (bf16[512,768]{1,0:T(8,128)(2,1)}, bf16[512,768]{1,0:T(8,128)(2,1)S(1)}, u32[]{:S(2)}, u32[]{:S(2)}) collective-permute-start(bf16[512,768]{1,0:T(8,128)(2,1)} %param.11), channel_id=1, source_target_pairs={{0,1},{1,3},{3,2},{2,0},{4,5},{5,7},{7,6},{6,4},{8,9},{9,11},{11,1... | collective-permute-start | bytes 2359304 | tf_op jit(solution)/shard_map/ppermute | solution.py:67
  27.3 24.9 %collective-permute-start.5 = (s32[2,128]{0,1:T(8,128)S(1)}, s32[2,128]{0,1:T(8,128)S(1)}, u32[]{:S(2)}, u32[]{:S(2)}) collective-permute-start(s32[2,128]{0,1:T(8,128)S(1)} %collective-permute-done.3), channel_id=1, source_target_pairs={{0,8},{4,12},{8,0},{12,4},{1,9},{5,13},{9,1},{13,5},{2,10},{6,14},... | collective-permute-start | bytes 3080 | tf_op jit(solution)/shard_map/ppermute | solution.py:54
  64.5 27.3 %collective-permute-start.22 = (bf16[512,768]{1,0:T(8,128)(2,1)S(1)}, bf16[512,768]{1,0:T(8,128)(2,1)S(1)}, u32[]{:S(2)}, u32[]{:S(2)}) collective-permute-start(bf16[512,768]{1,0:T(8,128)(2,1)S(1)} %collective-permute-done.18), channel_id=1, source_target_pairs={{0,1},{1,3},{3,2},{2,0},{4,5},{5,7},{7,6},{6,4},{8,9},{9,11},{11,1... | collective-permute-start | bytes 2359304 | tf_op jit(solution)/shard_map/ppermute | solution.py:67
  66.0 27.8 %collective-permute-start.20 = (bf16[512,768]{1,0:T(8,128)(2,1)S(1)}, bf16[512,768]{1,0:T(8,128)(2,1)}, u32[]{:S(2)}, u32[]{:S(2)}) collective-permute-start(bf16[512,768]{1,0:T(8,128)(2,1)S(1)} %collective-permute-done.18), channel_id=1, source_target_pairs={{0,8},{4,12},{8,0},{12,4},{1,9},{5,13},{9,1},{13,5},{2,10},{6,14},... | collective-permute-start | bytes 2359304 | tf_op jit(solution)/shard_map/ppermute | solution.py:54
  68.2 27.7 %collective-permute-start.17 = (bf16[512,768]{1,0:T(8,128)(2,1)S(1)}, bf16[512,768]{1,0:T(8,128)(2,1)S(1)}, u32[]{:S(2)}, u32[]{:S(2)}) collective-permute-start(bf16[512,768]{1,0:T(8,128)(2,1)S(1)} %collective-permute-done.16), channel_id=1, source_target_pairs={{0,4},{4,0},{8,12},{12,8},{1,5},{5,1},{9,13},{13,9},{2,6},{6,2},{1... | collective-permute-start | bytes 2359304 | tf_op jit(solution)/shard_map/ppermute | solution.py:54
  93.8 25.8 %collective-permute-start.21 = (bf16[512,768]{1,0:T(8,128)(2,1)}, bf16[512,768]{1,0:T(8,128)(2,1)S(1)}, u32[]{:S(2)}, u32[]{:S(2)}) collective-permute-start(bf16[512,768]{1,0:T(8,128)(2,1)} %collective-permute-done.20), channel_id=1, source_target_pairs={{0,4},{4,0},{8,12},{12,8},{1,5},{5,1},{9,13},{13,9},{2,6},{6,2},{1... | collective-permute-start | bytes 2359304 | tf_op jit(solution)/shard_map/ppermute | solution.py:54
  95.9 38.2 %collective-permute-start.23 = (bf16[512,768]{1,0:T(8,128)(2,1)S(1)}, bf16[512,768]{1,0:T(8,128)(2,1)S(1)}, u32[]{:S(2)}, u32[]{:S(2)}) collective-permute-start(bf16[512,768]{1,0:T(8,128)(2,1)S(1)} %collective-permute-done.22), channel_id=1, source_target_pairs={{0,4},{4,0},{8,12},{12,8},{1,5},{5,1},{9,13},{13,9},{2,6},{6,2},{1... | collective-permute-start | bytes 2359304 | tf_op jit(solution)/shard_map/ppermute | solution.py:54
  407.7 168.5 %reduce-scatter.7.cloned.1.call-start = ((), (), s32[]{:S(2)}) async-start(), calls=%async_computation.10 | async-start | bytes 1216512 | tf_op jit(solution)/shard_map/reduce_scatter | solution.py:504
  411.5 277.1 %reduce-scatter.9.cloned.1.call-start = ((), (), s32[]{:S(2)}) async-start(), calls=%async_computation.11 | async-start | bytes 4866048 | tf_op jit(solution)/shard_map/reduce_scatter | solution.py:505
  418.6 381.5 %reduce-scatter.11.cloned.1.call-start = ((), (), s32[]{:S(2)}) async-start(), calls=%async_computation.12 | async-start | bytes 4866048 | tf_op jit(solution)/shard_map/reduce_scatter | solution.py:506
  462.7 46.8 %collective-permute-start.39 = (bf16[512,768]{1,0:T(8,128)(2,1)S(1)}, bf16[512,768]{1,0:T(8,128)(2,1)}, u32[]{:S(2)}, u32[]{:S(2)}) collective-permute-start(bf16[512,768]{1,0:T(8,128)(2,1)S(1)} %get-tuple-element.42), channel_id=1, source_target_pairs={{0,4},{4,0},{8,12},{12,8},{1,5},{5,1},{9,13},{13,9},{2,6},{6,2},{1... | collective-permute-start | bytes 2359304 | tf_op jit(solution)/shard_map/ppermute | solution.py:54
  463.3 31.8 %collective-permute-start.44 = (bf16[512,768]{1,0:T(8,128)(2,1)S(1)}, bf16[512,768]{1,0:T(8,128)(2,1)S(1)}, u32[]{:S(2)}, u32[]{:S(2)}) collective-permute-start(bf16[512,768]{1,0:T(8,128)(2,1)S(1)} %get-tuple-element.41), channel_id=1, source_target_pairs={{0,8},{4,12},{8,0},{12,4},{1,9},{5,13},{9,1},{13,5},{2,10},{6,14},... | collective-permute-start | bytes 2359304 | tf_op jit(solution)/shard_map/ppermute | solution.py:54
  485.9 26.2 %collective-permute-start.41 = (bf16[512,768]{1,0:T(8,128)(2,1)}, bf16[512,768]{1,0:T(8,128)(2,1)}, u32[]{:S(2)}, u32[]{:S(2)}) collective-permute-start(bf16[512,768]{1,0:T(8,128)(2,1)} %get-tuple-element.39), channel_id=1, source_target_pairs={{0,8},{4,12},{8,0},{12,4},{1,9},{5,13},{9,1},{13,5},{2,10},{6,14},... | collective-permute-start | bytes 2359304 | tf_op jit(solution)/shard_map/ppermute | solution.py:54
  502.1 76.5 %collective-permute-start.36 = (bf16[512,768]{1,0:T(8,128)(2,1)}, bf16[512,768]{1,0:T(8,128)(2,1)}, u32[]{:S(2)}, u32[]{:S(2)}) collective-permute-start(bf16[512,768]{1,0:T(8,128)(2,1)} %get-tuple-element.48), channel_id=1, source_target_pairs={{0,4},{4,0},{8,12},{12,8},{1,5},{5,1},{9,13},{13,9},{2,6},{6,2},{1... | collective-permute-start | bytes 2359304 | tf_op jit(solution)/shard_map/ppermute | solution.py:54
  504.9 73.8 %collective-permute-start.38 = (bf16[512,768]{1,0:T(8,128)(2,1)}, bf16[512,768]{1,0:T(8,128)(2,1)}, u32[]{:S(2)}, u32[]{:S(2)}) collective-permute-start(bf16[512,768]{1,0:T(8,128)(2,1)} %fusion.41), channel_id=1, source_target_pairs={{0,8},{4,12},{8,0},{12,4},{1,9},{5,13},{9,1},{13,5},{2,10},{6,14},... | collective-permute-start | bytes 2359304 | tf_op jit(solution)/shard_map/ppermute | solution.py:54
  506.2 71.4 %all-to-all-start = ((bf16[4,24,576]{2,1,0:T(8,128)(2,1)}), bf16[4,24,576]{2,1,0:T(8,128)(2,1)S(1)}, u32[]{:S(2)}, u32[]{:S(2)}) async-start(bf16[4,24,576]{2,1,0:T(8,128)(2,1)} %bitcast.149), calls=%async_computation.1 | async-start | bytes 245760 | tf_op jit(solution)/shard_map/all_to_all | solution.py:482
  521.1 57.5 %collective-permute-start.50 = (bf16[512,768]{1,0:T(8,128)(2,1)S(1)}, bf16[512,768]{1,0:T(8,128)(2,1)}, u32[]{:S(2)}, u32[]{:S(2)}) collective-permute-start(bf16[512,768]{1,0:T(8,128)(2,1)S(1)} %fusion.39), channel_id=1, source_target_pairs={{0,2},{1,0},{3,1},{2,3},{4,6},{5,4},{7,5},{6,7},{8,10},{9,8},{11,9... | collective-permute-start | bytes 2359304 | tf_op jit(solution)/shard_map/ppermute | solution.py:67
  (85 other events, 1273.5 us)
Sparse Core Ops, SparseCore 0:
  11.4 72.2 all-gather.4
  86.5 55.4 all-gather.6
  144.8 62.9 all-gather.8
  210.4 63.2 all-gather.10
  407.8 61.8 reduce-scatter.4
  475.4 100.7 reduce-scatter.6
  582.6 105.9 reduce-scatter.8
  694.1 106.0 reduce-scatter.10

commit v2 on v1

v2 whole, which is shorter than its diff:
```python
from functools import partial

import jax
import jax.numpy as jnp
from jax import lax
from jax.experimental import pallas as pl
from jax.experimental.pallas import tpu as pltpu
from jax.sharding import PartitionSpec as P

D = 768
HEADS = 12
HDIM = 64
BLOCK = 512
LANES = 128
EPSILON = 1e-05
MASKED = -1e30
LOG2E = 1.4426950408889634
LN2 = 0.6931471805599453
ALL_AXES = ("seq", "head", "ctx")
BF16 = jnp.bfloat16
F32 = jnp.float32


def dot_on(left, right, left_dim, right_dim):
    return lax.dot_general(
        left, right, (((left_dim,), (right_dim,)), ((), ())), preferred_element_type=F32
    )


def norm_rows(values, gain_vec, bias_vec):
    row_mean = jnp.mean(values, axis=-1, keepdims=True)
    centered = values - row_mean
    variance = jnp.mean(centered * centered, axis=-1, keepdims=True)
    inv_rows = lax.rsqrt(variance + EPSILON)
    unit_rows = centered * inv_rows
    return (unit_rows * gain_vec + bias_vec, unit_rows, inv_rows)


def norm_back(grad_norm, unit_rows, inv_rows, gain_vec):
    scaled = grad_norm * gain_vec
    return inv_rows * (
        scaled
        - jnp.mean(scaled, axis=-1, keepdims=True)
        - unit_rows * jnp.mean(scaled * unit_rows, axis=-1, keepdims=True)
    )


def gelu_exact(values):
    return jax.nn.gelu(values, approximate=False)


def swap_head(value, mask):
    count = lax.axis_size("head")
    return lax.ppermute(value, "head", [(i, i ^ mask) for i in range(count)])


def ring_order(count):
    return [0, 1, 3, 2] if count == 4 else list(range(count))


def ring_pairs(count, step):
    order = ring_order(count)
    return [(order[i], order[(i + step) % count]) for i in range(count)]


def ring_send(value, step):
    return lax.ppermute(value, "ctx", ring_pairs(lax.axis_size("ctx"), step))


def plane_blocks(block):
    near = swap_head(block, 2)
    return [block, swap_head(block, 1), near, swap_head(near, 1)]


def split_three(values):
    high = values.astype(BF16)
    rest = values - high.astype(F32)
    middle = rest.astype(BF16)
    low = (rest - middle.astype(F32)).astype(BF16)
    return [high.astype(F32), middle.astype(F32), low.astype(F32)]


def key_marks(valid, lane):
    row = lax.broadcasted_iota(jnp.int32, (BLOCK, LANES), 0)
    real = row < valid
    marks = jnp.where((lane >= 64) & (lane < 67), 1.0, 0.0)
    marks = jnp.where((lane == 67) & jnp.logical_not(real), MASKED, marks)
    return jnp.where((lane == 68) & real, MASKED, marks)


def fill_keys(slots, kv_ref, valid_ref, keys_out, values_t=None, values_out=None, marks_first=0):
    lane = lax.broadcasted_iota(jnp.int32, (BLOCK, LANES), 1)

    def fill(slot, carry):
        rows = pl.ds(pl.multiple_of(slot * BLOCK, BLOCK), BLOCK)
        marks = key_marks(valid_ref[slot + marks_first], lane)
        for head in range(3):
            pair = kv_ref[rows, head * LANES : (head + 1) * LANES].astype(F32)
            keys_out[head, rows, :] = jnp.where(lane < 64, pair, marks).astype(BF16)
            if values_out is not None:
                ones = jnp.where(lane < 3, 1.0, 0.0)
                values_out[head, rows, :] = jnp.where(lane < 64, ones, pair).astype(BF16)
            if values_t is not None:
                turned = pair.T[64:128].astype(BF16)
                values_t[head, :, rows] = jnp.concatenate(
                    [turned, jnp.ones((16, BLOCK), BF16)], axis=0
                )
        return carry

    lax.fori_loop(0, slots, fill, 0)


def query_marks(valid, width):
    row = lax.broadcasted_iota(jnp.int32, (1, width), 1)
    real = jnp.where(row < valid, 1.0, 0.0)
    return [real, 1.0 - real]


def forward_kernel(plane, last, *refs):
    refs = list(refs)
    count_ref, list_ref, valid_ref = refs[:3]
    x_refs, norm_ref, w_kv_ref = refs[3:7], refs[7], refs[8]
    refs = refs[9:]
    if plane == 0:
        w_q_ref = refs.pop(0)
    else:
        q_ref, acc_in = refs.pop(0), refs.pop(0)
    if last:
        before, refs = refs[:plane], refs[plane:]
    kv_ref = refs.pop(0)
    if plane == 0:
        q_ref = refs.pop(0)
    if last:
        out_ref, lse_ref = refs.pop(0), refs.pop(0)
        keys, values_t, q_ext, acc, top, kv_copy, copied = refs
    else:
        acc = refs.pop(0)
        keys, values_t, q_ext = refs
    gain, bias = norm_ref[0:1, :], norm_ref[1:2, :]
    for slot, x_ref in enumerate(x_refs):
        rows = slice(slot * BLOCK, (slot + 1) * BLOCK)
        normed, ignored, ignored_too = norm_rows(x_ref[...].astype(F32), gain, bias)
        normed = normed.astype(BF16)
        kv_ref[rows, :] = dot_on(normed, w_kv_ref[...], 1, 0).astype(BF16)
        if plane == 0:
            own = dot_on(normed, w_q_ref[...], 1, 0) * (HDIM ** (-0.5) * LOG2E)
            q_ref[rows, :] = own.astype(BF16)
    fill_keys(4, kv_ref, valid_ref, keys, values_t=values_t, marks_first=4 * plane)
    if plane == 0:
        acc[...] = jnp.zeros_like(acc)
    else:
        acc[...] = acc_in[...]

    def set_queries(block):
        q_rows = pl.ds(pl.multiple_of(block * BLOCK, BLOCK), BLOCK)
        lane = lax.broadcasted_iota(jnp.int32, (BLOCK, LANES), 1)
        row = lax.broadcasted_iota(jnp.int32, (BLOCK, LANES), 0)
        real = row < valid_ref[block]
        marks = jnp.where((lane == 67) & real, 1.0, 0.0)
        marks = jnp.where((lane == 68) & jnp.logical_not(real), 1.0, marks)
        for head in range(3):
            own = q_ref[q_rows, head * LANES : (head + 1) * LANES].astype(F32)
            q_ext[head] = jnp.where(lane < 64, own, marks).astype(BF16)
        return q_rows

    def scores_of(slot, head):
        rows = pl.ds(pl.multiple_of(slot * BLOCK, BLOCK), BLOCK)
        return dot_on(keys[head, rows, :], q_ext[head], 1, 1)

    def over_queries(block, carry):
        q_rows = set_queries(block)

        def over_keys(item, carry_in):
            slot = list_ref[plane, block, item]
            rows = pl.ds(pl.multiple_of(slot * BLOCK, BLOCK), BLOCK)
            ready = [scores_of(slot, 0), scores_of(slot, 1)]
            for head in range(3):
                if head == 0:
                    ready.append(scores_of(slot, 2))
                weights = jnp.exp2(ready.pop(0)).astype(BF16)
                acc[head, :, q_rows] += dot_on(values_t[head, :, rows], weights, 1, 0)
            return carry_in

        lax.fori_loop(0, count_ref[plane, block], over_keys, 0)
        return carry

    lax.fori_loop(0, 4, over_queries, 0)
    if not last:
        return
    sums = acc[:, 64:65, :]
    good = (sums >= 2.0**-60) & (sums <= 2.0**100)
    safe = jnp.min(jnp.where(good, 1.0, 0.0)) > 0.5
    top[...] = jnp.zeros_like(top)

    @pl.when(jnp.logical_not(safe))
    def _():
        top[...] = jnp.full_like(top, MASKED)
        acc[...] = jnp.zeros_like(acc)
        for which, source in enumerate(list(before) + [kv_ref]):
            if which < plane:
                move = pltpu.make_async_copy(source, kv_copy, copied)
                move.start()
                move.wait()
                source = kv_copy
            fill_keys(4, source, valid_ref, keys, values_t=values_t, marks_first=4 * which)

            def over_queries_again(block, carry, which=which):
                q_rows = set_queries(block)

                def with_max(item, carry_in):
                    slot = list_ref[which, block, item]
                    rows = pl.ds(pl.multiple_of(slot * BLOCK, BLOCK), BLOCK)
                    for head in range(3):
                        scores = scores_of(slot, head)
                        old = top[head, :, q_rows]
                        now = jnp.maximum(old, jnp.max(scores, axis=0, keepdims=True))
                        weights = jnp.exp2(scores - now).astype(BF16)
                        top[head, :, q_rows] = now
                        acc[head, :, q_rows] = acc[head, :, q_rows] * jnp.exp2(
                            old - now
                        ) + dot_on(values_t[head, :, rows], weights, 1, 0)
                    return carry_in

                lax.fori_loop(0, count_ref[which, block], with_max, 0)
                return carry

            lax.fori_loop(0, 4, over_queries_again, 0)

    for head in range(3):
        total = acc[head, 64:65, :]
        out_ref[head] = (acc[head, 0:64, :] / total).astype(BF16)
        lse_ref[head] = top[head] + jnp.log2(total)


def attend_forward(plane, last, counts, lists, valid, blocks, norms, w_kv, w_q, queries, acc, before):
    kv_rows = 4 * BLOCK
    smem = pl.BlockSpec(memory_space=pltpu.SMEM)
    vmem = pl.BlockSpec(memory_space=pltpu.VMEM)
    anywhere = pl.BlockSpec(memory_space=pl.ANY)
    packed = jax.ShapeDtypeStruct((kv_rows, 3 * LANES), BF16)
    sums = jax.ShapeDtypeStruct((3, 80, kv_rows), F32)
    inputs = [counts, lists, valid] + list(blocks) + [norms, w_kv]
    inputs += [w_q] if plane == 0 else [queries, acc]
    outs = [packed] + ([packed] if plane == 0 else [])
    scratch = [
        pltpu.VMEM((3, kv_rows, LANES), BF16),
        pltpu.VMEM((3, 80, kv_rows), BF16),
        pltpu.VMEM((3, BLOCK, LANES), BF16),
    ]
    in_specs = [smem] * 3 + [vmem] * (len(inputs) - 3)
    if last:
        inputs += list(before)
        in_specs += [anywhere] * len(before)
        outs += [
            jax.ShapeDtypeStruct((3, HDIM, kv_rows), BF16),
            jax.ShapeDtypeStruct((3, 1, kv_rows), F32),
        ]
        scratch += [
            pltpu.VMEM((3, 80, kv_rows), F32),
            pltpu.VMEM((3, 1, kv_rows), F32),
            pltpu.VMEM((kv_rows, 3 * LANES), BF16),
            pltpu.SemaphoreType.DMA,
        ]
    else:
        outs += [sums]
    return pl.pallas_call(
        partial(forward_kernel, plane, last),
        out_shape=tuple(outs),
        in_specs=in_specs,
        out_specs=(vmem,) * len(outs),
        scratch_shapes=scratch,
        compiler_params=pltpu.CompilerParams(vmem_limit_bytes=40 << 20),
        cost_estimate=pl.CostEstimate(
            flops=12 * 1000 * 1000 * 1000, bytes_accessed=10 << 20, transcendentals=7 << 20
        ),
        name="attend_forward",
    )(*inputs)


def backward_kernel(plane, carried, last, *refs):
    refs = list(refs)
    count_ref, list_ref, valid_ref = refs[:3]
    q_ref, kv_ref, out_ref, lse_ref, grad_ref, norm_ref, w_kv_ref, w_q_ref = refs[3:11]
    x_from, refs = refs[11:15], refs[15:]
    if carried:
        dq_in, dw_in, sum_in = refs[:3]
        refs = refs[3:]
    if last:
        keep_ref, send_ref, dw_ref, dwq_ref, sum_ref = refs[:5]
        dq_ref = None
        refs = refs[5:]
    else:
        keep_ref, send_ref, dw_ref, dq_ref, sum_ref = refs[:5]
        refs = refs[5:]
    keys, values, q_ext, g_ext, q_turned, dq_acc, dkv_acc, x_ref, moved = refs
    slots = 4
    moves = [
        pltpu.make_async_copy(x_from[i], x_ref.at[pl.ds(i * BLOCK, BLOCK)], moved.at[i])
        for i in range(slots)
    ]
    if carried:
        moves.append(pltpu.make_async_copy(dq_in, dq_acc, moved.at[4]))
    for move in moves:
        move.start()
    fill_keys(slots, kv_ref, valid_ref, keys, values_out=values, marks_first=4 * plane)
    lane = lax.broadcasted_iota(jnp.int32, (BLOCK, LANES), 1)

    def clear(slot, carry):
        rows = pl.ds(pl.multiple_of(slot * BLOCK, BLOCK), BLOCK)
        for head in range(3):
            dkv_acc[head, :, rows] = jnp.zeros((LANES, BLOCK), F32)
        return carry

    lax.fori_loop(0, slots, clear, 0)
    if carried:
        moves[4].wait()
    else:
        dq_acc[...] = jnp.zeros_like(dq_acc)

    def over_queries(block, carry):
        q_rows = pl.ds(pl.multiple_of(block * BLOCK, BLOCK), BLOCK)
        for head in range(3):
            lanes = slice(head * LANES, (head + 1) * LANES)
            turned = q_ref[q_rows, lanes].astype(F32).T[0:64]
            grad_t = grad_ref[head, :, q_rows].astype(F32)
            delta = jnp.sum(grad_t * out_ref[head, :, q_rows].astype(F32), axis=0, keepdims=True)
            marks = split_three(-lse_ref[head, :, q_rows]) + query_marks(valid_ref[block], BLOCK)
            blank = jnp.zeros((64 - len(marks), BLOCK), F32)
            q_turned[head] = turned.astype(BF16)
            q_ext[head] = jnp.concatenate([turned] + marks + [blank], axis=0).T.astype(BF16)
            minus = split_three(-delta)
            blank = jnp.zeros((64 - len(minus), BLOCK), F32)
            g_ext[head] = jnp.concatenate(minus + [blank, grad_t], axis=0).T.astype(BF16)

        def over_keys(item, carry_in):
            slot = list_ref[plane, block, item]
            rows = pl.ds(pl.multiple_of(slot * BLOCK, BLOCK), BLOCK)

            def products(head):
                return (
                    dot_on(q_ext[head], keys[head, rows, :], 1, 1),
                    dot_on(g_ext[head], values[head, rows, :], 1, 1),
                )

            ready = [products(0)]
            for head in range(3):
                lanes = slice(head * LANES, (head + 1) * LANES)
                if head < 2:
                    ready.append(products(head + 1))
                scores, grad_probs = ready.pop(0)
                probs = jnp.exp2(scores)
                grad_scores = (probs * grad_probs).astype(BF16)
                dkv_acc[head, 64:128, rows] += dot_on(
                    grad_ref[head, :, q_rows], probs.astype(BF16), 1, 0
                )
                dkv_acc[head, 0:64, rows] += dot_on(q_turned[head], grad_scores, 1, 0)
                dq_acc[q_rows, lanes] += dot_on(grad_scores, keys[head, rows, :], 1, 0)
            return carry_in

        lax.fori_loop(0, count_ref[plane, block], over_keys, 0)
        return carry

    lax.fori_loop(0, 4, over_queries, 0)
    for move in moves[:4]:
        move.wait()
    if not last:
        leave = pltpu.make_async_copy(dq_acc, dq_ref, moved.at[4])
        leave.start()
    if carried:
        dw_ref[...] = dw_in[...]
        sum_ref[...] = sum_in[...]
    else:
        dw_ref[...] = jnp.zeros_like(dw_ref)
        sum_ref[...] = jnp.zeros_like(sum_ref)
    if last:
        dwq_ref[...] = jnp.zeros_like(dwq_ref)
    gain, bias = norm_ref[0:1, :], norm_ref[1:2, :]

    def finish(slot, carry):
        rows = pl.ds(pl.multiple_of(slot * BLOCK, BLOCK), BLOCK)
        pieces = []
        for head in range(3):
            pieces.append(dkv_acc[head, 0:64, rows] * LN2)
            pieces.append(dkv_acc[head, 64:128, rows])
        turned = jnp.concatenate(pieces, axis=0)
        part = dot_on(turned.T.astype(BF16), w_kv_ref[...], 1, 0)
        values_now = x_ref[rows, :].astype(F32)
        normed, unit, ignored = norm_rows(values_now, gain, bias)
        normed = normed.astype(BF16)
        dw_ref[...] += dot_on(turned.astype(BF16), normed, 1, 0)
        if last:
            scaled = [
                jnp.where(lane < 64, dq_acc[rows, h * LANES : (h + 1) * LANES], 0.0)
                for h in range(3)
            ]
            scaled = jnp.concatenate(scaled, axis=1) * HDIM ** (-0.5)
            part = part + dot_on(scaled.astype(BF16), w_q_ref[...], 1, 0)
            dwq_ref[...] += dot_on(scaled.T.astype(BF16), normed, 1, 0)
        sum_ref[0:1, :] += jnp.sum(part * unit, axis=0, keepdims=True)
        sum_ref[1:2, :] += jnp.sum(part, axis=0, keepdims=True)
        low = part.astype(BF16)

        @pl.when(slot % 2 == 0)
        def _():
            keep_ref[slot // 2] = low

        @pl.when(slot % 2 == 1)
        def _():
            send_ref[slot // 2] = low

        return carry

    lax.fori_loop(0, slots, finish, 0)
    if not last:
        leave.wait()


def attend_backward(
    plane, counts, lists, valid, queries, key_vals, attended, lse, grads, norms, w_kv_t, w_q_t, blocks, carry, last
):
    q_rows = queries.shape[0]
    smem = pl.BlockSpec(memory_space=pltpu.SMEM)
    vmem = pl.BlockSpec(memory_space=pltpu.VMEM)
    anywhere = pl.BlockSpec(memory_space=pl.ANY)
    carry = list(carry)
    half = jax.ShapeDtypeStruct((2, BLOCK, D), BF16)
    weight = jax.ShapeDtypeStruct((3 * LANES, D), F32)
    fourth = weight if last else jax.ShapeDtypeStruct((q_rows, 3 * LANES), F32)
    return pl.pallas_call(
        partial(backward_kernel, plane, bool(carry), last),
        out_shape=(half, half, weight, fourth, jax.ShapeDtypeStruct((8, D), F32)),
        in_specs=[smem] * 3 + [vmem] * 8 + [anywhere] * 4 + [anywhere, vmem, vmem][: len(carry)],
        out_specs=(vmem, vmem, vmem, vmem if last else anywhere, vmem),
        scratch_shapes=[
            pltpu.VMEM((3, q_rows, LANES), BF16),
            pltpu.VMEM((3, q_rows, LANES), BF16),
            pltpu.VMEM((3, BLOCK, LANES), BF16),
            pltpu.VMEM((3, BLOCK, LANES), BF16),
            pltpu.VMEM((3, HDIM, BLOCK), BF16),
            pltpu.VMEM((q_rows, 3 * LANES), F32),
            pltpu.VMEM((3, LANES, q_rows), F32),
            pltpu.VMEM((q_rows, D), BF16),
            pltpu.SemaphoreType.DMA((5,)),
        ],
        compiler_params=pltpu.CompilerParams(vmem_limit_bytes=44 << 20),
        cost_estimate=pl.CostEstimate(
            flops=25 * 1000 * 1000 * 1000, bytes_accessed=16 << 20, transcendentals=7 << 20
        ),
        name="attend_backward",
    )(
        counts, lists, valid, queries, key_vals, attended, lse, grads, norms, w_kv_t, w_q_t, *blocks, *carry
    )


def erf_of(values):
    clamped = jnp.clip(values, -4.0, 4.0)
    square = clamped * clamped
    top = jnp.float32(-2.72614225801306e-10)
    for term in (
        2.77068142495902e-08,
        -2.10102402082508e-06,
        -5.69250639462346e-05,
        -7.34990630326855e-04,
        -2.95459980854025e-03,
        -1.60960333262415e-02,
    ):
        top = top * square + term
    low = jnp.float32(-1.45660718464996e-05)
    for term in (
        -2.13374055278905e-04,
        -1.68282697438203e-03,
        -7.37332916720468e-03,
        -1.42647390514189e-02,
    ):
        low = low * square + term
    return clamped * top / low


def middle_kernel(pieces, shard, *refs):
    refs = list(refs)
    start_ref, group_ref = refs[:2]
    merged_refs, refs = refs[2:6], refs[6:]
    token_ref, cot_ref, norm_ref = refs[:3]
    piece_refs, refs = refs[3 : 3 + pieces], refs[3 + pieces :]
    output_ref, grad_y_ref, grad_z_ref, h_two_ref, hidden_ref, grad_up_ref = refs[:6]
    part_refs, sum_ref, refs = refs[6:10], refs[10], refs[11:]
    w_out, w_up, w_down, moved = refs
    pair = piece_refs[0].shape[0] // 9

    def moves_of(weight):
        moves = []
        for i, piece in enumerate(piece_refs):
            if weight < 5:
                source = piece.at[pl.ds(weight * pair, pair)]
                rows = pl.ds(pl.multiple_of(start_ref[i] * shard, pair), pair)
                target = w_out.at[rows] if weight == 0 else w_up.at[weight - 1, rows]
            else:
                source = piece.at[pl.ds(5 * pair, 4 * pair)]
                rows = pl.ds(pl.multiple_of(start_ref[i] * 4 * shard, 4 * pair), 4 * pair)
                target = w_down.at[rows]
            moves.append(pltpu.make_async_copy(source, target, moved.at[weight, i]))
        return moves

    arriving = [moves_of(weight) for weight in range(6)]
    for weight in (0, 1, 5, 2, 3, 4):
        for move in arriving[weight]:
            move.start()
    for move in arriving[0]:
        move.wait()
    y_one = token_ref[...].astype(F32)
    group = D // 4
    for j, merged_ref in enumerate(merged_refs):
        rows = pl.ds(pl.multiple_of(group_ref[j] * group, group), group)
        turned = merged_ref[...].astype(F32).T.astype(BF16)
        y_one = y_one + dot_on(turned, w_out[rows, :], 1, 0)
    grad_y_ref[...] = y_one
    gain, bias = norm_ref[0:1, :], norm_ref[1:2, :]
    normed, unit, inv_rows = norm_rows(y_one, gain, bias)
    h_two_ref[...] = normed.astype(BF16)

    output_sum = jnp.zeros((BLOCK, D), F32)
    grad_sum = jnp.zeros((BLOCK, D), F32)
    for j in range(4):
        for move in arriving[1 + j]:
            move.wait()
        if j == 0:
            for move in arriving[5]:
                move.wait()
        columns = slice(j * D, (j + 1) * D)
        up = dot_on(h_two_ref[...], w_up[j], 1, 0)
        grad_hidden = dot_on(cot_ref[...], w_down[columns, :], 1, 1)
        normal = 0.5 + 0.5 * erf_of(up * 0.7071067811865476)
        density = jnp.exp(-0.5 * up * up) * 0.3989422804014327
        hidden = (up * normal).astype(BF16)
        grad_up = (grad_hidden * (normal + up * density)).astype(BF16)
        hidden_ref[:, columns] = hidden
        grad_up_ref[:, columns] = grad_up
        output_sum = output_sum + dot_on(hidden, w_down[columns, :], 1, 0)
        grad_sum = grad_sum + dot_on(grad_up, w_up[j], 1, 1)
    y_one = grad_y_ref[...]
    output_ref[...] = (y_one + output_sum).astype(BF16)
    normed, unit, inv_rows = norm_rows(y_one, gain, bias)
    sum_ref[...] = jnp.zeros_like(sum_ref)
    sum_ref[0:1, :] = jnp.sum(grad_sum * unit, axis=0, keepdims=True)
    sum_ref[1:2, :] = jnp.sum(grad_sum, axis=0, keepdims=True)
    grad_y = cot_ref[...].astype(F32) + norm_back(grad_sum, unit, inv_rows, gain)
    grad_y_ref[...] = grad_y
    grad_z = grad_y.astype(BF16)
    grad_z_ref[...] = grad_z
    for j, part_ref in enumerate(part_refs):
        rows = pl.ds(pl.multiple_of(group_ref[j] * group, group), group)
        part_ref[...] = dot_on(w_out[rows, :], grad_z, 1, 1).astype(BF16)


def middle(starts, groups, merged, tokens, cotangent, norms, pieces, shard):
    smem = pl.BlockSpec(memory_space=pltpu.SMEM)
    vmem = pl.BlockSpec(memory_space=pltpu.VMEM)
    anywhere = pl.BlockSpec(memory_space=pl.ANY)
    rows = tokens.shape[0]

    def shape(columns, dtype, height=rows):
        return jax.ShapeDtypeStruct((height, columns), dtype)

    return pl.pallas_call(
        partial(middle_kernel, len(pieces), shard),
        out_shape=(
            shape(D, BF16),
            shape(D, F32),
            shape(D, BF16),
            shape(D, BF16),
            shape(4 * D, BF16),
            shape(4 * D, BF16),
        )
        + (shape(rows, BF16, D // 4),) * 4
        + (shape(D, F32, 8),),
        in_specs=[smem, smem] + [vmem] * 7 + [anywhere] * len(pieces),
        out_specs=(vmem,) * 11,
        scratch_shapes=[
            pltpu.VMEM((D, D), BF16),
            pltpu.VMEM((4, D, D), BF16),
            pltpu.VMEM((4 * D, D), BF16),
            pltpu.SemaphoreType.DMA((6, len(pieces))),
        ],
        compiler_params=pltpu.CompilerParams(vmem_limit_bytes=56 << 20),
        cost_estimate=pl.CostEstimate(
            flops=12 * 1000 * 1000 * 1000, bytes_accessed=24 << 20, transcendentals=3 << 20
        ),
        name="middle",
    )(starts, groups, *merged, tokens, cotangent, norms, *pieces)


def scene_lists(same):
    number = same.shape[-1]
    slot = jnp.arange(number)
    counts = jnp.sum(same, axis=-1).astype(jnp.int32)
    earlier = slot[None, :] < slot[:, None]
    place = jnp.sum(same[:, :, None, :] & earlier, axis=-1)
    hits = same[:, :, None, :] & (place[:, :, None, :] == slot[:, None])
    lists = jnp.sum(jnp.where(hits, slot, 0), axis=-1)
    return counts, lists.astype(jnp.int32)


def halve(value, axis, bit, send):
    keep = lax.dynamic_index_in_dim(value, bit, axis, keepdims=False)
    give = lax.dynamic_index_in_dim(value, 1 - bit, axis, keepdims=False)
    return (keep.astype(F32) + send(give).astype(F32)).astype(BF16)


def ring_sources(count):
    order = ring_order(count)
    table = [[order[(order.index(c) - r) % count] for r in range(count)] for c in range(count)]
    return jnp.array(table, jnp.int32)[lax.axis_index("ctx")]


def sum_over_seq(value):
    count = lax.axis_size("seq")
    me = lax.axis_index("seq")
    while count > 1:
        count //= 2
        bit = (me // count) % 2
        pairs = [(i, i ^ count) for i in range(lax.axis_size("seq"))]
        value = halve(
            value.reshape((2, count) + value.shape[1:]),
            0,
            bit,
            lambda give: lax.ppermute(give, "seq", pairs),
        )
    return value.reshape(value.shape[1:])


def gather_bit(value, bit, send):
    other = send(value)
    first = jnp.where(bit == 0, value, other)
    return jnp.concatenate([first, jnp.where(bit == 0, other, value)], axis=0)


def gather_seq(value):
    count, reach = lax.axis_size("seq"), 1
    me = lax.axis_index("seq")
    while reach < count:
        pairs = [(i, i ^ reach) for i in range(count)]
        value = gather_bit(
            value[None], (me // reach) % 2, lambda v: lax.ppermute(v, "seq", pairs)
        ).reshape((2 * reach,) + value.shape[1:])
        reach *= 2
    return value


def swap_seq(value, mask=1):
    return lax.ppermute(value, "seq", [(i, i ^ mask) for i in range(lax.axis_size("seq"))])


def in_order(blocks, sources, shard):
    count = len(blocks)
    full = jnp.zeros((count,) + blocks[0].shape, BF16)
    for r in range(count):
        full = lax.dynamic_update_index_in_dim(full, blocks[r], sources[r], 0)
    halves = []
    for half in range(2):
        part = full[half * (count // 2) : (half + 1) * (count // 2)]
        cut = [part[:, i * shard : (i + 1) * shard] for i in range(5)] + [part[:, 5 * shard :]]
        halves.append(jnp.concatenate([c.reshape(-1, D) for c in cut], axis=0))
    return halves


def join_halves(pieces, starts, offs, rows):
    cuts = [i * rows for i in range(1, 6)]
    joined, firsts = [], []
    for base in range(0, len(pieces), len(offs)):
        for i, (half, x, y) in enumerate(offs):
            if half == 0:
                other = base + offs.index((1, x, y))
                both = zip(jnp.split(pieces[base + i], cuts), jnp.split(pieces[other], cuts))
                joined.append(jnp.concatenate([part for pair in both for part in pair], axis=0))
                firsts.append(starts[base + i])
    return joined, firsts


def gather_ctx(value):
    count = lax.axis_size("ctx")
    sources = ring_sources(count)
    whole = jnp.zeros((count,) + value.shape, value.dtype)
    whole = lax.dynamic_update_index_in_dim(whole, value, sources[0], 0)
    for r in range(1, count):
        whole = lax.dynamic_update_index_in_dim(whole, ring_send(value, r), sources[r], 0)
    return whole


def sum_over_core(value):
    seqs, ctxs = lax.axis_size("seq"), lax.axis_size("ctx")
    rows = value.shape[0] // (seqs * ctxs * 4)
    value = value.reshape(seqs, 2, 2, ctxs, rows, value.shape[1])
    bit = lax.axis_index("head") % 2
    return halve(value, 2, bit, lambda give: swap_head(give, 1))


def sum_over_x(value):
    bit = lax.axis_index("head") // 2
    return halve(value, 0, bit, lambda give: swap_head(give, 2))


def send_term(value, r):
    source = ring_sources(lax.axis_size("ctx"))[r]
    return ring_send(lax.dynamic_index_in_dim(value, source, 0, keepdims=False), -r)


def sum_terms(value, terms):
    source = ring_sources(lax.axis_size("ctx"))[0]
    total = lax.dynamic_index_in_dim(value, source, 0, keepdims=False).astype(F32)
    for term in terms:
        total = total + term.astype(F32)
    return total


def sum_over_ctx(value):
    count = lax.axis_size("ctx")
    sources = ring_sources(count)
    total = lax.dynamic_index_in_dim(value, sources[0], 0, keepdims=False).astype(F32)
    for r in range(1, count):
        give = lax.dynamic_index_in_dim(value, sources[r], 0, keepdims=False)
        total = total + ring_send(give, -r).astype(F32)
    return total


def tie(*values):
    return lax.optimization_barrier(values)


def body(
    tokens,
    segment_ids,
    w_qkv,
    w_out,
    w_up,
    w_down,
    gain_one,
    bias_one,
    gain_two,
    bias_two,
    cotangent,
):
    heads_ax = lax.axis_size("head")
    ctx_ax = lax.axis_size("ctx")
    seq_ax = lax.axis_size("seq")
    me_head = lax.axis_index("head")
    tok_rows = tokens.shape[0]
    group = D // heads_ax
    shard = w_qkv.shape[0]

    order = [me_head ^ j for j in range(heads_ax)]
    sources = ring_sources(ctx_ax)

    padding = tok_rows - jnp.sum(segment_ids >= 0)
    about = jnp.stack([segment_ids[0], padding // 16, padding % 16]).astype(BF16)
    extra = jnp.stack([gain_one, bias_one, gain_two, bias_two], axis=1)
    extra = jnp.concatenate([extra, jnp.broadcast_to(about[None, :], (shard, 3))], axis=1)
    extra = jnp.pad(extra, ((0, 0), (0, LANES - 7)))
    packed = jnp.swapaxes(w_qkv.reshape(shard, heads_ax, 3 * group), 0, 1)
    packed = jnp.concatenate(
        [packed, jnp.broadcast_to(extra[None], (heads_ax,) + extra.shape)], axis=2
    )
    wide = 3 * group + LANES
    packed = gather_seq(packed[None])
    pieces = []
    for j in range(heads_ax):
        piece = lax.dynamic_index_in_dim(packed, order[j], 1, keepdims=False)
        pieces.append(swap_head(piece, j) if j else piece)
    packed = jnp.zeros((heads_ax, seq_ax, shard, wide), BF16)
    for j in range(heads_ax):
        packed = lax.dynamic_update_index_in_dim(packed, pieces[j], order[j], 0)
    packed = gather_ctx(packed)
    packed = jnp.transpose(packed, (2, 1, 0, 3, 4)).reshape(D, wide)

    w_rest = jnp.concatenate(
        [w_out] + [w_up[:, i * D : (i + 1) * D] for i in range(4)] + [w_down], axis=0
    )
    rest = [w_rest]
    near, ahead, behind = swap_head(tokens, 2), ring_send(tokens, 1), ring_send(w_rest, 1)
    near, ahead, behind, packed = tie(near, ahead, behind, packed)
    rest.append(behind)

    g_one, b_one, g_two, b_two = [packed[:, 3 * group + i].astype(F32) for i in range(4)]
    norm_one = jnp.pad(jnp.stack([g_one, b_one]), ((0, 6), (0, 0)))
    w_mine = packed[:, : 3 * group].reshape(D, 3, 3, HDIM)
    w_kv = w_mine[:, :, 1:].reshape(D, 6 * HDIM)
    w_q = jnp.pad(w_mine[:, :, :1], ((0, 0), (0, 0), (0, 1), (0, 0))).reshape(D, 6 * HDIM)
    w_kv_t, w_q_t = w_kv.T, w_q.T
    about_all = packed[::shard, 3 * group + 4 : 3 * group + 7].astype(jnp.int32)
    about_all = lax.dynamic_index_in_dim(
        about_all.reshape(seq_ax, heads_ax, ctx_ax, 3), lax.axis_index("seq"), 0, keepdims=False
    )
    pick_head = jnp.stack(order)[:, None] == jnp.arange(heads_ax)[None, :]
    pick_ctx = sources[:, None] == jnp.arange(ctx_ax)[None, :]
    pick = pick_ctx[:, None, None, :] & pick_head[None, :, :, None]
    slot_about = jnp.sum(jnp.where(pick[..., None], about_all[None, None], 0), axis=(2, 3))
    slot_ids = slot_about[:, :, 0]
    slot_valid = (tok_rows - (slot_about[:, :, 1] * 16 + slot_about[:, :, 2])).reshape(-1)
    counts, lists = scene_lists(slot_ids[0][None, :, None] == slot_ids[:, None, :])

    planes, key_vals, queries, acc = [], [], None, None
    block = tokens
    ready = None
    for r in range(ctx_ax + 1):
        if r < ctx_ax:
            travelers = [swap_head(block, 1), swap_head(near, 1)]
        else:
            travelers = []
        if r + 1 < ctx_ax:
            travelers.append(swap_head(ahead, 2))
        if r + 2 < ctx_ax:
            travelers.append(ring_send(ahead, 1))
            travelers.append(ring_send(rest[-1], 1))
        count = len(travelers)
        if r == ctx_ax - 2:
            halves = in_order(rest, sources, shard)
            travelers += [swap_head(halves[0], 2), swap_seq(halves[0]), swap_seq(halves[1])]
        if r == ctx_ax - 1:
            travelers += [swap_head(halves[1], 2), swap_seq(x_first)]
            travelers += [swap_head(v, 1) for v in halves]
        if r == ctx_ax:
            travelers += [swap_seq(x_second)]
            travelers += [swap_head(v, 1) for v in (x_first, y_first, y_second, xy_first)]
        results = []
        if ready is not None:
            results = list(
                attend_forward(
                    r - 1,
                    r == ctx_ax,
                    counts,
                    lists,
                    slot_valid,
                    ready,
                    norm_one,
                    w_kv,
                    w_q,
                    queries,
                    acc,
                    key_vals,
                )
            )
        tied = list(tie(*travelers, *results))
        extra, tied = tied[count : len(travelers)], tied[:count] + tied[len(travelers) :]
        if r == ctx_ax - 2:
            x_first, y_first, y_second = extra
        if r == ctx_ax - 1:
            x_second, xy_first = extra[:2]
            cores = extra[2:]
        if r == ctx_ax:
            xy_second = extra[0]
            cores += extra[1:]
            results = tied
            break
        planes.append([block, tied.pop(0), near, tied.pop(0)])
        ready = planes[-1]
        if r + 1 < ctx_ax:
            block, near = ahead, tied.pop(0)
        if r + 2 < ctx_ax:
            ahead = tied.pop(0)
            rest.append(tied.pop(0))
        if results:
            key_vals.append(tied.pop(0))
            if r == 1:
                queries = tied.pop(0)
            acc = tied.pop(0)
    key_vals.append(results[0])
    attended, lse = results[1:]
    cores += [swap_head(v, 1) for v in (x_second, xy_second)]
    owns = [halves[0], halves[1], x_first, y_first, y_second, xy_first, x_second, xy_second]
    offs = [(0, 0, 0), (1, 0, 0), (0, 1, 0), (0, 0, 1), (1, 0, 1), (0, 1, 1), (1, 1, 0), (1, 1, 1)]
    me_x, me_core, me_seq = me_head // 2, me_head % 2, lax.axis_index("seq")
    pieces, starts = [], []
    for core, arrays in enumerate((owns, cores)):
        for array, (half, x, y) in zip(arrays, offs):
            pieces.append(array)
            starts.append((half, (me_x ^ x) * 2 + (me_core ^ core), y))
    reach = 2
    while reach < seq_ax:
        pieces += [swap_seq(array, reach) for array in pieces]
        starts += [(half, place, y ^ reach) for half, place, y in starts]
        reach *= 2
    starts = [
        ((me_seq ^ y) * heads_ax + place) * ctx_ax + half * (ctx_ax // 2)
        for half, place, y in starts
    ]
    if (ctx_ax // 2 * shard) % 8:
        pieces, starts = join_halves(pieces, starts, offs, ctx_ax // 2 * shard)
    starts = jnp.stack(starts).astype(jnp.int32)

    merged = []
    for j in range(heads_ax):
        part = attended[:, :, j * tok_rows : (j + 1) * tok_rows].reshape(group, tok_rows)
        merged.append(swap_head(part, j) if j else part)

    norm_two = jnp.pad(jnp.stack([g_two, b_two]), ((0, 6), (0, 0)))
    groups = jnp.stack(order).astype(jnp.int32)
    output, grad_y_one, grad_z, h_two, hidden, grad_up, *rest_out = middle(
        starts, groups, merged, tokens, cotangent, norm_two, pieces, shard
    )
    grad_merged, sums_two = rest_out[:4], rest_out[4]

    grad_parts = [swap_head(p, j) if j else p for j, p in enumerate(grad_merged)]
    grad_w_down = jnp.einsum("tf,td->fd", hidden, cotangent, preferred_element_type=F32)
    down_sum = sum_over_core(grad_w_down.astype(BF16))
    grad_w_up = jnp.einsum("td,tf->df", h_two, grad_up, preferred_element_type=F32)
    grad_w_up = grad_w_up.astype(BF16)
    grad_w_out = jnp.zeros((heads_ax, group, D), BF16)
    for j in range(heads_ax):
        part = jnp.einsum("at,td->ad", merged[j], grad_z, preferred_element_type=F32)
        grad_w_out = lax.dynamic_update_index_in_dim(grad_w_out, part.astype(BF16), order[j], 0)
    sums_two = jnp.pad(sums_two, ((0, LANES - 8), (0, 0))).T.astype(BF16)
    grad_w_out = jnp.concatenate([grad_w_out.reshape(D, D), sums_two], axis=1)
    tied = tie(down_sum, grad_w_up, grad_w_out, *grad_parts)
    down_sum, grad_w_up, grad_w_out = tied[:3]
    grad_local = jnp.concatenate(tied[3:], axis=1).reshape(3, HDIM, heads_ax * tok_rows)
    up_sum, out_sum = sum_over_core(grad_w_up), sum_over_core(grad_w_out)
    down_sum = sum_over_seq(down_sum)

    carry, traveling, by_x, given = (), None, None, None
    down_terms, wide_terms = [], []
    for r in reversed(range(ctx_ax)):
        step = ctx_ax - 1 - r
        travelers = []
        if step >= 1:
            low = keep.astype(F32) + swap_head(give, 1).astype(F32)
            travelers.append(low.astype(BF16))
        if step >= 2:
            moved = by_x[0].astype(F32) + swap_head(by_x[1], 2).astype(F32)
            if step >= 3:
                moved = moved + ring_send(traveling, -1).astype(F32)
            travelers.append(moved.astype(BF16))
        count = len(travelers)
        if step == 0:
            travelers += [down_sum, up_sum, out_sum]
        if step == 1:
            wide_sum = sum_over_seq(jnp.concatenate([up_sum, out_sum], axis=-1))
            down_sum = sum_over_x(down_sum)
            travelers += [down_sum, wide_sum]
        if step == 2:
            wide_sum = sum_over_x(wide_sum)
            travelers += [wide_sum] + [send_term(down_sum, i) for i in (1, 2)]
        if step == 3:
            travelers += [send_term(down_sum, 3), send_term(wide_sum, 1)]
        keep, give, dw_kv, fourth, sums = attend_backward(
            r,
            counts,
            lists,
            slot_valid,
            queries,
            key_vals[r],
            attended,
            lse,
            grad_local,
            norm_one,
            w_kv_t,
            w_q_t,
            planes[r],
            carry,
            r == 0,
        )
        keep, give, fourth, dw_kv, sums, *travelers = tie(
            keep, give, fourth, dw_kv, sums, *travelers
        )
        carry = (fourth, dw_kv, sums)
        if step >= 1:
            by_x = travelers[0]
        if step >= 2:
            traveling = travelers[1]
        travelers = travelers[count:]
        if step == 0:
            down_sum, up_sum, out_sum = travelers
        if step == 1:
            down_sum, wide_sum = travelers
        if step == 2:
            wide_sum, *down_terms = travelers
        if step == 3:
            down_terms.append(travelers[0])
            wide_terms.append(travelers[1])
    last_x = keep.astype(F32) + swap_head(give, 1).astype(F32)
    moved = by_x[0].astype(F32) + swap_head(by_x[1], 2).astype(F32)
    moved = (moved + ring_send(traveling, -1).astype(F32)).astype(BF16)
    grad_h_one = last_x[0] + swap_head(last_x[1].astype(BF16), 2).astype(F32)
    grad_h_one = grad_h_one + ring_send(moved, -1).astype(F32)
    wide_terms += [send_term(wide_sum, i) for i in (2, 3)]
    down_sum, wide_sum = sum_terms(down_sum, down_terms), sum_terms(wide_sum, wide_terms)
    up_sum, out_sum = wide_sum[:, : 4 * D], wide_sum[:, 4 * D :]
    dw_q = fourth

    dw_kv = dw_kv.reshape(3, 2, HDIM, D)
    dw_q = dw_q.reshape(3, 2, HDIM, D)
    dw_mine = jnp.concatenate([dw_q[:, :1], dw_kv], axis=1).reshape(3 * group, D)
    dw_mine = jnp.concatenate([dw_mine, jnp.pad(sums, ((0, LANES - 8), (0, 0)))], axis=0)
    dw_mine = dw_mine.T.astype(BF16).reshape(seq_ax, heads_ax, ctx_ax, shard, wide)
    dw_mine = sum_over_seq(dw_mine)
    dw_mine = sum_over_ctx(jnp.swapaxes(dw_mine, 0, 1)).astype(BF16)
    groups = []
    for j in range(heads_ax):
        part = lax.dynamic_index_in_dim(dw_mine, order[j], 0, keepdims=False)
        groups.append(swap_head(part, j) if j else part)
    groups = jnp.stack(groups)
    groups = jnp.stack(
        [lax.dynamic_index_in_dim(groups, o, 0, keepdims=False) for o in order]
    ).astype(F32)
    grad_w_qkv = jnp.swapaxes(groups[:, :, : 3 * group], 0, 1).reshape(shard, 3 * D)
    norm_sums = jnp.sum(groups[:, :, 3 * group : 3 * group + 2], axis=0)

    ignored, unit_one, inv_one = norm_rows(tokens.astype(F32), g_one, b_one)
    grad_tokens = (grad_y_one + norm_back(grad_h_one, unit_one, inv_one, g_one)).astype(BF16)
    return (
        output,
        grad_tokens,
        grad_w_qkv,
        out_sum[:, :D],
        up_sum,
        down_sum,
        norm_sums[:, 0],
        norm_sums[:, 1],
        out_sum[:, D],
        out_sum[:, D + 1],
    )


def solution(mesh):
    rows = P(ALL_AXES, None)
    vector = P(ALL_AXES)
    return jax.shard_map(
        body,
        mesh=mesh,
        in_specs=(rows, vector, rows, rows, rows, rows, vector, vector, vector, vector, rows),
        out_specs=(rows, rows, rows, rows, rows, rows, vector, vector, vector, vector),
        check_vma=False,
    )
```

time: 819 us -> 512 us (0.63)
  waiting for transfers between devices: 381 us -> 134 us
  matrix products: 104 us -> 10.1 us
  Pallas kernels: 111 us -> 192 us
  starting transfers between devices: 38.6 us -> 82.4 us
  blocking collectives: 40.4 us -> 0 us
  other arithmetic: 66.7 us -> 33.9 us
  local copies, waits for them, and re-layouts: 52.1 us -> 39.8 us
    reduce_scatter x4 -> x0, waiting for transfers between devices: 218 us -> none  [the longest x1 110 us: body(): scatter(grad_w_down.astype(BF16)).astype(F32)]
    dot_general x13 -> x4, matrix products: 92.8 us -> 2.48 us  [body(): jnp.einsum('at,td->ad', merged[j], grad_z, preferred_element_type=F32)]
    pallas_call x2 -> x9, Pallas kernels: 111 us -> 192 us  [the longest x4 117 us: attend_backward(): pl.pallas_call(partial(backward_kernel, plane, bool(carry), last), out_sh...]
    unnamed x1 -> x0, blocking collectives: 40.4 us -> none
    ppermute x9 -> x21, starting transfers between devices: 11.2 us -> 46.9 us  [ring_send(): return lax.ppermute(value, 'ctx', ring_pairs(lax.axis_size('ctx'), step))]
    ppermute x0 -> x8, waiting for transfers between devices: none -> 35.2 us  [the longest x4 18.5 us: swap_seq(): lax.ppermute(value, 'seq', [(i, i ^ mask) for i in range(lax.axis_size('s...]
    ppermute x42 -> x47, waiting for transfers between devices: 61.2 us -> 30.1 us  [swap_head(): return lax.ppermute(value, 'head', [(i, i ^ mask) for i in range(count)])]
    all_gather x4 -> x0, waiting for transfers between devices: 27.8 us -> none  [the longest x1 27.8 us: body(): full_down = lax.all_gather(w_down, ALL_AXES, axis=0, tiled=True)]
  transfers between devices with their start and end apart: 60 -> 76, of which waited for: 22 -> 21; matrix products, arithmetic and copies ran while one was open for 20% -> 11% of each run, Pallas kernels for 4% -> 33%
where the time goes in v2:
time: 512 us; the launch traced here: 503 us
  Pallas kernels  192 us (38%)
  waiting for transfers between devices  134 us (26%)
  starting transfers between devices  82.4 us (16%)
  local copies, waits for them, and re-layouts  39.8 us (8%)
  other arithmetic  33.9 us (7%)
  between operations  11.3 us (2%)
  matrix products  10.1 us (2%)
    pallas_call x4, Pallas kernels, attend_backward(): pl.pallas_call(partial(backward_kernel, plane, bool(carry), last), out_sh...  117 us
    ppermute x21, waiting for transfers between devices, ring_send(): return lax.ppermute(value, 'ctx', ring_pairs(lax.axis_size('ctx'), step))  68.7 us
    pallas_call x4, Pallas kernels, attend_forward(): pl.pallas_call(partial(forward_kernel, plane, last), out_shape=tuple(outs...  50.3 us
    ppermute x21, starting transfers between devices, ring_send(): return lax.ppermute(value, 'ctx', ring_pairs(lax.axis_size('ctx'), step))  46.9 us
    ppermute x47, waiting for transfers between devices, swap_head(): return lax.ppermute(value, 'head', [(i, i ^ mask) for i in range(count)])  30.1 us
    ppermute x47, starting transfers between devices, swap_head(): return lax.ppermute(value, 'head', [(i, i ^ mask) for i in range(count)])  25.2 us
    pallas_call x1, Pallas kernels, middle(): pl.pallas_call(partial(middle_kernel, len(pieces), shard), out_shape=(sha...  25 us
    ppermute x4, waiting for transfers between devices, swap_seq(): lax.ppermute(value, 'seq', [(i, i ^ mask) for i in range(lax.axis_size('s...  18.5 us
  transfers between devices with their start and end apart: 76, of which 21 were waited for; matrix products, arithmetic and copies ran while one was open for 11% of the time, Pallas kernels for 33%

profile of v2, /device:TPU:0, one launch (start us, length us, event | category | flops | bytes accessed | tf_op | source)
XLA Modules:
  0.0 503.2 jit_solution(7681202480064203447)
XLA Ops:
  40.8 8.3 %collective-permute-done.8 = bf16[4,2,24,704]{3,2,1,0:T(8,128)(2,1)S(1)} collective-permute-done((bf16[4,2,24,704]{3,2,1,0:T(8,128)(2,1)S(1)}, bf16[4,2,24,704]{3,2,1,0:T(8,128)(2,1)S(1)}, u32[]{:S(2)}, u32[]{:S(2)}) %collective-permute-start.8) | collective-permute-done | bytes 270368 | tf_op jit(solution)/shard_map/ppermute | solution.py:67
  49.1 5.6 %collective-permute-done.9 = bf16[4,2,24,704]{3,2,1,0:T(8,128)(2,1)S(1)} collective-permute-done((bf16[4,2,24,704]{3,2,1,0:T(8,128)(2,1)S(1)}, bf16[4,2,24,704]{3,2,1,0:T(8,128)(2,1)S(1)}, u32[]{:S(2)}, u32[]{:S(2)}) %collective-permute-start.9) | collective-permute-done | bytes 270368 | tf_op jit(solution)/shard_map/ppermute | solution.py:67
  58.7 5.8 %collective-permute-start.14 = (bf16[512,768]{1,0:T(8,128)(2,1)}, bf16[512,768]{1,0:T(8,128)(2,1)}, u32[]{:S(2)}, u32[]{:S(2)}) collective-permute-start(bf16[512,768]{1,0:T(8,128)(2,1)} %collective-permute-done.1.refs_3_.refs_11_), channel_id=1, source_target_pairs={{0,1},{1,3},{3,2},{2,0},{4,5},{5,7},{7,6},{6,4},{8,9},{9,11},{11,1... | collective-permute-start | bytes 2359304 | tf_op jit(solution)/shard_map/ppermute | solution.py:67
  70.2 20.6 %collective-permute-done.15 = bf16[216,768]{1,0:T(8,128)(2,1)} collective-permute-done((bf16[216,768]{1,0:T(8,128)(2,1)S(1)}, bf16[216,768]{1,0:T(8,128)(2,1)}, u32[]{:S(2)}, u32[]{:S(2)}) %collective-permute-start.15) | collective-permute-done | bytes 331808 | tf_op jit(solution)/shard_map/ppermute | solution.py:67
  94.3 15.8 %attend_forward.4 = (bf16[2048,384]{1,0:T(8,128)(2,1)S(1)}, bf16[2048,384]{1,0:T(8,128)(2,1)S(1)}, f32[3,80,2048]{2,1,0:T(8,128)S(1)}) custom-call(s32[4,4]{1,0:T(4,128)S(1)} %get-tuple-element.271.refs_0_, s32[4,4,4]{2,1,0:T(4,128)S(1)} %select_reduce_fusion.1.refs_1_, s32[16]{0:T(128)S(1)} %sub.60.refs_2_, bf16[512,768]{1,0:T(8,128)(2,1)S(1)} %copy-done, ...), custom_call_target="tpu_custom_call" | custom-call | flops 12000000000 | bytes 10485760 | tf_op jit(solution)/shard_map/attend_forward/pallas_call | solution.py:266
  111.8 7.6 %collective-permute-done.19 = bf16[216,768]{1,0:T(8,128)(2,1)S(1)} collective-permute-done((bf16[216,768]{1,0:T(8,128)(2,1)}, bf16[216,768]{1,0:T(8,128)(2,1)S(1)}, u32[]{:S(2)}, u32[]{:S(2)}) %collective-permute-start.19) | collective-permute-done | bytes 331808 | tf_op jit(solution)/shard_map/ppermute | solution.py:67
  124.0 13.6 %collective-permute-done.26.refs_13_ = bf16[432,768]{1,0:T(8,128)(2,1)S(1)} collective-permute-done((bf16[432,768]{1,0:T(8,128)(2,1)S(1)}, bf16[432,768]{1,0:T(8,128)(2,1)S(1)}, u32[]{:S(2)}, u32[]{:S(2)}) %collective-permute-start.26) | collective-permute-done | bytes 663584 | tf_op jit(solution)/shard_map/ppermute | solution.py:650
  138.2 10.5 %attend_forward.5 = (bf16[2048,384]{1,0:T(8,128)(2,1)S(1)}, f32[3,80,2048]{2,1,0:T(8,128)S(1)}) custom-call(s32[4,4]{1,0:T(4,128)S(1)} %get-tuple-element.271.refs_0_, s32[4,4,4]{2,1,0:T(4,128)S(1)} %select_reduce_fusion.1.refs_1_, s32[16]{0:T(128)S(1)} %sub.60.refs_2_, bf16[512,768]{1,0:T(8,128)(2,1)} %collective-permute-done.1.refs_3_.refs_11_, ...), custom_call_target="tpu_custom_call" | custom-call | flops 12000000000 | bytes 10485760 | tf_op jit(solution)/shard_map/attend_forward/pallas_call | solution.py:266
  149.8 16.7 %collective-permute-done.23.refs_5_.refs_13_ = bf16[512,768]{1,0:T(8,128)(2,1)S(1)} collective-permute-done((bf16[512,768]{1,0:T(8,128)(2,1)S(1)}, bf16[512,768]{1,0:T(8,128)(2,1)S(1)}, u32[]{:S(2)}, u32[]{:S(2)}) %collective-permute-start.23) | collective-permute-done | bytes 786464 | tf_op jit(solution)/shard_map/ppermute | solution.py:54
  168.1 10.4 %attend_forward.6 = (bf16[2048,384]{1,0:T(8,128)(2,1)S(1)}, f32[3,80,2048]{2,1,0:T(8,128)S(1)}) custom-call(s32[4,4]{1,0:T(4,128)S(1)} %get-tuple-element.271.refs_0_, s32[4,4,4]{2,1,0:T(4,128)S(1)} %select_reduce_fusion.1.refs_1_, s32[16]{0:T(128)S(1)} %sub.60.refs_2_, bf16[512,768]{1,0:T(8,128)(2,1)} %collective-permute-done.14.refs_3_.refs_11_, ...), custom_call_target="tpu_custom_call" | custom-call | flops 12000000000 | bytes 10485760 | tf_op jit(solution)/shard_map/attend_forward/pallas_call | solution.py:266
  179.5 4.4 collective-permute-done.29.refs_14_
  185.5 13.6 %attend_forward.7 = (bf16[2048,384]{1,0:T(8,128)(2,1)S(1)}, bf16[3,64,2048]{2,1,0:T(8,128)(2,1)S(1)}, f32[3,1,2048]{2,1,0:T(1,128)S(1)}) custom-call(s32[4,4]{1,0:T(4,128)S(1)} %get-tuple-element.271.refs_0_, s32[4,4,4]{2,1,0:T(4,128)S(1)} %select_reduce_fusion.1.refs_1_, s32[16]{0:T(128)S(1)} %sub.60.refs_2_, ...), custom_call_target="tpu_custom_call" | custom-call | flops 12000000000 | bytes 10485760 | tf_op jit(solution)/shard_map/attend_forward/pallas_call | solution.py:266
  205.2 5.0 collective-permute-done.38.refs_4_
  213.3 25.0 %middle.1 = (bf16[512,768]{1,0:T(8,128)(2,1)}, f32[512,768]{1,0:T(8,128)}, bf16[512,768]{1,0:T(8,128)(2,1)}, bf16[512,768]{1,0:T(8,128)(2,1)}, bf16[512,3072]{1,...) custom-call(s32[16]{0:T(128)} %stack.140.refs_0_, ...), custom_call_target="tpu_custom_call" | custom-call | flops 12000000000 | bytes 25165824 | tf_op jit(solution)/shard_map/middle/pallas_call | solution.py:564
  238.3 4.5 convolution_convert_fusion.1
  265.7 30.5 %attend_backward.4 = (bf16[2,512,768]{2,1,0:T(8,128)(2,1)S(1)}, bf16[2,512,768]{2,1,0:T(8,128)(2,1)S(1)}, f32[384,768]{1,0:T(8,128)S(1)}, f32[2048,384]{1,0:T(8,128)}, f32[8,768]{1,0:T(8,128)S(1)}) custom-call(s32[4,4]{1,0:T(4,128)S(1)} %get-tuple-element.271.refs_0_, s32[4,4,4]{2,1,0:T(4,128)S(1)} %select_reduce_fusion.1.refs_1_, s32[16]{0:T(128)S(1)} %sub.60.refs_2_, ...), custom_call_target="tpu_custom_call" | custom-call | flops 24999999488 | bytes 16777216 | tf_op jit(solution)/shard_map/attend_backward/pallas_call | solution.py:429
  303.4 24.6 %attend_backward.5 = (bf16[2,512,768]{2,1,0:T(8,128)(2,1)S(1)}, bf16[2,512,768]{2,1,0:T(8,128)(2,1)}, f32[384,768]{1,0:T(8,128)S(1)}, f32[2048,384]{1,0:T(8,128)}, f32[8,768]{1,0:T(8,128)S(1)}) custom-call(s32[4,4]{1,0:T(4,128)S(1)} %get-tuple-element.271.refs_0_, s32[4,4,4]{2,1,0:T(4,128)S(1)} %select_reduce_fusion.1.refs_1_, s32[16]{0:T(128)S(1)} %sub.60.refs_2_, ...), custom_call_target="tpu_custom_call" | custom-call | flops 24999999488 | bytes 16777216 | tf_op jit(solution)/shard_map/attend_backward/pallas_call | solution.py:429
  329.2 8.1 %collective-permute-done.51 = bf16[1,2,4,24,3968]{4,3,2,1,0:T(8,128)(2,1)} collective-permute-done((bf16[1,2,4,24,3968]{4,3,2,1,0:T(8,128)(2,1)}, bf16[1,2,4,24,3968]{4,3,2,1,0:T(8,128)(2,1)}, u32[]{:S(2)}, u32[]{:S(2)}) %collective-permute-start.51) | collective-permute-done | bytes 1523744 | tf_op jit(solution)/shard_map/ppermute | solution.py:626
  342.6 24.6 %attend_backward.6 = (bf16[2,512,768]{2,1,0:T(8,128)(2,1)S(1)}, bf16[2,512,768]{2,1,0:T(8,128)(2,1)}, f32[384,768]{1,0:T(8,128)S(1)}, f32[2048,384]{1,0:T(8,128)}, f32[8,768]{1,0:T(8,128)S(1)}) custom-call(s32[4,4]{1,0:T(4,128)S(1)} %get-tuple-element.271.refs_0_, s32[4,4,4]{2,1,0:T(4,128)S(1)} %select_reduce_fusion.1.refs_1_, s32[16]{0:T(128)S(1)} %sub.60.refs_2_, ...), custom_call_target="tpu_custom_call" | custom-call | flops 24999999488 | bytes 16777216 | tf_op jit(solution)/shard_map/attend_backward/pallas_call | solution.py:429
  367.2 10.0 %collective-permute-start.60 = (bf16[96,768]{1,0:T(8,128)(2,1)}, bf16[96,768]{1,0:T(8,128)(2,1)S(1)}, u32[]{:S(2)}, u32[]{:S(2)}) collective-permute-start(bf16[96,768]{1,0:T(8,128)(2,1)} %get-tuple-element.297), channel_id=1, source_target_pairs={{0,1},{1,3},{3,2},{2,0},{4,5},{5,7},{7,6},{6,4},{8,9},{9,11},{11,1... | collective-permute-start | bytes 442376 | tf_op jit(solution)/shard_map/ppermute | solution.py:67
  379.5 36.9 %attend_backward.7 = (bf16[2,512,768]{2,1,0:T(8,128)(2,1)}, bf16[2,512,768]{2,1,0:T(8,128)(2,1)}, f32[384,768]{1,0:T(8,128)S(1)}, f32[384,768]{1,0:T(8,128)S(1)}, f32[8,768]{1,0:T(8,128)S(1)}) custom-call(s32[4,4]{1,0:T(4,128)S(1)} %get-tuple-element.271.refs_0_, s32[4,4,4]{2,1,0:T(4,128)S(1)} %select_reduce_fusion.1.refs_1_, s32[16]{0:T(128)S(1)} %sub.60.refs_2_, ...), custom_call_target="tpu_custom_call" | custom-call | flops 24999999488 | bytes 16777216 | tf_op jit(solution)/shard_map/attend_backward/pallas_call | solution.py:429
  430.9 8.6 %collective-permute-done.67 = bf16[1,4,4,24,704]{4,3,2,1,0:T(8,128)(2,1)S(1)} collective-permute-done((bf16[1,4,4,24,704]{4,3,2,1,0:T(8,128)(2,1)S(1)}, bf16[1,4,4,24,704]{4,3,2,1,0:T(8,128)(2,1)S(1)}, u32[]{:S(2)}, u32[]{:S(2)}) %collective-permute-start.67) | collective-permute-done | bytes 540704 | tf_op jit(solution)/shard_map/ppermute | solution.py:626
  444.9 20.7 %collective-permute-start.69 = (bf16[4,24,704]{2,1,0:T(8,128)(2,1)S(1)}, bf16[4,24,704]{2,1,0:T(8,128)(2,1)S(1)}, u32[]{:S(2)}, u32[]{:S(2)}) collective-permute-start(bf16[4,24,704]{2,1,0:T(8,128)(2,1)S(1)} %get-tuple-element.296), channel_id=1, source_target_pairs={{0,3},{1,2},{3,0},{2,1},{4,7},{5,6},{7,4},{6,5},{8,11},{9,10},{11,... | collective-permute-start | bytes 405512 | tf_op jit(solution)/shard_map/ppermute | solution.py:67
  483.7 13.7 %collective-permute-done.66 = bf16[512,768]{1,0:T(8,128)(2,1)S(1)} collective-permute-done((bf16[512,768]{1,0:T(8,128)(2,1)}, bf16[512,768]{1,0:T(8,128)(2,1)S(1)}, u32[]{:S(2)}, u32[]{:S(2)}) %collective-permute-start.66) | collective-permute-done | bytes 786464 | tf_op jit(solution)/shard_map/ppermute | solution.py:67
  (451 shorter events, 147.1 us)
Async XLA Ops:
  0.6 54.1 %collective-permute-start = (bf16[512,768]{1,0:T(8,128)(2,1)}, bf16[512,768]{1,0:T(8,128)(2,1)}, u32[]{:S(2)}, u32[]{:S(2)}) collective-permute-start(bf16[512,768]{1,0:T(8,128)(2,1)} %refs_11_.1), channel_id=1, source_target_pairs={{0,8},{4,12},{8,0},{12,4},{1,9},{5,13},{9,1},{13,5},{2,10},{6,14},... | collective-permute-start | bytes 2359304 | tf_op jit(solution)/shard_map/ppermute | solution.py:54
  3.6 51.1 %collective-permute-start.1 = (bf16[512,768]{1,0:T(8,128)(2,1)}, bf16[512,768]{1,0:T(8,128)(2,1)}, u32[]{:S(2)}, u32[]{:S(2)}) collective-permute-start(bf16[512,768]{1,0:T(8,128)(2,1)} %refs_11_.1), channel_id=1, source_target_pairs={{0,1},{1,3},{3,2},{2,0},{4,5},{5,7},{7,6},{6,4},{8,9},{9,11},{11,1... | collective-permute-start | bytes 2359304 | tf_op jit(solution)/shard_map/ppermute | solution.py:67
  17.0 37.7 %collective-permute-start.2 = (bf16[216,768]{1,0:T(8,128)(2,1)S(1)}, bf16[216,768]{1,0:T(8,128)(2,1)S(1)}, u32[]{:S(2)}, u32[]{:S(2)}) collective-permute-start(bf16[216,768]{1,0:T(8,128)(2,1)S(1)} %constant_dynamic-update-slice_fusion), channel_id=1, source_target_pairs={{0,1},{1,3},{3,2},{2,0},{4,5},{5,7},{7,6},{6,4},{8,9},{9,11},{11,1... | collective-permute-start | bytes 995336 | tf_op jit(solution)/shard_map/ppermute | solution.py:67
  58.1 32.7 %collective-permute-start.13 = (bf16[512,768]{1,0:T(8,128)(2,1)}, bf16[512,768]{1,0:T(8,128)(2,1)}, u32[]{:S(2)}, u32[]{:S(2)}) collective-permute-start(bf16[512,768]{1,0:T(8,128)(2,1)} %collective-permute-done.1.refs_3_.refs_11_), channel_id=1, source_target_pairs={{0,8},{4,12},{8,0},{12,4},{1,9},{5,13},{9,1},{13,5},{2,10},{6,14},... | collective-permute-start | bytes 2359304 | tf_op jit(solution)/shard_map/ppermute | solution.py:54
  58.7 32.1 %collective-permute-start.14 = (bf16[512,768]{1,0:T(8,128)(2,1)}, bf16[512,768]{1,0:T(8,128)(2,1)}, u32[]{:S(2)}, u32[]{:S(2)}) collective-permute-start(bf16[512,768]{1,0:T(8,128)(2,1)} %collective-permute-done.1.refs_3_.refs_11_), channel_id=1, source_target_pairs={{0,1},{1,3},{3,2},{2,0},{4,5},{5,7},{7,6},{6,4},{8,9},{9,11},{11,1... | collective-permute-start | bytes 2359304 | tf_op jit(solution)/shard_map/ppermute | solution.py:67
  69.9 41.5 %collective-permute-start.10 = (bf16[512,768]{1,0:T(8,128)(2,1)}, bf16[512,768]{1,0:T(8,128)(2,1)S(1)}, u32[]{:S(2)}, u32[]{:S(2)}) collective-permute-start(bf16[512,768]{1,0:T(8,128)(2,1)} %collective-permute-done.1.refs_3_.refs_11_), channel_id=1, source_target_pairs={{0,4},{4,0},{8,12},{12,8},{1,5},{5,1},{9,13},{13,9},{2,6},{6,2},{1... | collective-permute-start | bytes 2359304 | tf_op jit(solution)/shard_map/ppermute | solution.py:54
  122.5 44.0 %collective-permute-start.28 = (bf16[432,768]{1,0:T(8,128)(2,1)S(1)}, bf16[432,768]{1,0:T(8,128)(2,1)}, u32[]{:S(2)}, u32[]{:S(2)}) collective-permute-start(bf16[432,768]{1,0:T(8,128)(2,1)S(1)} %constant_dynamic-update-slice_fusion.12.refs_10_), channel_id=1, source_target_pairs={{0,8},{4,12},{8,0},{12,4},{1,9},{5,13},{9,1},{13,5},{2,10},{6,14},... | collective-permute-start | bytes 1990664 | tf_op jit(solution)/shard_map/ppermute | solution.py:54
  261.8 34.4 %collective-permute-start.48 = (bf16[2,2,4,24,896]{4,3,2,1,0:T(8,128)(2,1)S(1)}, bf16[2,2,4,24,896]{4,3,2,1,0:T(8,128)(2,1)S(1)}, u32[]{:S(2)}, u32[]{:S(2)}) collective-permute-start(bf16[2,2,4,24,896]{4,3,2,1,0:T(8,128)(2,1)S(1)} %dynamic-slice_bitcast_fusion.3), channel_id=1, source_target_pairs={{0,4},{4,0},{8,12},{12,8},{1,5},{5,1},{9,13},{13,9},{2,6},{6,2},{1... | collective-permute-start | bytes 2064392 | tf_op jit(solution)/shard_map/ppermute | solution.py:54
  263.8 32.8 %collective-permute-start.47 = (bf16[2,2,4,24,3072]{4,3,2,1,0:T(8,128)(2,1)}, bf16[2,2,4,24,3072]{4,3,2,1,0:T(8,128)(2,1)}, u32[]{:S(2)}, u32[]{:S(2)}) collective-permute-start(bf16[2,2,4,24,3072]{4,3,2,1,0:T(8,128)(2,1)} %dynamic-slice_bitcast_fusion), channel_id=1, source_target_pairs={{0,4},{4,0},{8,12},{12,8},{1,5},{5,1},{9,13},{13,9},{2,6},{6,2},{1... | collective-permute-start | bytes 7077896 | tf_op jit(solution)/shard_map/ppermute | solution.py:54
  264.2 32.2 %collective-permute-start.46 = (bf16[1,2,4,96,768]{4,3,2,1,0:T(8,128)(2,1)S(1)}, bf16[1,2,4,96,768]{4,3,2,1,0:T(8,128)(2,1)S(1)}, u32[]{:S(2)}, u32[]{:S(2)}) collective-permute-start(bf16[1,2,4,96,768]{4,3,2,1,0:T(8,128)(2,1)S(1)} %constant_dynamic-slice_fusion.5), channel_id=1, source_target_pairs={{0,16},{16,0},{1,17},{17,1},{2,18},{18,2},{3,19},{19,3},{4,20},{20... | collective-permute-start | bytes 3538952 | tf_op jit(solution)/shard_map/ppermute | solution.py:626
  301.6 35.8 %collective-permute-start.51 = (bf16[1,2,4,24,3968]{4,3,2,1,0:T(8,128)(2,1)}, bf16[1,2,4,24,3968]{4,3,2,1,0:T(8,128)(2,1)}, u32[]{:S(2)}, u32[]{:S(2)}) collective-permute-start(bf16[1,2,4,24,3968]{4,3,2,1,0:T(8,128)(2,1)} %constant_dynamic-slice_fusion.4), channel_id=1, source_target_pairs={{0,16},{16,0},{1,17},{17,1},{2,18},{18,2},{3,19},{19,3},{4,20},{20... | collective-permute-start | bytes 4571144 | tf_op jit(solution)/shard_map/ppermute | solution.py:626
  303.4 35.7 %collective-permute-start.49 = (bf16[2,512,768]{2,1,0:T(8,128)(2,1)S(1)}, bf16[2,512,768]{2,1,0:T(8,128)(2,1)S(1)}, u32[]{:S(2)}, u32[]{:S(2)}) collective-permute-start(bf16[2,512,768]{2,1,0:T(8,128)(2,1)S(1)} %get-tuple-element.217), channel_id=1, source_target_pairs={{0,4},{4,0},{8,12},{12,8},{1,5},{5,1},{9,13},{13,9},{2,6},{6,2},{1... | collective-permute-start | bytes 4718600 | tf_op jit(solution)/shard_map/ppermute | solution.py:54
  340.2 37.2 %collective-permute-start.53 = (bf16[512,768]{1,0:T(8,128)(2,1)S(1)}, bf16[512,768]{1,0:T(8,128)(2,1)S(1)}, u32[]{:S(2)}, u32[]{:S(2)}) collective-permute-start(bf16[512,768]{1,0:T(8,128)(2,1)S(1)} %slice_bitcast_fusion.3), channel_id=1, source_target_pairs={{0,8},{4,12},{8,0},{12,4},{1,9},{5,13},{9,1},{13,5},{2,10},{6,14},... | collective-permute-start | bytes 2359304 | tf_op jit(solution)/shard_map/ppermute | solution.py:54
  341.8 35.9 %collective-permute-start.52 = (bf16[2,512,768]{2,1,0:T(8,128)(2,1)}, bf16[2,512,768]{2,1,0:T(8,128)(2,1)S(1)}, u32[]{:S(2)}, u32[]{:S(2)}) collective-permute-start(bf16[2,512,768]{2,1,0:T(8,128)(2,1)} %get-tuple-element.230), channel_id=1, source_target_pairs={{0,4},{4,0},{8,12},{12,8},{1,5},{5,1},{9,13},{13,9},{2,6},{6,2},{1... | collective-permute-start | bytes 4718600 | tf_op jit(solution)/shard_map/ppermute | solution.py:54
  342.5 35.5 %collective-permute-start.55 = (bf16[96,768]{1,0:T(8,128)(2,1)}, bf16[96,768]{1,0:T(8,128)(2,1)S(1)}, u32[]{:S(2)}, u32[]{:S(2)}) collective-permute-start(bf16[96,768]{1,0:T(8,128)(2,1)} %get-tuple-element.299), channel_id=1, source_target_pairs={{0,2},{1,0},{3,1},{2,3},{4,6},{5,4},{7,5},{6,7},{8,10},{9,8},{11,9... | collective-permute-start | bytes 442376 | tf_op jit(solution)/shard_map/ppermute | solution.py:67
  342.5 35.5 %collective-permute-start.56 = (bf16[96,768]{1,0:T(8,128)(2,1)}, bf16[96,768]{1,0:T(8,128)(2,1)}, u32[]{:S(2)}, u32[]{:S(2)}) collective-permute-start(bf16[96,768]{1,0:T(8,128)(2,1)} %get-tuple-element.298), channel_id=1, source_target_pairs={{0,3},{1,2},{3,0},{2,1},{4,7},{5,6},{7,4},{6,5},{8,11},{9,10},{11,... | collective-permute-start | bytes 442376 | tf_op jit(solution)/shard_map/ppermute | solution.py:67
  367.2 50.9 %collective-permute-start.60 = (bf16[96,768]{1,0:T(8,128)(2,1)}, bf16[96,768]{1,0:T(8,128)(2,1)S(1)}, u32[]{:S(2)}, u32[]{:S(2)}) collective-permute-start(bf16[96,768]{1,0:T(8,128)(2,1)} %get-tuple-element.297), channel_id=1, source_target_pairs={{0,1},{1,3},{3,2},{2,0},{4,5},{5,7},{7,6},{6,4},{8,9},{9,11},{11,1... | collective-permute-start | bytes 442376 | tf_op jit(solution)/shard_map/ppermute | solution.py:67
  378.1 38.4 %collective-permute-start.58 = (bf16[512,768]{1,0:T(8,128)(2,1)S(1)}, bf16[512,768]{1,0:T(8,128)(2,1)S(1)}, u32[]{:S(2)}, u32[]{:S(2)}) collective-permute-start(bf16[512,768]{1,0:T(8,128)(2,1)S(1)} %slice_bitcast_fusion.2), channel_id=1, source_target_pairs={{0,8},{4,12},{8,0},{12,4},{1,9},{5,13},{9,1},{13,5},{2,10},{6,14},... | collective-permute-start | bytes 2359304 | tf_op jit(solution)/shard_map/ppermute | solution.py:54
  378.7 37.8 %collective-permute-start.59 = (bf16[512,768]{1,0:T(8,128)(2,1)S(1)}, bf16[512,768]{1,0:T(8,128)(2,1)S(1)}, u32[]{:S(2)}, u32[]{:S(2)}) collective-permute-start(bf16[512,768]{1,0:T(8,128)(2,1)S(1)} %fusion.20), channel_id=1, source_target_pairs={{0,2},{1,0},{3,1},{2,3},{4,6},{5,4},{7,5},{6,7},{8,10},{9,8},{11,9... | collective-permute-start | bytes 2359304 | tf_op jit(solution)/shard_map/ppermute | solution.py:67
  378.7 39.0 %collective-permute-start.57 = (bf16[2,512,768]{2,1,0:T(8,128)(2,1)}, bf16[2,512,768]{2,1,0:T(8,128)(2,1)S(1)}, u32[]{:S(2)}, u32[]{:S(2)}) collective-permute-start(bf16[2,512,768]{2,1,0:T(8,128)(2,1)} %get-tuple-element.243), channel_id=1, source_target_pairs={{0,4},{4,0},{8,12},{12,8},{1,5},{5,1},{9,13},{13,9},{2,6},{6,2},{1... | collective-permute-start | bytes 4718600 | tf_op jit(solution)/shard_map/ppermute | solution.py:54
  379.5 38.6 %collective-permute-start.61 = (bf16[24,3968]{1,0:T(8,128)(2,1)S(1)}, bf16[24,3968]{1,0:T(8,128)(2,1)S(1)}, u32[]{:S(2)}, u32[]{:S(2)}) collective-permute-start(bf16[24,3968]{1,0:T(8,128)(2,1)S(1)} %get-tuple-element.293), channel_id=1, source_target_pairs={{0,2},{1,0},{3,1},{2,3},{4,6},{5,4},{7,5},{6,7},{8,10},{9,8},{11,9... | collective-permute-start | bytes 571400 | tf_op jit(solution)/shard_map/ppermute | solution.py:67
  429.3 48.1 %collective-permute-start.62 = (bf16[2,512,768]{2,1,0:T(8,128)(2,1)}, bf16[2,512,768]{2,1,0:T(8,128)(2,1)S(1)}, u32[]{:S(2)}, u32[]{:S(2)}) collective-permute-start(bf16[2,512,768]{2,1,0:T(8,128)(2,1)} %get-tuple-element.248), channel_id=1, source_target_pairs={{0,4},{4,0},{8,12},{12,8},{1,5},{5,1},{9,13},{13,9},{2,6},{6,2},{1... | collective-permute-start | bytes 4718600 | tf_op jit(solution)/shard_map/ppermute | solution.py:54
  429.4 46.0 %collective-permute-start.64 = (bf16[512,768]{1,0:T(8,128)(2,1)S(1)}, bf16[512,768]{1,0:T(8,128)(2,1)S(1)}, u32[]{:S(2)}, u32[]{:S(2)}) collective-permute-start(bf16[512,768]{1,0:T(8,128)(2,1)S(1)} %slice_bitcast_fusion.1), channel_id=1, source_target_pairs={{0,8},{4,12},{8,0},{12,4},{1,9},{5,13},{9,1},{13,5},{2,10},{6,14},... | collective-permute-start | bytes 2359304 | tf_op jit(solution)/shard_map/ppermute | solution.py:54
  439.5 36.7 %collective-permute-start.65 = (bf16[512,768]{1,0:T(8,128)(2,1)S(1)}, bf16[512,768]{1,0:T(8,128)(2,1)S(1)}, u32[]{:S(2)}, u32[]{:S(2)}) collective-permute-start(bf16[512,768]{1,0:T(8,128)(2,1)S(1)} %copy-done.37), channel_id=1, source_target_pairs={{0,2},{1,0},{3,1},{2,3},{4,6},{5,4},{7,5},{6,7},{8,10},{9,8},{11,9... | collective-permute-start | bytes 2359304 | tf_op jit(solution)/shard_map/ppermute | solution.py:67
  (130 other events, 1987.6 us)

commit v3 on v2

--- a/solution.py
+++ b/solution.py
@@ -119,8 +119,9 @@
 def forward_kernel(plane, last, *refs):
     refs = list(refs)
     count_ref, list_ref, valid_ref = refs[:3]
-    x_refs, norm_ref, w_kv_ref = refs[3:7], refs[7], refs[8]
-    refs = refs[9:]
+    x_refs = [refs[3], refs[5].at[0], refs[4], refs[5].at[1]]
+    norm_ref, w_kv_ref = refs[6:8]
+    refs = refs[8:]
     if plane == 0:
         w_q_ref = refs.pop(0)
     else:
@@ -281,14 +282,16 @@
     refs = list(refs)
     count_ref, list_ref, valid_ref = refs[:3]
     q_ref, kv_ref, out_ref, lse_ref, grad_ref, norm_ref, w_kv_ref, w_q_ref = refs[3:11]
-    x_from, refs = refs[11:15], refs[15:]
+    x_from = [refs[11], refs[13].at[0], refs[12], refs[13].at[1]]
+    refs = refs[14:]
     if carried:
         dq_in, dw_in, sum_in = refs[:3]
         refs = refs[3:]
     if last:
-        keep_ref, send_ref, dw_ref, dwq_ref, sum_ref = refs[:5]
+        keep_ref, send_ref, dw_out = refs[:3]
+        dw_ref, dwq_ref, sum_ref = refs[-3:]
         dq_ref = None
-        refs = refs[5:]
+        refs = refs[3:-3]
     else:
         keep_ref, send_ref, dw_ref, dq_ref, sum_ref = refs[:5]
         refs = refs[5:]
@@ -413,6 +416,14 @@
     lax.fori_loop(0, slots, finish, 0)
     if not last:
         leave.wait()
+        return
+    pieces = []
+    for head in range(3):
+        first = head * LANES
+        pieces.append(dwq_ref[first : first + 64, :])
+        pieces.append(dw_ref[first : first + LANES, :])
+    pieces += [sum_ref[...], jnp.zeros((LANES - 8, D), F32)]
+    dw_out[...] = jnp.concatenate(pieces, axis=0).T.astype(BF16)
 
 
 def attend_backward(
@@ -425,12 +436,18 @@
     carry = list(carry)
     half = jax.ShapeDtypeStruct((2, BLOCK, D), BF16)
     weight = jax.ShapeDtypeStruct((3 * LANES, D), F32)
-    fourth = weight if last else jax.ShapeDtypeStruct((q_rows, 3 * LANES), F32)
-    return pl.pallas_call(
+    sums = jax.ShapeDtypeStruct((8, D), F32)
+    if last:
+        outs = (jax.ShapeDtypeStruct((D, 9 * HDIM + LANES), BF16),)
+        spaces, kept = (vmem,), [weight, weight, sums]
+    else:
+        outs = (weight, jax.ShapeDtypeStruct((q_rows, 3 * LANES), F32), sums)
+        spaces, kept = (vmem, anywhere, vmem), []
+    result = pl.pallas_call(
         partial(backward_kernel, plane, bool(carry), last),
-        out_shape=(half, half, weight, fourth, jax.ShapeDtypeStruct((8, D), F32)),
-        in_specs=[smem] * 3 + [vmem] * 8 + [anywhere] * 4 + [anywhere, vmem, vmem][: len(carry)],
-        out_specs=(vmem, vmem, vmem, vmem if last else anywhere, vmem),
+        out_shape=(half, half) + outs,
+        in_specs=[smem] * 3 + [vmem] * 8 + [anywhere] * 3 + [anywhere, vmem, vmem][: len(carry)],
+        out_specs=(vmem, vmem) + spaces,
         scratch_shapes=[
             pltpu.VMEM((3, q_rows, LANES), BF16),
             pltpu.VMEM((3, q_rows, LANES), BF16),
@@ -441,7 +458,8 @@
             pltpu.VMEM((3, LANES, q_rows), F32),
             pltpu.VMEM((q_rows, D), BF16),
             pltpu.SemaphoreType.DMA((5,)),
-        ],
+        ]
+        + [pltpu.VMEM(k.shape, k.dtype) for k in kept],
         compiler_params=pltpu.CompilerParams(vmem_limit_bytes=44 << 20),
         cost_estimate=pl.CostEstimate(
             flops=25 * 1000 * 1000 * 1000, bytes_accessed=16 << 20, transcendentals=7 << 20
@@ -450,6 +468,7 @@
     )(
         counts, lists, valid, queries, key_vals, attended, lse, grads, norms, w_kv_t, w_q_t, *blocks, *carry
     )
+    return tuple(result) + (None,) * (5 - len(result))
 
 
 def erf_of(values):
@@ -476,7 +495,7 @@
     return clamped * top / low
 
 
-def middle_kernel(pieces, shard, *refs):
+def middle_kernel(pieces, pair, shard, *refs):
     refs = list(refs)
     start_ref, group_ref = refs[:2]
     merged_refs, refs = refs[2:6], refs[6:]
@@ -485,17 +504,19 @@
     output_ref, grad_y_ref, grad_z_ref, h_two_ref, hidden_ref, grad_up_ref = refs[:6]
     part_refs, sum_ref, refs = refs[6:10], refs[10], refs[11:]
     w_out, w_up, w_down, moved = refs
-    pair = piece_refs[0].shape[0] // 9
+    parts = []
+    for piece in piece_refs:
+        parts += [(piece, base) for base in range(0, piece.shape[0], 9 * pair)]
 
     def moves_of(weight):
         moves = []
-        for i, piece in enumerate(piece_refs):
+        for i, (piece, base) in enumerate(parts):
             if weight < 5:
-                source = piece.at[pl.ds(weight * pair, pair)]
+                source = piece.at[pl.ds(base + weight * pair, pair)]
                 rows = pl.ds(pl.multiple_of(start_ref[i] * shard, pair), pair)
                 target = w_out.at[rows] if weight == 0 else w_up.at[weight - 1, rows]
             else:
-                source = piece.at[pl.ds(5 * pair, 4 * pair)]
+                source = piece.at[pl.ds(base + 5 * pair, 4 * pair)]
                 rows = pl.ds(pl.multiple_of(start_ref[i] * 4 * shard, 4 * pair), 4 * pair)
                 target = w_down.at[rows]
             moves.append(pltpu.make_async_copy(source, target, moved.at[weight, i]))
@@ -557,12 +578,14 @@
     vmem = pl.BlockSpec(memory_space=pltpu.VMEM)
     anywhere = pl.BlockSpec(memory_space=pl.ANY)
     rows = tokens.shape[0]
+    number = starts.shape[0]
+    pair = sum(piece.shape[0] for piece in pieces) // (9 * number)
 
     def shape(columns, dtype, height=rows):
         return jax.ShapeDtypeStruct((height, columns), dtype)
 
     return pl.pallas_call(
-        partial(middle_kernel, len(pieces), shard),
+        partial(middle_kernel, len(pieces), pair, shard),
         out_shape=(
             shape(D, BF16),
             shape(D, F32),
@@ -579,7 +602,7 @@
             pltpu.VMEM((D, D), BF16),
             pltpu.VMEM((4, D, D), BF16),
             pltpu.VMEM((4 * D, D), BF16),
-            pltpu.SemaphoreType.DMA((6, len(pieces))),
+            pltpu.SemaphoreType.DMA((6, number)),
         ],
         compiler_params=pltpu.CompilerParams(vmem_limit_bytes=56 << 20),
         cost_estimate=pl.CostEstimate(
@@ -655,25 +678,30 @@
     full = jnp.zeros((count,) + blocks[0].shape, BF16)
     for r in range(count):
         full = lax.dynamic_update_index_in_dim(full, blocks[r], sources[r], 0)
-    halves = []
+    cuts = []
     for half in range(2):
         part = full[half * (count // 2) : (half + 1) * (count // 2)]
         cut = [part[:, i * shard : (i + 1) * shard] for i in range(5)] + [part[:, 5 * shard :]]
-        halves.append(jnp.concatenate([c.reshape(-1, D) for c in cut], axis=0))
-    return halves
-
-
-def join_halves(pieces, starts, offs, rows):
-    cuts = [i * rows for i in range(1, 6)]
-    joined, firsts = [], []
-    for base in range(0, len(pieces), len(offs)):
-        for i, (half, x, y) in enumerate(offs):
-            if half == 0:
-                other = base + offs.index((1, x, y))
-                both = zip(jnp.split(pieces[base + i], cuts), jnp.split(pieces[other], cuts))
-                joined.append(jnp.concatenate([part for pair in both for part in pair], axis=0))
-                firsts.append(starts[base + i])
-    return joined, firsts
+        cuts += [c.reshape(-1, D) for c in cut]
+    return jnp.concatenate(cuts, axis=0)
+
+
+def join_halves(pieces, places, number):
+    def woven(first, second):
+        rows = first.shape[0] // 9
+        cuts = [i * rows for i in range(1, 6)]
+        both = zip(jnp.split(first, cuts), jnp.split(second, cuts))
+        return jnp.concatenate([part for pair in both for part in pair], axis=0)
+
+    joined, kept = [], []
+    for base in range(0, len(pieces), number):
+        for i in (0, 1):
+            joined.append(woven(*jnp.split(pieces[base + i], 2)))
+            kept.append(((0,),) + places[base + i][1:])
+        for i in (2, 4):
+            joined.append(woven(pieces[base + i], pieces[base + i + 1]))
+            kept.append(((0,),) + places[base + i][1:])
+    return joined, kept
 
 
 def gather_ctx(value):
@@ -760,49 +788,50 @@
         [packed, jnp.broadcast_to(extra[None], (heads_ax,) + extra.shape)], axis=2
     )
     wide = 3 * group + LANES
-    packed = gather_seq(packed[None])
-    pieces = []
+    mine = jnp.zeros((heads_ax, shard, wide), BF16)
     for j in range(heads_ax):
-        piece = lax.dynamic_index_in_dim(packed, order[j], 1, keepdims=False)
-        pieces.append(swap_head(piece, j) if j else piece)
-    packed = jnp.zeros((heads_ax, seq_ax, shard, wide), BF16)
-    for j in range(heads_ax):
-        packed = lax.dynamic_update_index_in_dim(packed, pieces[j], order[j], 0)
-    packed = gather_ctx(packed)
-    packed = jnp.transpose(packed, (2, 1, 0, 3, 4)).reshape(D, wide)
+        piece = lax.dynamic_index_in_dim(packed, order[j], 0, keepdims=False)
+        piece = swap_head(piece, j) if j else piece
+        mine = lax.dynamic_update_index_in_dim(mine, piece, order[j], 0)
+    ring_mine = [mine] + [ring_send(mine, i) for i in range(1, ctx_ax)]
 
     w_rest = jnp.concatenate(
         [w_out] + [w_up[:, i * D : (i + 1) * D] for i in range(4)] + [w_down], axis=0
     )
     rest = [w_rest]
     near, ahead, behind = swap_head(tokens, 2), ring_send(tokens, 1), ring_send(w_rest, 1)
-    near, ahead, behind, packed = tie(near, ahead, behind, packed)
+    near, ahead, behind, *ring_mine = tie(near, ahead, behind, *ring_mine)
     rest.append(behind)
-
-    g_one, b_one, g_two, b_two = [packed[:, 3 * group + i].astype(F32) for i in range(4)]
-    norm_one = jnp.pad(jnp.stack([g_one, b_one]), ((0, 6), (0, 0)))
-    w_mine = packed[:, : 3 * group].reshape(D, 3, 3, HDIM)
-    w_kv = w_mine[:, :, 1:].reshape(D, 6 * HDIM)
-    w_q = jnp.pad(w_mine[:, :, :1], ((0, 0), (0, 0), (0, 1), (0, 0))).reshape(D, 6 * HDIM)
-    w_kv_t, w_q_t = w_kv.T, w_q.T
-    about_all = packed[::shard, 3 * group + 4 : 3 * group + 7].astype(jnp.int32)
-    about_all = lax.dynamic_index_in_dim(
-        about_all.reshape(seq_ax, heads_ax, ctx_ax, 3), lax.axis_index("seq"), 0, keepdims=False
-    )
-    pick_head = jnp.stack(order)[:, None] == jnp.arange(heads_ax)[None, :]
-    pick_ctx = sources[:, None] == jnp.arange(ctx_ax)[None, :]
-    pick = pick_ctx[:, None, None, :] & pick_head[None, :, :, None]
-    slot_about = jnp.sum(jnp.where(pick[..., None], about_all[None, None], 0), axis=(2, 3))
-    slot_ids = slot_about[:, :, 0]
-    slot_valid = (tok_rows - (slot_about[:, :, 1] * 16 + slot_about[:, :, 2])).reshape(-1)
-    counts, lists = scene_lists(slot_ids[0][None, :, None] == slot_ids[:, None, :])
+    packed = jnp.zeros((ctx_ax,) + mine.shape, BF16)
+    for r in range(ctx_ax):
+        packed = lax.dynamic_update_index_in_dim(packed, ring_mine[r], sources[r], 0)
+
+    def weights_here(packed):
+        packed = jnp.swapaxes(gather_seq(packed[None]), 1, 2).reshape(D, wide)
+        g_one, b_one, g_two, b_two = [packed[:, 3 * group + i].astype(F32) for i in range(4)]
+        norm_one = jnp.pad(jnp.stack([g_one, b_one]), ((0, 6), (0, 0)))
+        w_mine = packed[:, : 3 * group].reshape(D, 3, 3, HDIM)
+        w_kv = w_mine[:, :, 1:].reshape(D, 6 * HDIM)
+        w_q = jnp.pad(w_mine[:, :, :1], ((0, 0), (0, 0), (0, 1), (0, 0))).reshape(D, 6 * HDIM)
+        about_all = packed[::shard, 3 * group + 4 : 3 * group + 7].astype(jnp.int32)
+        about_all = lax.dynamic_index_in_dim(
+            about_all.reshape(seq_ax, heads_ax, ctx_ax, 3), lax.axis_index("seq"), 0, keepdims=False
+        )
+        pick_head = jnp.stack(order)[:, None] == jnp.arange(heads_ax)[None, :]
+        pick_ctx = sources[:, None] == jnp.arange(ctx_ax)[None, :]
+        pick = pick_ctx[:, None, None, :] & pick_head[None, :, :, None]
+        slot_about = jnp.sum(jnp.where(pick[..., None], about_all[None, None], 0), axis=(2, 3))
+        slot_ids = slot_about[:, :, 0]
+        slot_valid = (tok_rows - (slot_about[:, :, 1] * 16 + slot_about[:, :, 2])).reshape(-1)
+        counts, lists = scene_lists(slot_ids[0][None, :, None] == slot_ids[:, None, :])
+        return (g_one, b_one, g_two, b_two), norm_one, (w_kv, w_q), (counts, lists, slot_valid)
 
     planes, key_vals, queries, acc = [], [], None, None
     block = tokens
     ready = None
     for r in range(ctx_ax + 1):
         if r < ctx_ax:
-            travelers = [swap_head(block, 1), swap_head(near, 1)]
+            travelers = [swap_head(jnp.stack([block, near]), 1)]
         else:
             travelers = []
         if r + 1 < ctx_ax:
@@ -812,14 +841,13 @@
             travelers.append(ring_send(rest[-1], 1))
         count = len(travelers)
         if r == ctx_ax - 2:
-            halves = in_order(rest, sources, shard)
-            travelers += [swap_head(halves[0], 2), swap_seq(halves[0]), swap_seq(halves[1])]
+            line = in_order(rest, sources, shard)
+            middle_row = line.shape[0] // 2
+            travelers += [swap_head(line[:middle_row], 2), swap_seq(line)]
         if r == ctx_ax - 1:
-            travelers += [swap_head(halves[1], 2), swap_seq(x_first)]
-            travelers += [swap_head(v, 1) for v in halves]
+            travelers += [swap_head(line[middle_row:], 2), swap_seq(x_first), swap_head(line, 1)]
         if r == ctx_ax:
-            travelers += [swap_seq(x_second)]
-            travelers += [swap_head(v, 1) for v in (x_first, y_first, y_second, xy_first)]
+            travelers += [swap_seq(x_second), swap_head(y_line, 1), swap_head(x_first, 1)]
         results = []
         if ready is not None:
             results = list(
@@ -840,17 +868,21 @@
             )
         tied = list(tie(*travelers, *results))
         extra, tied = tied[count : len(travelers)], tied[:count] + tied[len(travelers) :]
+        if r == 0:
+            norms, norm_one, weights, scenes = weights_here(packed)
+            g_one, b_one, g_two, b_two = norms
+            w_kv, w_q = weights
+            w_kv_t, w_q_t = w_kv.T, w_q.T
+            counts, lists, slot_valid = scenes
         if r == ctx_ax - 2:
-            x_first, y_first, y_second = extra
+            x_first, y_line = extra
         if r == ctx_ax - 1:
-            x_second, xy_first = extra[:2]
-            cores = extra[2:]
+            x_second, xy_first, core_line = extra
         if r == ctx_ax:
-            xy_second = extra[0]
-            cores += extra[1:]
+            xy_second, core_y, core_x_first = extra
             results = tied
             break
-        planes.append([block, tied.pop(0), near, tied.pop(0)])
+        planes.append([block, near, tied.pop(0)])
         ready = planes[-1]
         if r + 1 < ctx_ax:
             block, near = ahead, tied.pop(0)
@@ -864,26 +896,28 @@
             acc = tied.pop(0)
     key_vals.append(results[0])
     attended, lse = results[1:]
-    cores += [swap_head(v, 1) for v in (x_second, xy_second)]
-    owns = [halves[0], halves[1], x_first, y_first, y_second, xy_first, x_second, xy_second]
-    offs = [(0, 0, 0), (1, 0, 0), (0, 1, 0), (0, 0, 1), (1, 0, 1), (0, 1, 1), (1, 1, 0), (1, 1, 1)]
+    owns = [line, y_line, x_first, x_second, xy_first, xy_second]
+    cores = [core_line, core_y, core_x_first]
+    cores += [swap_head(v, 1) for v in (x_second, xy_first, xy_second)]
+    offs = [((0, 1), 0, 0), ((0, 1), 0, 1), ((0,), 1, 0), ((1,), 1, 0), ((0,), 1, 1), ((1,), 1, 1)]
     me_x, me_core, me_seq = me_head // 2, me_head % 2, lax.axis_index("seq")
-    pieces, starts = [], []
+    pieces, places = [], []
     for core, arrays in enumerate((owns, cores)):
-        for array, (half, x, y) in zip(arrays, offs):
+        for array, (halves, x, y) in zip(arrays, offs):
             pieces.append(array)
-            starts.append((half, (me_x ^ x) * 2 + (me_core ^ core), y))
+            places.append((halves, (me_x ^ x) * 2 + (me_core ^ core), y))
     reach = 2
     while reach < seq_ax:
         pieces += [swap_seq(array, reach) for array in pieces]
-        starts += [(half, place, y ^ reach) for half, place, y in starts]
+        places += [(halves, place, y ^ reach) for halves, place, y in places]
         reach *= 2
+    if (ctx_ax // 2 * shard) % 8:
+        pieces, places = join_halves(pieces, places, len(offs))
     starts = [
         ((me_seq ^ y) * heads_ax + place) * ctx_ax + half * (ctx_ax // 2)
-        for half, place, y in starts
+        for halves, place, y in places
+        for half in halves
     ]
-    if (ctx_ax // 2 * shard) % 8:
-        pieces, starts = join_halves(pieces, starts, offs, ctx_ax // 2 * shard)
     starts = jnp.stack(starts).astype(jnp.int32)
 
     merged = []
@@ -915,32 +949,25 @@
     up_sum, out_sum = sum_over_core(grad_w_up), sum_over_core(grad_w_out)
     down_sum = sum_over_seq(down_sum)
 
-    carry, traveling, by_x, given = (), None, None, None
-    down_terms, wide_terms = [], []
+    carry, traveling, near_half, far_half = (), None, None, None
     for r in reversed(range(ctx_ax)):
         step = ctx_ax - 1 - r
         travelers = []
         if step >= 1:
-            low = keep.astype(F32) + swap_head(give, 1).astype(F32)
-            travelers.append(low.astype(BF16))
+            travelers.append(swap_head(far_half, 2))
         if step >= 2:
-            moved = by_x[0].astype(F32) + swap_head(by_x[1], 2).astype(F32)
-            if step >= 3:
-                moved = moved + ring_send(traveling, -1).astype(F32)
-            travelers.append(moved.astype(BF16))
+            travelers.append(ring_send(traveling, -1))
         count = len(travelers)
         if step == 0:
             travelers += [down_sum, up_sum, out_sum]
         if step == 1:
             wide_sum = sum_over_seq(jnp.concatenate([up_sum, out_sum], axis=-1))
-            down_sum = sum_over_x(down_sum)
-            travelers += [down_sum, wide_sum]
+            travelers += [sum_over_x(down_sum), wide_sum]
         if step == 2:
-            wide_sum = sum_over_x(wide_sum)
-            travelers += [wide_sum] + [send_term(down_sum, i) for i in (1, 2)]
+            travelers += [sum_over_x(wide_sum)] + [send_term(down_sum, i) for i in (1, 3)]
         if step == 3:
-            travelers += [send_term(down_sum, 3), send_term(wide_sum, 1)]
-        keep, give, dw_kv, fourth, sums = attend_backward(
+            travelers += [send_term(down_sum, 2)] + [send_term(wide_sum, i) for i in (1, 3)]
+        keep, give, dw, fourth, sums = attend_backward(
             r,
             counts,
             lists,
@@ -957,40 +984,53 @@
             carry,
             r == 0,
         )
-        keep, give, fourth, dw_kv, sums, *travelers = tie(
-            keep, give, fourth, dw_kv, sums, *travelers
-        )
-        carry = (fourth, dw_kv, sums)
+        if r == 0:
+            keep, give, dw, *travelers = tie(keep, give, dw, *travelers)
+        else:
+            keep, give, fourth, dw, sums, *travelers = tie(
+                keep, give, fourth, dw, sums, *travelers
+            )
+        extra = travelers[count:]
         if step >= 1:
-            by_x = travelers[0]
-        if step >= 2:
-            traveling = travelers[1]
-        travelers = travelers[count:]
+            moved = near_half.astype(F32) + travelers[0].astype(F32)
+            if step >= 2:
+                moved = moved + travelers[1].astype(F32)
+            traveling = moved.astype(BF16)
         if step == 0:
-            down_sum, up_sum, out_sum = travelers
+            down_sum, up_sum, out_sum = extra
         if step == 1:
-            down_sum, wide_sum = travelers
+            down_sum, wide_sum = extra
         if step == 2:
-            wide_sum, *down_terms = travelers
+            wide_sum, *down_terms = extra
         if step == 3:
-            down_terms.append(travelers[0])
-            wide_terms.append(travelers[1])
-    last_x = keep.astype(F32) + swap_head(give, 1).astype(F32)
-    moved = by_x[0].astype(F32) + swap_head(by_x[1], 2).astype(F32)
-    moved = (moved + ring_send(traveling, -1).astype(F32)).astype(BF16)
-    grad_h_one = last_x[0] + swap_head(last_x[1].astype(BF16), 2).astype(F32)
-    grad_h_one = grad_h_one + ring_send(moved, -1).astype(F32)
-    wide_terms += [send_term(wide_sum, i) for i in (2, 3)]
+            down_terms.append(extra[0])
+            wide_terms = extra[1:]
+        taken = swap_head(give, 1)
+        near_half = (keep[0].astype(F32) + taken[0].astype(F32)).astype(BF16)
+        far_half = (keep[1].astype(F32) + taken[1].astype(F32)).astype(BF16)
+        if r:
+            tied = [near_half, far_half, fourth, dw, sums, down_sum]
+            tied += [up_sum, out_sum] if step == 0 else [wide_sum]
+            tied += [traveling] if step >= 1 else []
+            near_half, far_half, fourth, dw, sums, down_sum, *tied = tie(*tied)
+            if step == 0:
+                up_sum, out_sum, *tied = tied
+            else:
+                wide_sum, *tied = tied
+            if step >= 1:
+                traveling = tied[0]
+        carry = (fourth, dw, sums)
+    near_half, far_half, traveling, dw, wide_sum = tie(
+        near_half, far_half, traveling, dw, wide_sum
+    )
+    dw_mine = sum_over_seq(dw.reshape(seq_ax, heads_ax, ctx_ax, shard, wide))
+    taken, carried, term, dw_mine = tie(
+        swap_head(far_half, 2), ring_send(traveling, -1), send_term(wide_sum, 2), dw_mine
+    )
+    grad_h_one = near_half.astype(F32) + taken.astype(F32) + carried.astype(F32)
+    wide_terms.append(term)
     down_sum, wide_sum = sum_terms(down_sum, down_terms), sum_terms(wide_sum, wide_terms)
     up_sum, out_sum = wide_sum[:, : 4 * D], wide_sum[:, 4 * D :]
-    dw_q = fourth
-
-    dw_kv = dw_kv.reshape(3, 2, HDIM, D)
-    dw_q = dw_q.reshape(3, 2, HDIM, D)
-    dw_mine = jnp.concatenate([dw_q[:, :1], dw_kv], axis=1).reshape(3 * group, D)
-    dw_mine = jnp.concatenate([dw_mine, jnp.pad(sums, ((0, LANES - 8), (0, 0)))], axis=0)
-    dw_mine = dw_mine.T.astype(BF16).reshape(seq_ax, heads_ax, ctx_ax, shard, wide)
-    dw_mine = sum_over_seq(dw_mine)
     dw_mine = sum_over_ctx(jnp.swapaxes(dw_mine, 0, 1)).astype(BF16)
     groups = []
     for j in range(heads_ax):

time: 512 us -> 486 us (0.949)
  waiting for transfers between devices: 134 us -> 115 us
  starting transfers between devices: 82.4 us -> 64.9 us
  local copies, waits for them, and re-layouts: 39.8 us -> 50.7 us
    ppermute x21, waiting for transfers between devices: 68.7 us -> 35.3 us  [ring_send(): return lax.ppermute(value, 'ctx', ring_pairs(lax.axis_size('ctx'), step))]
    ppermute x47 -> x41, waiting for transfers between devices: 30.1 us -> 57 us  [swap_head(): return lax.ppermute(value, 'head', [(i, i ^ mask) for i in range(count)])]
    ppermute x4 -> x3, waiting for transfers between devices: 18.5 us -> 0.24 us  [swap_seq(): lax.ppermute(value, 'seq', [(i, i ^ mask) for i in range(lax.axis_size('s...]
    ppermute x21, starting transfers between devices: 46.9 us -> 32 us  [ring_send(): return lax.ppermute(value, 'ctx', ring_pairs(lax.axis_size('ctx'), step))]
    unnamed x176 -> x157, local copies, waits for them, and re-layouts: 10.4 us -> 13.8 us
    ppermute x47 -> x41, starting transfers between devices: 25.2 us -> 24.9 us  [swap_head(): return lax.ppermute(value, 'head', [(i, i ^ mask) for i in range(count)])]
  transfers between devices with their start and end apart: 76 -> 69, of which waited for: 21 -> 26; matrix products, arithmetic and copies ran while one was open for 11% -> 13% of each run, Pallas kernels for 33% -> 34%
where the time goes in v3:
time: 486 us; the launch traced here: 477 us
  Pallas kernels  189 us (39%)
  waiting for transfers between devices  115 us (24%)
  starting transfers between devices  64.9 us (13%)
  local copies, waits for them, and re-layouts  50.7 us (10%)
  other arithmetic  37.3 us (8%)
  between operations  11 us (2%)
  matrix products  8.88 us (2%)
    pallas_call x4, Pallas kernels, attend_backward(): pl.pallas_call(partial(backward_kernel, plane, bool(carry), last), out_sh...  114 us
    ppermute x41, waiting for transfers between devices, swap_head(): return lax.ppermute(value, 'head', [(i, i ^ mask) for i in range(count)])  57 us
    pallas_call x4, Pallas kernels, attend_forward(): pl.pallas_call(partial(forward_kernel, plane, last), out_shape=tuple(outs...  50.1 us
    ppermute x21, waiting for transfers between devices, ring_send(): return lax.ppermute(value, 'ctx', ring_pairs(lax.axis_size('ctx'), step))  35.3 us
    ppermute x21, starting transfers between devices, ring_send(): return lax.ppermute(value, 'ctx', ring_pairs(lax.axis_size('ctx'), step))  32 us
    pallas_call x1, Pallas kernels, middle(): pl.pallas_call(partial(middle_kernel, len(pieces), pair, shard), out_shap...  25 us
    ppermute x41, starting transfers between devices, swap_head(): return lax.ppermute(value, 'head', [(i, i ^ mask) for i in range(count)])  24.9 us
    ppermute x3, waiting for transfers between devices, sum_over_seq(): lax.ppermute(give, 'seq', pairs)  18.4 us
  transfers between devices with their start and end apart: 69, of which 26 were waited for; matrix products, arithmetic and copies ran while one was open for 13% of the time, Pallas kernels for 34%

profile of v3, /device:TPU:0, one launch (start us, length us, event | category | flops | bytes accessed | tf_op | source)
XLA Modules:
  0.0 476.6 jit_solution(17144513582235950715)
XLA Ops:
  37.3 6.0 %collective-permute-done.7 = bf16[4,24,704]{2,1,0:T(8,128)(2,1)S(1)} collective-permute-done((bf16[4,24,704]{2,1,0:T(8,128)(2,1)S(1)}, bf16[4,24,704]{2,1,0:T(8,128)(2,1)S(1)}, u32[]{:S(2)}, u32[]{:S(2)}) %collective-permute-start.7) | collective-permute-done | bytes 135200 | tf_op jit(solution)/shard_map/ppermute | solution.py:67
  85.9 15.7 %attend_forward.4 = (bf16[2048,384]{1,0:T(8,128)(2,1)S(1)}, bf16[2048,384]{1,0:T(8,128)(2,1)S(1)}, f32[3,80,2048]{2,1,0:T(8,128)S(1)}) custom-call(s32[4,4]{1,0:T(4,128)S(1)} %get-tuple-element.320.refs_0_, s32[4,4,4]{2,1,0:T(4,128)S(1)} %select_reduce_fusion.1.refs_1_, s32[16]{0:T(128)S(1)} %sub.60.refs_2_, bf16[512,768]{1,0:T(8,128)(2,1)S(1)} %copy-done, ...), custom_call_target="tpu_custom_call" | custom-call | flops 12000000000 | bytes 10485760 | tf_op jit(solution)/shard_map/attend_forward/pallas_call | solution.py:267
  103.6 9.1 %collective-permute-done.16 = bf16[216,768]{1,0:T(8,128)(2,1)S(1)} collective-permute-done((bf16[216,768]{1,0:T(8,128)(2,1)}, bf16[216,768]{1,0:T(8,128)(2,1)S(1)}, u32[]{:S(2)}, u32[]{:S(2)}) %collective-permute-start.16) | collective-permute-done | bytes 331808 | tf_op jit(solution)/shard_map/ppermute | solution.py:67
  121.5 10.3 %attend_forward.5 = (bf16[2048,384]{1,0:T(8,128)(2,1)S(1)}, f32[3,80,2048]{2,1,0:T(8,128)S(1)}) custom-call(s32[4,4]{1,0:T(4,128)S(1)} %get-tuple-element.320.refs_0_, s32[4,4,4]{2,1,0:T(4,128)S(1)} %select_reduce_fusion.1.refs_1_, s32[16]{0:T(128)S(1)} %sub.60.refs_2_, bf16[512,768]{1,0:T(8,128)(2,1)S(1)} %collective-permute-done.1.refs_3_.refs_11_, ...), custom_call_target="tpu_custom_call" | custom-call | flops 12000000000 | bytes 10485760 | tf_op jit(solution)/shard_map/attend_forward/pallas_call | solution.py:267
  131.9 5.4 %collective-permute-done.20.refs_11_ = bf16[432,768]{1,0:T(8,128)(2,1)S(1)} collective-permute-done((bf16[432,768]{1,0:T(8,128)(2,1)S(1)}, bf16[432,768]{1,0:T(8,128)(2,1)S(1)}, u32[]{:S(2)}, u32[]{:S(2)}) %collective-permute-start.20) | collective-permute-done | bytes 663584 | tf_op jit(solution)/shard_map/ppermute | solution.py:54
  137.2 16.1 %collective-permute-done.19.refs_4_.refs_12_ = bf16[512,768]{1,0:T(8,128)(2,1)S(1)} collective-permute-done((bf16[512,768]{1,0:T(8,128)(2,1)S(1)}, bf16[512,768]{1,0:T(8,128)(2,1)S(1)}, u32[]{:S(2)}, u32[]{:S(2)}) %collective-permute-start.19) | collective-permute-done | bytes 786464 | tf_op jit(solution)/shard_map/ppermute | solution.py:54
  155.2 10.5 %attend_forward.6 = (bf16[2048,384]{1,0:T(8,128)(2,1)S(1)}, f32[3,80,2048]{2,1,0:T(8,128)S(1)}) custom-call(s32[4,4]{1,0:T(4,128)S(1)} %get-tuple-element.320.refs_0_, s32[4,4,4]{2,1,0:T(4,128)S(1)} %select_reduce_fusion.1.refs_1_, s32[16]{0:T(128)S(1)} %sub.60.refs_2_, bf16[512,768]{1,0:T(8,128)(2,1)} %collective-permute-done.11.refs_3_.refs_11_, ...), custom_call_target="tpu_custom_call" | custom-call | flops 12000000000 | bytes 10485760 | tf_op jit(solution)/shard_map/attend_forward/pallas_call | solution.py:267
  165.7 5.4 %collective-permute-done.23.refs_12_ = bf16[432,768]{1,0:T(8,128)(2,1)} collective-permute-done((bf16[432,768]{1,0:T(8,128)(2,1)S(1)}, bf16[432,768]{1,0:T(8,128)(2,1)}, u32[]{:S(2)}, u32[]{:S(2)}) %collective-permute-start.23) | collective-permute-done | bytes 663584 | tf_op jit(solution)/shard_map/ppermute | solution.py:54
  172.7 13.6 %attend_forward.7 = (bf16[2048,384]{1,0:T(8,128)(2,1)S(1)}, bf16[3,64,2048]{2,1,0:T(8,128)(2,1)S(1)}, f32[3,1,2048]{2,1,0:T(1,128)S(1)}) custom-call(s32[4,4]{1,0:T(4,128)S(1)} %get-tuple-element.320.refs_0_, s32[4,4,4]{2,1,0:T(4,128)S(1)} %select_reduce_fusion.1.refs_1_, s32[16]{0:T(128)S(1)} %sub.60.refs_2_, ...), custom_call_target="tpu_custom_call" | custom-call | flops 12000000000 | bytes 10485760 | tf_op jit(solution)/shard_map/attend_forward/pallas_call | solution.py:267
  194.3 4.2 collective-permute-done.30.refs_4_
  201.7 25.0 %middle.1 = (bf16[512,768]{1,0:T(8,128)(2,1)}, f32[512,768]{1,0:T(8,128)}, bf16[512,768]{1,0:T(8,128)(2,1)}, bf16[512,768]{1,0:T(8,128)(2,1)}, bf16[512,3072]{1,...) custom-call(s32[16]{0:T(128)} %stack.176.refs_0_, ...), custom_call_target="tpu_custom_call" | custom-call | flops 12000000000 | bytes 25165824 | tf_op jit(solution)/shard_map/middle/pallas_call | solution.py:587
  226.7 4.5 convolution_convert_fusion.1
  251.1 31.2 %attend_backward.4 = (bf16[2,512,768]{2,1,0:T(8,128)(2,1)S(1)}, bf16[2,512,768]{2,1,0:T(8,128)(2,1)}, f32[384,768]{1,0:T(8,128)S(1)}, f32[2048,384]{1,0:T(8,128)}, f32[8,768]{1,0:T(8,128)S(1)}) custom-call(s32[4,4]{1,0:T(4,128)S(1)} %get-tuple-element.320.refs_0_, s32[4,4,4]{2,1,0:T(4,128)S(1)} %select_reduce_fusion.1.refs_1_, s32[16]{0:T(128)S(1)} %sub.60.refs_2_, ...), custom_call_target="tpu_custom_call" | custom-call | flops 24999999488 | bytes 16777216 | tf_op jit(solution)/shard_map/attend_backward/pallas_call | solution.py:446
  300.4 23.9 %attend_backward.5 = (bf16[2,512,768]{2,1,0:T(8,128)(2,1)S(1)}, bf16[2,512,768]{2,1,0:T(8,128)(2,1)S(1)}, f32[384,768]{1,0:T(8,128)S(1)}, f32[2048,384]{1,0:T(8,128)}, f32[8,768]{1,0:T(8,128)S(1)}) custom-call(s32[4,4]{1,0:T(4,128)S(1)} %get-tuple-element.320.refs_0_, s32[4,4,4]{2,1,0:T(4,128)S(1)} %select_reduce_fusion.1.refs_1_, s32[16]{0:T(128)S(1)} %sub.60.refs_2_, ...), custom_call_target="tpu_custom_call" | custom-call | flops 24999999488 | bytes 16777216 | tf_op jit(solution)/shard_map/attend_backward/pallas_call | solution.py:446
  325.5 7.1 %collective-permute-done.45 = bf16[1,2,4,24,3968]{4,3,2,1,0:T(8,128)(2,1)S(1)} collective-permute-done((bf16[1,2,4,24,3968]{4,3,2,1,0:T(8,128)(2,1)S(1)}, bf16[1,2,4,24,3968]{4,3,2,1,0:T(8,128)(2,1)S(1)}, u32[]{:S(2)}, u32[]{:S(2)}) %collective-permute-start.45) | collective-permute-done | bytes 1523744 | tf_op jit(solution)/shard_map/ppermute | solution.py:649
  341.2 23.7 %attend_backward.6 = (bf16[2,512,768]{2,1,0:T(8,128)(2,1)S(1)}, bf16[2,512,768]{2,1,0:T(8,128)(2,1)S(1)}, f32[384,768]{1,0:T(8,128)S(1)}, f32[2048,384]{1,0:T(8,128)}, f32[8,768]{1,0:T(8,128)S(1)}) custom-call(s32[4,4]{1,0:T(4,128)S(1)} %get-tuple-element.320.refs_0_, s32[4,4,4]{2,1,0:T(4,128)S(1)} %select_reduce_fusion.1.refs_1_, s32[16]{0:T(128)S(1)} %sub.60.refs_2_, ...), custom_call_target="tpu_custom_call" | custom-call | flops 24999999488 | bytes 16777216 | tf_op jit(solution)/shard_map/attend_backward/pallas_call | solution.py:446
  365.1 7.8 %collective-permute-done.47 = bf16[512,768]{1,0:T(8,128)(2,1)S(1)} collective-permute-done((bf16[512,768]{1,0:T(8,128)(2,1)S(1)}, bf16[512,768]{1,0:T(8,128)(2,1)S(1)}, u32[]{:S(2)}, u32[]{:S(2)}) %collective-permute-start.47) | collective-permute-done | bytes 786464 | tf_op jit(solution)/shard_map/ppermute | solution.py:54
  381.4 4.4 collective-permute-start.55
  385.8 35.3 %attend_backward.7 = (bf16[2,512,768]{2,1,0:T(8,128)(2,1)S(1)}, bf16[2,512,768]{2,1,0:T(8,128)(2,1)S(1)}, bf16[768,704]{1,0:T(8,128)(2,1)S(1)}) custom-call(s32[4,4]{1,0:T(4,128)S(1)} %get-tuple-element.320.refs_0_, s32[4,4,4]{2,1,0:T(4,128)S(1)} %select_reduce_fusion.1.refs_1_, s32[16]{0:T(128)S(1)} %sub.60.refs_2_, bf16[2048,384]{1,0:T(8,128)(2,1)} %copy-done.23, ...), custom_call_target="tpu_custom_call" | custom-call | flops 24999999488 | bytes 16777216 | tf_op jit(solution)/shard_map/attend_backward/pallas_call | solution.py:446
  429.3 11.3 %collective-permute-done.62 = bf16[1,4,4,24,704]{4,3,1,2,0:T(8,128)(2,1)S(1)} collective-permute-done((bf16[1,4,4,24,704]{4,3,1,2,0:T(8,128)(2,1)S(1)}, bf16[1,4,4,24,704]{4,3,1,2,0:T(8,128)(2,1)S(1)}, u32[]{:S(2)}, u32[]{:S(2)}) %collective-permute-start.62) | collective-permute-done | bytes 540704 | tf_op jit(solution)/shard_map/ppermute | solution.py:649
  440.8 8.9 %collective-permute-done.61 = bf16[24,3968]{1,0:T(8,128)(2,1)S(1)} collective-permute-done((bf16[24,3968]{1,0:T(8,128)(2,1)S(1)}, bf16[24,3968]{1,0:T(8,128)(2,1)S(1)}, u32[]{:S(2)}, u32[]{:S(2)}) %collective-permute-start.61) | collective-permute-done | bytes 190496 | tf_op jit(solution)/shard_map/ppermute | solution.py:67
  450.1 5.3 %collective-permute-start.63 = (bf16[4,24,704]{2,1,0:T(8,128)(2,1)S(1)}, bf16[4,24,704]{2,1,0:T(8,128)(2,1)S(1)}, u32[]{:S(2)}, u32[]{:S(2)}) collective-permute-start(bf16[4,24,704]{2,1,0:T(8,128)(2,1)S(1)} %get-tuple-element.354), channel_id=1, source_target_pairs={{0,2},{1,0},{3,1},{2,3},{4,6},{5,4},{7,5},{6,7},{8,10},{9,8},{11,9... | collective-permute-start | bytes 405512 | tf_op jit(solution)/shard_map/ppermute | solution.py:67
  459.7 4.6 collective-permute-done.64
  464.3 4.7 collective-permute-done.65
  (412 shorter events, 171.5 us)
Async XLA Ops:
  0.6 44.1 %collective-permute-start = (bf16[512,768]{1,0:T(8,128)(2,1)}, bf16[512,768]{1,0:T(8,128)(2,1)S(1)}, u32[]{:S(2)}, u32[]{:S(2)}) collective-permute-start(bf16[512,768]{1,0:T(8,128)(2,1)} %refs_11_.1), channel_id=1, source_target_pairs={{0,8},{4,12},{8,0},{12,4},{1,9},{5,13},{9,1},{13,5},{2,10},{6,14},... | collective-permute-start | bytes 2359304 | tf_op jit(solution)/shard_map/ppermute | solution.py:54
  3.6 41.1 %collective-permute-start.1 = (bf16[512,768]{1,0:T(8,128)(2,1)}, bf16[512,768]{1,0:T(8,128)(2,1)S(1)}, u32[]{:S(2)}, u32[]{:S(2)}) collective-permute-start(bf16[512,768]{1,0:T(8,128)(2,1)} %refs_11_.1), channel_id=1, source_target_pairs={{0,1},{1,3},{3,2},{2,0},{4,5},{5,7},{7,6},{6,4},{8,9},{9,11},{11,1... | collective-permute-start | bytes 2359304 | tf_op jit(solution)/shard_map/ppermute | solution.py:67
  16.6 28.1 %collective-permute-start.2 = (bf16[216,768]{1,0:T(8,128)(2,1)S(1)}, bf16[216,768]{1,0:T(8,128)(2,1)}, u32[]{:S(2)}, u32[]{:S(2)}) collective-permute-start(bf16[216,768]{1,0:T(8,128)(2,1)S(1)} %constant_dynamic-update-slice_fusion), channel_id=1, source_target_pairs={{0,1},{1,3},{3,2},{2,0},{4,5},{5,7},{7,6},{6,4},{8,9},{9,11},{11,1... | collective-permute-start | bytes 995336 | tf_op jit(solution)/shard_map/ppermute | solution.py:67
  48.8 30.2 %collective-permute-start.10 = (bf16[512,768]{1,0:T(8,128)(2,1)S(1)}, bf16[512,768]{1,0:T(8,128)(2,1)}, u32[]{:S(2)}, u32[]{:S(2)}) collective-permute-start(bf16[512,768]{1,0:T(8,128)(2,1)S(1)} %collective-permute-done.1.refs_3_.refs_11_), channel_id=1, source_target_pairs={{0,8},{4,12},{8,0},{12,4},{1,9},{5,13},{9,1},{13,5},{2,10},{6,14},... | collective-permute-start | bytes 2359304 | tf_op jit(solution)/shard_map/ppermute | solution.py:54
  50.2 28.7 %collective-permute-start.11 = (bf16[512,768]{1,0:T(8,128)(2,1)S(1)}, bf16[512,768]{1,0:T(8,128)(2,1)}, u32[]{:S(2)}, u32[]{:S(2)}) collective-permute-start(bf16[512,768]{1,0:T(8,128)(2,1)S(1)} %collective-permute-done.1.refs_3_.refs_11_), channel_id=1, source_target_pairs={{0,1},{1,3},{3,2},{2,0},{4,5},{5,7},{7,6},{6,4},{8,9},{9,11},{11,1... | collective-permute-start | bytes 2359304 | tf_op jit(solution)/shard_map/ppermute | solution.py:67
  80.4 32.3 %collective-permute-start.13 = (bf16[2,512,768]{2,1,0:T(8,128)(2,1)S(1)}, bf16[2,512,768]{2,1,0:T(8,128)(2,1)S(1)}, u32[]{:S(2)}, u32[]{:S(2)}) collective-permute-start(bf16[2,512,768]{2,1,0:T(8,128)(2,1)S(1)} %pad_maximum_fusion.1), channel_id=1, source_target_pairs={{0,4},{4,0},{8,12},{12,8},{1,5},{5,1},{9,13},{13,9},{2,6},{6,2},{1... | collective-permute-start | bytes 4718600 | tf_op jit(solution)/shard_map/ppermute | solution.py:54
  80.9 31.8 %collective-permute-start.14 = (bf16[512,768]{1,0:T(8,128)(2,1)}, bf16[512,768]{1,0:T(8,128)(2,1)S(1)}, u32[]{:S(2)}, u32[]{:S(2)}) collective-permute-start(bf16[512,768]{1,0:T(8,128)(2,1)} %collective-permute-done.11.refs_3_.refs_11_), channel_id=1, source_target_pairs={{0,8},{4,12},{8,0},{12,4},{1,9},{5,13},{9,1},{13,5},{2,10},{6,14},... | collective-permute-start | bytes 2359304 | tf_op jit(solution)/shard_map/ppermute | solution.py:54
  82.3 30.4 %collective-permute-start.15 = (bf16[512,768]{1,0:T(8,128)(2,1)}, bf16[512,768]{1,0:T(8,128)(2,1)S(1)}, u32[]{:S(2)}, u32[]{:S(2)}) collective-permute-start(bf16[512,768]{1,0:T(8,128)(2,1)} %collective-permute-done.11.refs_3_.refs_11_), channel_id=1, source_target_pairs={{0,1},{1,3},{3,2},{2,0},{4,5},{5,7},{7,6},{6,4},{8,9},{9,11},{11,1... | collective-permute-start | bytes 2359304 | tf_op jit(solution)/shard_map/ppermute | solution.py:67
  117.5 35.8 %collective-permute-start.18 = (bf16[2,512,768]{2,1,0:T(8,128)(2,1)S(1)}, bf16[2,512,768]{2,1,0:T(8,128)(2,1)S(1)}, u32[]{:S(2)}, u32[]{:S(2)}) collective-permute-start(bf16[2,512,768]{2,1,0:T(8,128)(2,1)S(1)} %pad_maximum_fusion.2), channel_id=1, source_target_pairs={{0,4},{4,0},{8,12},{12,8},{1,5},{5,1},{9,13},{13,9},{2,6},{6,2},{1... | collective-permute-start | bytes 4718600 | tf_op jit(solution)/shard_map/ppermute | solution.py:54
  117.9 35.5 %collective-permute-start.21 = (bf16[864,768]{1,0:T(8,128)(2,1)S(1)}, bf16[864,768]{1,0:T(8,128)(2,1)}, u32[]{:S(2)}, u32[]{:S(2)}) collective-permute-start(bf16[864,768]{1,0:T(8,128)(2,1)S(1)} %get-tuple-element.360.refs_9_), channel_id=1, source_target_pairs={{0,16},{16,0},{1,17},{17,1},{2,18},{18,2},{3,19},{19,3},{4,20},{20... | collective-permute-start | bytes 3981320 | tf_op jit(solution)/shard_map/ppermute | solution.py:673
  120.0 33.3 %collective-permute-start.19 = (bf16[512,768]{1,0:T(8,128)(2,1)S(1)}, bf16[512,768]{1,0:T(8,128)(2,1)S(1)}, u32[]{:S(2)}, u32[]{:S(2)}) collective-permute-start(bf16[512,768]{1,0:T(8,128)(2,1)S(1)} %collective-permute-done.15.refs_3_.refs_11_), channel_id=1, source_target_pairs={{0,8},{4,12},{8,0},{12,4},{1,9},{5,13},{9,1},{13,5},{2,10},{6,14},... | collective-permute-start | bytes 2359304 | tf_op jit(solution)/shard_map/ppermute | solution.py:54
  155.2 34.2 %collective-permute-start.27 = (bf16[864,768]{1,0:T(8,128)(2,1)}, bf16[864,768]{1,0:T(8,128)(2,1)}, u32[]{:S(2)}, u32[]{:S(2)}) collective-permute-start(bf16[864,768]{1,0:T(8,128)(2,1)} %collective-permute-done.21.refs_10_), channel_id=1, source_target_pairs={{0,4},{4,0},{8,12},{12,8},{1,5},{5,1},{9,13},{13,9},{2,6},{6,2},{1... | collective-permute-start | bytes 3981320 | tf_op jit(solution)/shard_map/ppermute | solution.py:54
  247.3 35.0 %collective-permute-start.41 = (bf16[2,2,4,24,896]{4,3,2,1,0:T(8,128)(2,1)}, bf16[2,2,4,24,896]{4,3,2,1,0:T(8,128)(2,1)S(1)}, u32[]{:S(2)}, u32[]{:S(2)}) collective-permute-start(bf16[2,2,4,24,896]{4,3,2,1,0:T(8,128)(2,1)} %dynamic-slice_bitcast_fusion.3), channel_id=1, source_target_pairs={{0,4},{4,0},{8,12},{12,8},{1,5},{5,1},{9,13},{13,9},{2,6},{6,2},{1... | collective-permute-start | bytes 2064392 | tf_op jit(solution)/shard_map/ppermute | solution.py:54
  249.2 37.1 %collective-permute-start.40 = (bf16[2,2,4,24,3072]{4,3,2,1,0:T(8,128)(2,1)}, bf16[2,2,4,24,3072]{4,3,2,1,0:T(8,128)(2,1)}, u32[]{:S(2)}, u32[]{:S(2)}) collective-permute-start(bf16[2,2,4,24,3072]{4,3,2,1,0:T(8,128)(2,1)} %dynamic-slice_bitcast_fusion), channel_id=1, source_target_pairs={{0,4},{4,0},{8,12},{12,8},{1,5},{5,1},{9,13},{13,9},{2,6},{6,2},{1... | collective-permute-start | bytes 7077896 | tf_op jit(solution)/shard_map/ppermute | solution.py:54
  249.6 34.1 %collective-permute-start.39 = (bf16[1,2,4,96,768]{4,3,2,1,0:T(8,128)(2,1)S(1)}, bf16[1,2,4,96,768]{4,3,2,1,0:T(8,128)(2,1)}, u32[]{:S(2)}, u32[]{:S(2)}) collective-permute-start(bf16[1,2,4,96,768]{4,3,2,1,0:T(8,128)(2,1)S(1)} %constant_dynamic-slice_fusion.8), channel_id=1, source_target_pairs={{0,16},{16,0},{1,17},{17,1},{2,18},{18,2},{3,19},{19,3},{4,20},{20... | collective-permute-start | bytes 3538952 | tf_op jit(solution)/shard_map/ppermute | solution.py:649
  297.1 35.4 %collective-permute-start.45 = (bf16[1,2,4,24,3968]{4,3,2,1,0:T(8,128)(2,1)S(1)}, bf16[1,2,4,24,3968]{4,3,2,1,0:T(8,128)(2,1)S(1)}, u32[]{:S(2)}, u32[]{:S(2)}) collective-permute-start(bf16[1,2,4,24,3968]{4,3,2,1,0:T(8,128)(2,1)S(1)} %constant_dynamic-slice_fusion.7), channel_id=1, source_target_pairs={{0,16},{16,0},{1,17},{17,1},{2,18},{18,2},{3,19},{19,3},{4,20},{20... | collective-permute-start | bytes 4571144 | tf_op jit(solution)/shard_map/ppermute | solution.py:649
  299.8 33.1 %collective-permute-start.43 = (bf16[512,768]{1,0:T(8,128)(2,1)S(1)}, bf16[512,768]{1,0:T(8,128)(2,1)S(1)}, u32[]{:S(2)}, u32[]{:S(2)}) collective-permute-start(bf16[512,768]{1,0:T(8,128)(2,1)S(1)} %get-tuple-element.244), channel_id=1, source_target_pairs={{0,8},{4,12},{8,0},{12,4},{1,9},{5,13},{9,1},{13,5},{2,10},{6,14},... | collective-permute-start | bytes 2359304 | tf_op jit(solution)/shard_map/ppermute | solution.py:54
  338.4 34.5 %collective-permute-start.47 = (bf16[512,768]{1,0:T(8,128)(2,1)S(1)}, bf16[512,768]{1,0:T(8,128)(2,1)S(1)}, u32[]{:S(2)}, u32[]{:S(2)}) collective-permute-start(bf16[512,768]{1,0:T(8,128)(2,1)S(1)} %get-tuple-element.265), channel_id=1, source_target_pairs={{0,8},{4,12},{8,0},{12,4},{1,9},{5,13},{9,1},{13,5},{2,10},{6,14},... | collective-permute-start | bytes 2359304 | tf_op jit(solution)/shard_map/ppermute | solution.py:54
  339.0 33.9 %collective-permute-start.48 = (bf16[512,768]{1,0:T(8,128)(2,1)S(1)}, bf16[512,768]{1,0:T(8,128)(2,1)S(1)}, u32[]{:S(2)}, u32[]{:S(2)}) collective-permute-start(bf16[512,768]{1,0:T(8,128)(2,1)S(1)} %add_convert_fusion.8), channel_id=1, source_target_pairs={{0,2},{1,0},{3,1},{2,3},{4,6},{5,4},{7,5},{6,7},{8,10},{9,8},{11,9... | collective-permute-start | bytes 2359304 | tf_op jit(solution)/shard_map/ppermute | solution.py:67
  376.7 44.5 %collective-permute-start.53 = (bf16[512,768]{1,0:T(8,128)(2,1)S(1)}, bf16[512,768]{1,0:T(8,128)(2,1)S(1)}, u32[]{:S(2)}, u32[]{:S(2)}) collective-permute-start(bf16[512,768]{1,0:T(8,128)(2,1)S(1)} %get-tuple-element.284), channel_id=1, source_target_pairs={{0,8},{4,12},{8,0},{12,4},{1,9},{5,13},{9,1},{13,5},{2,10},{6,14},... | collective-permute-start | bytes 2359304 | tf_op jit(solution)/shard_map/ppermute | solution.py:54
  378.1 43.0 %collective-permute-start.54 = (bf16[512,768]{1,0:T(8,128)(2,1)S(1)}, bf16[512,768]{1,0:T(8,128)(2,1)S(1)}, u32[]{:S(2)}, u32[]{:S(2)}) collective-permute-start(bf16[512,768]{1,0:T(8,128)(2,1)S(1)} %add_convert_fusion.5), channel_id=1, source_target_pairs={{0,2},{1,0},{3,1},{2,3},{4,6},{5,4},{7,5},{6,7},{8,10},{9,8},{11,9... | collective-permute-start | bytes 2359304 | tf_op jit(solution)/shard_map/ppermute | solution.py:67
  378.2 42.9 %collective-permute-start.56 = (bf16[24,3968]{1,0:T(8,128)(2,1)S(1)}, bf16[24,3968]{1,0:T(8,128)(2,1)S(1)}, u32[]{:S(2)}, u32[]{:S(2)}) collective-permute-start(bf16[24,3968]{1,0:T(8,128)(2,1)S(1)} %get-tuple-element.353), channel_id=1, source_target_pairs={{0,2},{1,0},{3,1},{2,3},{4,6},{5,4},{7,5},{6,7},{8,10},{9,8},{11,9... | collective-permute-start | bytes 571400 | tf_op jit(solution)/shard_map/ppermute | solution.py:67
  378.3 42.9 %collective-permute-start.57 = (bf16[24,3968]{1,0:T(8,128)(2,1)S(1)}, bf16[24,3968]{1,0:T(8,128)(2,1)S(1)}, u32[]{:S(2)}, u32[]{:S(2)}) collective-permute-start(bf16[24,3968]{1,0:T(8,128)(2,1)S(1)} %get-tuple-element.352), channel_id=1, source_target_pairs={{0,1},{1,3},{3,2},{2,0},{4,5},{5,7},{7,6},{6,4},{8,9},{9,11},{11,1... | collective-permute-start | bytes 571400 | tf_op jit(solution)/shard_map/ppermute | solution.py:67
  381.4 39.7 %collective-permute-start.55 = (bf16[96,768]{1,0:T(8,128)(2,1)S(1)}, bf16[96,768]{1,0:T(8,128)(2,1)S(1)}, u32[]{:S(2)}, u32[]{:S(2)}) collective-permute-start(bf16[96,768]{1,0:T(8,128)(2,1)S(1)} %dynamic-slice_bitcast_fusion.11), channel_id=1, source_target_pairs={{0,3},{1,2},{3,0},{2,1},{4,7},{5,6},{7,4},{6,5},{8,11},{9,10},{11,... | collective-permute-start | bytes 442376 | tf_op jit(solution)/shard_map/ppermute | solution.py:67
  (113 other events, 1505.6 us)

commit v4 on v3

--- a/solution.py
+++ b/solution.py
@@ -120,11 +120,9 @@
     refs = list(refs)
     count_ref, list_ref, valid_ref = refs[:3]
     x_refs = [refs[3], refs[5].at[0], refs[4], refs[5].at[1]]
-    norm_ref, w_kv_ref = refs[6:8]
-    refs = refs[8:]
-    if plane == 0:
-        w_q_ref = refs.pop(0)
-    else:
+    w_ref = refs[6]
+    refs = refs[7:]
+    if plane:
         q_ref, acc_in = refs.pop(0), refs.pop(0)
     if last:
         before, refs = refs[:plane], refs[plane:]
@@ -137,14 +135,15 @@
     else:
         acc = refs.pop(0)
         keys, values_t, q_ext = refs
-    gain, bias = norm_ref[0:1, :], norm_ref[1:2, :]
+    marks = w_ref[:, 3 * LANES : 4 * LANES].astype(F32).T
+    gain, bias = marks[64:65], marks[65:66]
     for slot, x_ref in enumerate(x_refs):
         rows = slice(slot * BLOCK, (slot + 1) * BLOCK)
         normed, ignored, ignored_too = norm_rows(x_ref[...].astype(F32), gain, bias)
         normed = normed.astype(BF16)
-        kv_ref[rows, :] = dot_on(normed, w_kv_ref[...], 1, 0).astype(BF16)
+        kv_ref[rows, :] = dot_on(normed, w_ref[:, : 3 * LANES], 1, 0).astype(BF16)
         if plane == 0:
-            own = dot_on(normed, w_q_ref[...], 1, 0) * (HDIM ** (-0.5) * LOG2E)
+            own = dot_on(normed, w_ref[:, 3 * LANES :], 1, 0) * (HDIM ** (-0.5) * LOG2E)
             q_ref[rows, :] = own.astype(BF16)
     fill_keys(4, kv_ref, valid_ref, keys, values_t=values_t, marks_first=4 * plane)
     if plane == 0:
@@ -233,15 +232,15 @@
         lse_ref[head] = top[head] + jnp.log2(total)
 
 
-def attend_forward(plane, last, counts, lists, valid, blocks, norms, w_kv, w_q, queries, acc, before):
+def attend_forward(plane, last, counts, lists, valid, blocks, weights, queries, acc, before):
     kv_rows = 4 * BLOCK
     smem = pl.BlockSpec(memory_space=pltpu.SMEM)
     vmem = pl.BlockSpec(memory_space=pltpu.VMEM)
     anywhere = pl.BlockSpec(memory_space=pl.ANY)
     packed = jax.ShapeDtypeStruct((kv_rows, 3 * LANES), BF16)
     sums = jax.ShapeDtypeStruct((3, 80, kv_rows), F32)
-    inputs = [counts, lists, valid] + list(blocks) + [norms, w_kv]
-    inputs += [w_q] if plane == 0 else [queries, acc]
+    inputs = [counts, lists, valid] + list(blocks) + [weights]
+    inputs += [queries, acc] if plane else []
     outs = [packed] + ([packed] if plane == 0 else [])
     scratch = [
         pltpu.VMEM((3, kv_rows, LANES), BF16),
@@ -281,12 +280,13 @@
 def backward_kernel(plane, carried, last, *refs):
     refs = list(refs)
     count_ref, list_ref, valid_ref = refs[:3]
-    q_ref, kv_ref, out_ref, lse_ref, grad_ref, norm_ref, w_kv_ref, w_q_ref = refs[3:11]
-    x_from = [refs[11], refs[13].at[0], refs[12], refs[13].at[1]]
-    refs = refs[14:]
+    q_ref, kv_ref, out_ref, lse_ref, grad_ref, w_ref = refs[3:9]
+    x_from = [refs[9], refs[11].at[0], refs[10], refs[11].at[1]]
+    refs = refs[12:]
+    sum_in, refs = refs[0], refs[1:]
     if carried:
-        dq_in, dw_in, sum_in = refs[:3]
-        refs = refs[3:]
+        dq_in, dw_in = refs[:2]
+        refs = refs[2:]
     if last:
         keep_ref, send_ref, dw_out = refs[:3]
         dw_ref, dwq_ref, sum_ref = refs[-3:]
@@ -371,13 +371,13 @@
         leave.start()
     if carried:
         dw_ref[...] = dw_in[...]
-        sum_ref[...] = sum_in[...]
     else:
         dw_ref[...] = jnp.zeros_like(dw_ref)
-        sum_ref[...] = jnp.zeros_like(sum_ref)
+    sum_ref[...] = sum_in[...]
     if last:
         dwq_ref[...] = jnp.zeros_like(dwq_ref)
-    gain, bias = norm_ref[0:1, :], norm_ref[1:2, :]
+    marks = w_ref[:, 3 * LANES : 4 * LANES].astype(F32).T
+    gain, bias = marks[64:65], marks[65:66]
 
     def finish(slot, carry):
         rows = pl.ds(pl.multiple_of(slot * BLOCK, BLOCK), BLOCK)
@@ -386,7 +386,7 @@
             pieces.append(dkv_acc[head, 0:64, rows] * LN2)
             pieces.append(dkv_acc[head, 64:128, rows])
         turned = jnp.concatenate(pieces, axis=0)
-        part = dot_on(turned.T.astype(BF16), w_kv_ref[...], 1, 0)
+        part = dot_on(turned.T.astype(BF16), w_ref[:, : 3 * LANES], 1, 1)
         values_now = x_ref[rows, :].astype(F32)
         normed, unit, ignored = norm_rows(values_now, gain, bias)
         normed = normed.astype(BF16)
@@ -397,7 +397,7 @@
                 for h in range(3)
             ]
             scaled = jnp.concatenate(scaled, axis=1) * HDIM ** (-0.5)
-            part = part + dot_on(scaled.astype(BF16), w_q_ref[...], 1, 0)
+            part = part + dot_on(scaled.astype(BF16), w_ref[:, 3 * LANES :], 1, 1)
             dwq_ref[...] += dot_on(scaled.T.astype(BF16), normed, 1, 0)
         sum_ref[0:1, :] += jnp.sum(part * unit, axis=0, keepdims=True)
         sum_ref[1:2, :] += jnp.sum(part, axis=0, keepdims=True)
@@ -427,7 +427,7 @@
 
 
 def attend_backward(
-    plane, counts, lists, valid, queries, key_vals, attended, lse, grads, norms, w_kv_t, w_q_t, blocks, carry, last
+    plane, counts, lists, valid, queries, key_vals, attended, lse, grads, weights, blocks, carry, last
 ):
     q_rows = queries.shape[0]
     smem = pl.BlockSpec(memory_space=pltpu.SMEM)
@@ -444,9 +444,9 @@
         outs = (weight, jax.ShapeDtypeStruct((q_rows, 3 * LANES), F32), sums)
         spaces, kept = (vmem, anywhere, vmem), []
     result = pl.pallas_call(
-        partial(backward_kernel, plane, bool(carry), last),
+        partial(backward_kernel, plane, len(carry) > 1, last),
         out_shape=(half, half) + outs,
-        in_specs=[smem] * 3 + [vmem] * 8 + [anywhere] * 3 + [anywhere, vmem, vmem][: len(carry)],
+        in_specs=[smem] * 3 + [vmem] * 6 + [anywhere] * 3 + [vmem, anywhere, vmem][: len(carry)],
         out_specs=(vmem, vmem) + spaces,
         scratch_shapes=[
             pltpu.VMEM((3, q_rows, LANES), BF16),
@@ -460,13 +460,13 @@
             pltpu.SemaphoreType.DMA((5,)),
         ]
         + [pltpu.VMEM(k.shape, k.dtype) for k in kept],
-        compiler_params=pltpu.CompilerParams(vmem_limit_bytes=44 << 20),
+        compiler_params=pltpu.CompilerParams(vmem_limit_bytes=34 << 20),
         cost_estimate=pl.CostEstimate(
             flops=25 * 1000 * 1000 * 1000, bytes_accessed=16 << 20, transcendentals=7 << 20
         ),
         name="attend_backward",
     )(
-        counts, lists, valid, queries, key_vals, attended, lse, grads, norms, w_kv_t, w_q_t, *blocks, *carry
+        counts, lists, valid, queries, key_vals, attended, lse, grads, weights, *blocks, *carry
     )
     return tuple(result) + (None,) * (5 - len(result))
 
@@ -499,10 +499,10 @@
     refs = list(refs)
     start_ref, group_ref = refs[:2]
     merged_refs, refs = refs[2:6], refs[6:]
-    token_ref, cot_ref, norm_ref = refs[:3]
+    token_ref, cot_ref, mark_ref = refs[:3]
     piece_refs, refs = refs[3 : 3 + pieces], refs[3 + pieces :]
     output_ref, grad_y_ref, grad_z_ref, h_two_ref, hidden_ref, grad_up_ref = refs[:6]
-    part_refs, sum_ref, refs = refs[6:10], refs[10], refs[11:]
+    part_refs, sum_ref, norm_ref, refs = refs[6:10], refs[10], refs[11], refs[12:]
     w_out, w_up, w_down, moved = refs
     parts = []
     for piece in piece_refs:
@@ -526,6 +526,7 @@
     for weight in (0, 1, 5, 2, 3, 4):
         for move in arriving[weight]:
             move.start()
+    norm_ref[...] = mark_ref[...].astype(F32).T[64:72]
     for move in arriving[0]:
         move.wait()
     y_one = token_ref[...].astype(F32)
@@ -535,7 +536,7 @@
         turned = merged_ref[...].astype(F32).T.astype(BF16)
         y_one = y_one + dot_on(turned, w_out[rows, :], 1, 0)
     grad_y_ref[...] = y_one
-    gain, bias = norm_ref[0:1, :], norm_ref[1:2, :]
+    gain, bias = norm_ref[2:3, :], norm_ref[3:4, :]
     normed, unit, inv_rows = norm_rows(y_one, gain, bias)
     h_two_ref[...] = normed.astype(BF16)
 
@@ -562,8 +563,8 @@
     output_ref[...] = (y_one + output_sum).astype(BF16)
     normed, unit, inv_rows = norm_rows(y_one, gain, bias)
     sum_ref[...] = jnp.zeros_like(sum_ref)
-    sum_ref[0:1, :] = jnp.sum(grad_sum * unit, axis=0, keepdims=True)
-    sum_ref[1:2, :] = jnp.sum(grad_sum, axis=0, keepdims=True)
+    sum_ref[2:3, :] = jnp.sum(grad_sum * unit, axis=0, keepdims=True)
+    sum_ref[3:4, :] = jnp.sum(grad_sum, axis=0, keepdims=True)
     grad_y = cot_ref[...].astype(F32) + norm_back(grad_sum, unit, inv_rows, gain)
     grad_y_ref[...] = grad_y
     grad_z = grad_y.astype(BF16)
@@ -573,7 +574,7 @@
         part_ref[...] = dot_on(w_out[rows, :], grad_z, 1, 1).astype(BF16)
 
 
-def middle(starts, groups, merged, tokens, cotangent, norms, pieces, shard):
+def middle(starts, groups, merged, tokens, cotangent, marks, pieces, shard):
     smem = pl.BlockSpec(memory_space=pltpu.SMEM)
     vmem = pl.BlockSpec(memory_space=pltpu.VMEM)
     anywhere = pl.BlockSpec(memory_space=pl.ANY)
@@ -595,21 +596,107 @@
             shape(4 * D, BF16),
         )
         + (shape(rows, BF16, D // 4),) * 4
-        + (shape(D, F32, 8),),
+        + (shape(D, F32, 8),) * 2,
         in_specs=[smem, smem] + [vmem] * 7 + [anywhere] * len(pieces),
-        out_specs=(vmem,) * 11,
+        out_specs=(vmem,) * 12,
         scratch_shapes=[
             pltpu.VMEM((D, D), BF16),
             pltpu.VMEM((4, D, D), BF16),
             pltpu.VMEM((4 * D, D), BF16),
             pltpu.SemaphoreType.DMA((6, number)),
         ],
-        compiler_params=pltpu.CompilerParams(vmem_limit_bytes=56 << 20),
+        compiler_params=pltpu.CompilerParams(vmem_limit_bytes=58 << 20),
         cost_estimate=pl.CostEstimate(
             flops=12 * 1000 * 1000 * 1000, bytes_accessed=24 << 20, transcendentals=3 << 20
         ),
         name="middle",
-    )(starts, groups, *merged, tokens, cotangent, norms, *pieces)
+    )(starts, groups, *merged, tokens, cotangent, marks, *pieces)
+
+
+def put_halves(core, rows, keep_ref, give_ref, place, columns, values):
+    for i in range(values.shape[0] // (2 * rows)):
+        for which in range(2):
+            first = (2 * i + which) * rows
+            piece = values[first : first + rows].astype(BF16)
+            start = place + i * rows
+            if not isinstance(start, int):
+                start = pl.multiple_of(start, rows)
+            target = pl.ds(start, rows)
+
+            @pl.when(core == which)
+            def _(piece=piece, target=target):
+                keep_ref[target, columns] = piece
+
+            @pl.when(core != which)
+            def _(piece=piece, target=target):
+                give_ref[target, columns] = piece
+
+
+def down_kernel(line, core_ref, hidden_ref, cot_ref, keep_ref, give_ref):
+    block = dot_on(hidden_ref[...], cot_ref[...], 0, 0)
+    put_halves(core_ref[0], 4 * line, keep_ref, give_ref, 0, slice(0, D), block)
+
+
+def wide_kernel(line, *refs):
+    core_ref, group_ref, h_two_ref, grad_up_ref, grad_z_ref = refs[:5]
+    merged_refs, (keep_ref, give_ref) = refs[5:9], refs[9:]
+    core, step = core_ref[0], pl.program_id(0)
+    columns = slice(0, D)
+
+    @pl.when(step < 4)
+    def _():
+        block = dot_on(h_two_ref[...], grad_up_ref[...], 0, 0)
+        put_halves(core, line, keep_ref, give_ref, 0, columns, block)
+
+    @pl.when(step == 4)
+    def _():
+        group = D // 4
+        for j, merged_ref in enumerate(merged_refs):
+            block = dot_on(merged_ref[...], grad_z_ref[...], 1, 0)
+            place = group_ref[j] * (group // 2)
+            put_halves(core, line, keep_ref, give_ref, place, columns, block)
+
+
+def halves_of_down(line, core, hidden, cotangent):
+    rows = cotangent.shape[0]
+    half = pl.BlockSpec((D // 2, D), lambda j: (j, 0))
+    return pl.pallas_call(
+        partial(down_kernel, line),
+        grid=(4,),
+        out_shape=(jax.ShapeDtypeStruct((2 * D, D), BF16),) * 2,
+        in_specs=[
+            pl.BlockSpec(memory_space=pltpu.SMEM),
+            pl.BlockSpec((rows, D), lambda j: (0, j)),
+            pl.BlockSpec((rows, D), lambda j: (0, 0)),
+        ],
+        out_specs=(half, half),
+        compiler_params=pltpu.CompilerParams(vmem_limit_bytes=54 << 20),
+        cost_estimate=pl.CostEstimate(
+            flops=3 * 10**9, bytes_accessed=10 << 20, transcendentals=0
+        ),
+        name="grad_down",
+    )(core, hidden, cotangent)
+
+
+def halves_of_wide(line, core, groups, h_two, grad_up, grad_z, merged):
+    rows = h_two.shape[0]
+    smem = pl.BlockSpec(memory_space=pltpu.SMEM)
+    whole = pl.BlockSpec((rows, D), lambda j: (0, 0))
+    half = pl.BlockSpec((D // 2, D), lambda j: (0, j))
+    return pl.pallas_call(
+        partial(wide_kernel, line),
+        grid=(5,),
+        out_shape=(jax.ShapeDtypeStruct((D // 2, 5 * D), BF16),) * 2,
+        in_specs=[smem, smem, whole]
+        + [pl.BlockSpec((rows, D), lambda j: (0, jnp.minimum(j, 3))), whole]
+        + [pl.BlockSpec((D // 4, rows), lambda j: (0, 0))] * 4,
+        out_specs=(half, half),
+        compiler_params=pltpu.CompilerParams(vmem_limit_bytes=54 << 20),
+        cost_estimate=pl.CostEstimate(
+            flops=4 * 10**9, bytes_accessed=12 << 20, transcendentals=0
+        ),
+        name="grad_wide",
+    )(core, groups, h_two, grad_up, grad_z, *merged)
 
 
 def scene_lists(same):
@@ -624,9 +711,14 @@
 
 
 def halve(value, axis, bit, send):
+    give = lax.dynamic_index_in_dim(value, 1 - bit, axis, keepdims=False)
+    return value, send(give)
+
+
+def settle(pending, axis, bit):
+    value, taken = pending
     keep = lax.dynamic_index_in_dim(value, bit, axis, keepdims=False)
-    give = lax.dynamic_index_in_dim(value, 1 - bit, axis, keepdims=False)
-    return (keep.astype(F32) + send(give).astype(F32)).astype(BF16)
+    return (keep.astype(F32) + taken.astype(F32)).astype(BF16)
 
 
 def ring_sources(count):
@@ -635,19 +727,25 @@
     return jnp.array(table, jnp.int32)[lax.axis_index("ctx")]
 
 
-def sum_over_seq(value):
+def give_over_seq(value):
     count = lax.axis_size("seq")
     me = lax.axis_index("seq")
-    while count > 1:
+    while True:
         count //= 2
-        bit = (me // count) % 2
         pairs = [(i, i ^ count) for i in range(lax.axis_size("seq"))]
-        value = halve(
+        pending = halve(
             value.reshape((2, count) + value.shape[1:]),
             0,
-            bit,
+            (me // count) % 2,
             lambda give: lax.ppermute(give, "seq", pairs),
         )
+        if count == 1:
+            return pending
+        value = settle(pending, 0, (me // count) % 2)
+
+
+def sum_over_seq(pending):
+    value = settle(pending, 0, lax.axis_index("seq") % 2)
     return value.reshape(value.shape[1:])
 
 
@@ -714,17 +812,17 @@
     return whole
 
 
-def sum_over_core(value):
-    seqs, ctxs = lax.axis_size("seq"), lax.axis_size("ctx")
-    rows = value.shape[0] // (seqs * ctxs * 4)
-    value = value.reshape(seqs, 2, 2, ctxs, rows, value.shape[1])
-    bit = lax.axis_index("head") % 2
-    return halve(value, 2, bit, lambda give: swap_head(give, 1))
-
-
-def sum_over_x(value):
-    bit = lax.axis_index("head") // 2
-    return halve(value, 0, bit, lambda give: swap_head(give, 2))
+def sum_over_core(pending):
+    keep, taken = pending
+    return (keep.astype(F32) + taken.astype(F32)).astype(BF16)
+
+
+def give_over_x(value):
+    return halve(value, 0, lax.axis_index("head") // 2, lambda give: swap_head(give, 2))
+
+
+def sum_over_x(pending):
+    return settle(pending, 0, lax.axis_index("head") // 2)
 
 
 def send_term(value, r):
@@ -777,27 +875,39 @@
 
     order = [me_head ^ j for j in range(heads_ax)]
     sources = ring_sources(ctx_ax)
+    wide = 3 * group + LANES
 
     padding = tok_rows - jnp.sum(segment_ids >= 0)
     about = jnp.stack([segment_ids[0], padding // 16, padding % 16]).astype(BF16)
     extra = jnp.stack([gain_one, bias_one, gain_two, bias_two], axis=1)
     extra = jnp.concatenate([extra, jnp.broadcast_to(about[None, :], (shard, 3))], axis=1)
-    extra = jnp.pad(extra, ((0, 0), (0, LANES - 7)))
-    packed = jnp.swapaxes(w_qkv.reshape(shard, heads_ax, 3 * group), 0, 1)
+    extra = jnp.pad(extra, ((0, 0), (0, HDIM - 7)))
+    by_head = w_qkv.reshape(shard, heads_ax, 3, 3, HDIM)
+    beside = jnp.zeros((shard, heads_ax, 2, HDIM), BF16)
+    beside = jnp.concatenate(
+        [jnp.broadcast_to(extra[:, None, None], (shard, heads_ax, 1, HDIM)), beside], axis=2
+    )
     packed = jnp.concatenate(
-        [packed, jnp.broadcast_to(extra[None], (heads_ax,) + extra.shape)], axis=2
+        [
+            by_head[:, :, :, 1:].reshape(shard, heads_ax, 3 * LANES),
+            jnp.stack([by_head[:, :, :, 0], beside], axis=3).reshape(shard, heads_ax, 3 * LANES),
+        ],
+        axis=2,
     )
-    wide = 3 * group + LANES
-    mine = jnp.zeros((heads_ax, shard, wide), BF16)
-    for j in range(heads_ax):
-        piece = lax.dynamic_index_in_dim(packed, order[j], 0, keepdims=False)
-        piece = swap_head(piece, j) if j else piece
-        mine = lax.dynamic_update_index_in_dim(mine, piece, order[j], 0)
-    ring_mine = [mine] + [ring_send(mine, i) for i in range(1, ctx_ax)]
-
+    packed = jnp.swapaxes(packed, 0, 1)
+    got = tie(
+        *[lax.dynamic_index_in_dim(packed, o, 0, keepdims=False) for o in order]
+    )
+    got = [swap_head(piece, j) if j else piece for j, piece in enumerate(got)]
     w_rest = jnp.concatenate(
         [w_out] + [w_up[:, i * D : (i + 1) * D] for i in range(4)] + [w_down], axis=0
     )
+    w_rest, *got = tie(w_rest, *got)
+    mine = jnp.zeros((heads_ax, shard, D), BF16)
+    for j in range(heads_ax):
+        mine = lax.dynamic_update_index_in_dim(mine, got[j], order[j], 0)
+    ring_mine = [mine] + [ring_send(mine, i) for i in range(1, ctx_ax)]
+
     rest = [w_rest]
     near, ahead, behind = swap_head(tokens, 2), ring_send(tokens, 1), ring_send(w_rest, 1)
     near, ahead, behind, *ring_mine = tie(near, ahead, behind, *ring_mine)
@@ -807,15 +917,14 @@
         packed = lax.dynamic_update_index_in_dim(packed, ring_mine[r], sources[r], 0)
 
     def weights_here(packed):
-        packed = jnp.swapaxes(gather_seq(packed[None]), 1, 2).reshape(D, wide)
-        g_one, b_one, g_two, b_two = [packed[:, 3 * group + i].astype(F32) for i in range(4)]
-        norm_one = jnp.pad(jnp.stack([g_one, b_one]), ((0, 6), (0, 0)))
-        w_mine = packed[:, : 3 * group].reshape(D, 3, 3, HDIM)
-        w_kv = w_mine[:, :, 1:].reshape(D, 6 * HDIM)
-        w_q = jnp.pad(w_mine[:, :, :1], ((0, 0), (0, 0), (0, 1), (0, 0))).reshape(D, 6 * HDIM)
-        about_all = packed[::shard, 3 * group + 4 : 3 * group + 7].astype(jnp.int32)
+        weights = jnp.swapaxes(gather_seq(packed[None]), 1, 2).reshape(D, D)
+        first = 3 * LANES + HDIM + 4
+        about_all = weights[::shard, first : first + 3].astype(jnp.int32)
         about_all = lax.dynamic_index_in_dim(
-            about_all.reshape(seq_ax, heads_ax, ctx_ax, 3), lax.axis_index("seq"), 0, keepdims=False
+            about_all.reshape(seq_ax, heads_ax, ctx_ax, 3),
+            lax.axis_index("seq"),
+            0,
+            keepdims=False,
         )
         pick_head = jnp.stack(order)[:, None] == jnp.arange(heads_ax)[None, :]
         pick_ctx = sources[:, None] == jnp.arange(ctx_ax)[None, :]
@@ -824,7 +933,7 @@
         slot_ids = slot_about[:, :, 0]
         slot_valid = (tok_rows - (slot_about[:, :, 1] * 16 + slot_about[:, :, 2])).reshape(-1)
         counts, lists = scene_lists(slot_ids[0][None, :, None] == slot_ids[:, None, :])
-        return (g_one, b_one, g_two, b_two), norm_one, (w_kv, w_q), (counts, lists, slot_valid)
+        return weights, counts, lists, slot_valid
 
     planes, key_vals, queries, acc = [], [], None, None
     block = tokens
@@ -858,9 +967,7 @@
                     lists,
                     slot_valid,
                     ready,
-                    norm_one,
-                    w_kv,
-                    w_q,
+                    weights,
                     queries,
                     acc,
                     key_vals,
@@ -869,11 +976,7 @@
         tied = list(tie(*travelers, *results))
         extra, tied = tied[count : len(travelers)], tied[:count] + tied[len(travelers) :]
         if r == 0:
-            norms, norm_one, weights, scenes = weights_here(packed)
-            g_one, b_one, g_two, b_two = norms
-            w_kv, w_q = weights
-            w_kv_t, w_q_t = w_kv.T, w_q.T
-            counts, lists, slot_valid = scenes
+            weights, counts, lists, slot_valid = weights_here(packed)
         if r == ctx_ax - 2:
             x_first, y_line = extra
         if r == ctx_ax - 1:
@@ -925,31 +1028,30 @@
         part = attended[:, :, j * tok_rows : (j + 1) * tok_rows].reshape(group, tok_rows)
         merged.append(swap_head(part, j) if j else part)
 
-    norm_two = jnp.pad(jnp.stack([g_two, b_two]), ((0, 6), (0, 0)))
+    marks = weights[:, 3 * LANES : 4 * LANES]
     groups = jnp.stack(order).astype(jnp.int32)
     output, grad_y_one, grad_z, h_two, hidden, grad_up, *rest_out = middle(
-        starts, groups, merged, tokens, cotangent, norm_two, pieces, shard
+        starts, groups, merged, tokens, cotangent, marks, pieces, shard
     )
-    grad_merged, sums_two = rest_out[:4], rest_out[4]
+    grad_merged, sums_two, norms = rest_out[:4], rest_out[4], rest_out[5]
 
     grad_parts = [swap_head(p, j) if j else p for j, p in enumerate(grad_merged)]
-    grad_w_down = jnp.einsum("tf,td->fd", hidden, cotangent, preferred_element_type=F32)
-    down_sum = sum_over_core(grad_w_down.astype(BF16))
-    grad_w_up = jnp.einsum("td,tf->df", h_two, grad_up, preferred_element_type=F32)
-    grad_w_up = grad_w_up.astype(BF16)
-    grad_w_out = jnp.zeros((heads_ax, group, D), BF16)
-    for j in range(heads_ax):
-        part = jnp.einsum("at,td->ad", merged[j], grad_z, preferred_element_type=F32)
-        grad_w_out = lax.dynamic_update_index_in_dim(grad_w_out, part.astype(BF16), order[j], 0)
-    sums_two = jnp.pad(sums_two, ((0, LANES - 8), (0, 0))).T.astype(BF16)
-    grad_w_out = jnp.concatenate([grad_w_out.reshape(D, D), sums_two], axis=1)
-    tied = tie(down_sum, grad_w_up, grad_w_out, *grad_parts)
-    down_sum, grad_w_up, grad_w_out = tied[:3]
-    grad_local = jnp.concatenate(tied[3:], axis=1).reshape(3, HDIM, heads_ax * tok_rows)
-    up_sum, out_sum = sum_over_core(grad_w_up), sum_over_core(grad_w_out)
-    down_sum = sum_over_seq(down_sum)
-
-    carry, traveling, near_half, far_half = (), None, None, None
+    line = ctx_ax * shard
+    outer = (seq_ax, 2, ctx_ax)
+    me_bit = (me_head % 2)[None].astype(jnp.int32)
+    keep, give = halves_of_down(line, me_bit, hidden, cotangent)
+    shape = outer + (4 * shard, D)
+    down_sum = (keep.reshape(shape), swap_head(give.reshape(shape), 1))
+    h_two, keep, *_ = tie(h_two, down_sum[0])
+    keep, give = halves_of_wide(line, me_bit, groups, h_two, grad_up, grad_z, merged)
+    shape = outer + (shard, 5 * D)
+    keep, give, *tied = tie(keep, give, *down_sum, *grad_parts)
+    down_sum, grad_parts = sum_over_core(tied[:2]), tied[2:]
+    grad_local = jnp.concatenate(grad_parts, axis=1).reshape(3, HDIM, heads_ax * tok_rows)
+    wide_sum = (keep.reshape(shape), swap_head(give.reshape(shape), 1))
+    down_sum = give_over_seq(down_sum)
+
+    carry, traveling, near_half, far_half = (sums_two,), None, None, None
     for r in reversed(range(ctx_ax)):
         step = ctx_ax - 1 - r
         travelers = []
@@ -959,14 +1061,13 @@
             travelers.append(ring_send(traveling, -1))
         count = len(travelers)
         if step == 0:
-            travelers += [down_sum, up_sum, out_sum]
+            travelers += [down_sum, wide_sum]
         if step == 1:
-            wide_sum = sum_over_seq(jnp.concatenate([up_sum, out_sum], axis=-1))
-            travelers += [sum_over_x(down_sum), wide_sum]
+            travelers += [give_over_x(down_sum), give_over_seq(wide_sum)]
         if step == 2:
-            travelers += [sum_over_x(wide_sum)] + [send_term(down_sum, i) for i in (1, 3)]
+            travelers += [give_over_x(wide_sum)] + [send_term(down_sum, i) for i in (1, 2, 3)]
         if step == 3:
-            travelers += [send_term(down_sum, 2)] + [send_term(wide_sum, i) for i in (1, 3)]
+            travelers += [send_term(wide_sum, i) for i in (1, 2, 3)]
         keep, give, dw, fourth, sums = attend_backward(
             r,
             counts,
@@ -977,9 +1078,7 @@
             attended,
             lse,
             grad_local,
-            norm_one,
-            w_kv_t,
-            w_q_t,
+            weights,
             planes[r],
             carry,
             r == 0,
@@ -997,38 +1096,33 @@
                 moved = moved + travelers[1].astype(F32)
             traveling = moved.astype(BF16)
         if step == 0:
-            down_sum, up_sum, out_sum = extra
+            down_sum = sum_over_seq(extra[0])
+            wide_sum = sum_over_core(extra[1])
         if step == 1:
-            down_sum, wide_sum = extra
+            down_sum, wide_sum = sum_over_x(extra[0]), sum_over_seq(extra[1])
         if step == 2:
-            wide_sum, *down_terms = extra
+            wide_sum, down_terms = sum_over_x(extra[0]), list(extra[1:])
         if step == 3:
-            down_terms.append(extra[0])
-            wide_terms = extra[1:]
+            wide_terms = list(extra)
         taken = swap_head(give, 1)
         near_half = (keep[0].astype(F32) + taken[0].astype(F32)).astype(BF16)
         far_half = (keep[1].astype(F32) + taken[1].astype(F32)).astype(BF16)
         if r:
-            tied = [near_half, far_half, fourth, dw, sums, down_sum]
-            tied += [up_sum, out_sum] if step == 0 else [wide_sum]
+            tied = [near_half, far_half, fourth, dw, sums, down_sum, wide_sum]
             tied += [traveling] if step >= 1 else []
-            near_half, far_half, fourth, dw, sums, down_sum, *tied = tie(*tied)
-            if step == 0:
-                up_sum, out_sum, *tied = tied
-            else:
-                wide_sum, *tied = tied
+            near_half, far_half, fourth, dw, sums, down_sum, wide_sum, *tied = tie(*tied)
             if step >= 1:
                 traveling = tied[0]
-        carry = (fourth, dw, sums)
+        carry = (sums, fourth, dw)
     near_half, far_half, traveling, dw, wide_sum = tie(
         near_half, far_half, traveling, dw, wide_sum
     )
-    dw_mine = sum_over_seq(dw.reshape(seq_ax, heads_ax, ctx_ax, shard, wide))
-    taken, carried, term, dw_mine = tie(
-        swap_head(far_half, 2), ring_send(traveling, -1), send_term(wide_sum, 2), dw_mine
+    dw_mine = give_over_seq(dw.reshape(seq_ax, heads_ax, ctx_ax, shard, wide))
+    taken, carried, *dw_mine = tie(
+        swap_head(far_half, 2), ring_send(traveling, -1), *dw_mine
     )
+    dw_mine = sum_over_seq(dw_mine)
     grad_h_one = near_half.astype(F32) + taken.astype(F32) + carried.astype(F32)
-    wide_terms.append(term)
     down_sum, wide_sum = sum_terms(down_sum, down_terms), sum_terms(wide_sum, wide_terms)
     up_sum, out_sum = wide_sum[:, : 4 * D], wide_sum[:, 4 * D :]
     dw_mine = sum_over_ctx(jnp.swapaxes(dw_mine, 0, 1)).astype(BF16)
@@ -1041,21 +1135,22 @@
         [lax.dynamic_index_in_dim(groups, o, 0, keepdims=False) for o in order]
     ).astype(F32)
     grad_w_qkv = jnp.swapaxes(groups[:, :, : 3 * group], 0, 1).reshape(shard, 3 * D)
-    norm_sums = jnp.sum(groups[:, :, 3 * group : 3 * group + 2], axis=0)
-
-    ignored, unit_one, inv_one = norm_rows(tokens.astype(F32), g_one, b_one)
+    norm_sums = jnp.sum(groups[:, :, 3 * group : 3 * group + 4], axis=0)
+
+    g_one = norms[0]
+    ignored, unit_one, inv_one = norm_rows(tokens.astype(F32), g_one, norms[1])
     grad_tokens = (grad_y_one + norm_back(grad_h_one, unit_one, inv_one, g_one)).astype(BF16)
     return (
         output,
         grad_tokens,
         grad_w_qkv,
-        out_sum[:, :D],
+        out_sum,
         up_sum,
         down_sum,
         norm_sums[:, 0],
         norm_sums[:, 1],
-        out_sum[:, D],
-        out_sum[:, D + 1],
+        norm_sums[:, 2],
+        norm_sums[:, 3],
     )
 
 

time: 486 us -> 473 us (0.973)
  Pallas kernels: 189 us -> 203 us
  local copies, waits for them, and re-layouts: 50.7 us -> 37.6 us
  matrix products: 8.88 us -> 0 us
  starting transfers between devices: 64.9 us -> 59.4 us
    pallas_call x4 -> x6, Pallas kernels: 114 us -> 126 us  [the longest x4 110 us: attend_backward(): pl.pallas_call(partial(backward_kernel, plane, len(carry) > 1, last), out...]
    ppermute x21, waiting for transfers between devices: 35.3 us -> 44.9 us  [ring_send(): return lax.ppermute(value, 'ctx', ring_pairs(lax.axis_size('ctx'), step))]
    dot_general x6 -> x0, matrix products: 8.88 us -> none  [the longest x1 4.55 us: body(): jnp.einsum('tf,td->fd', hidden, cotangent, preferred_element_type=F32)]
    unnamed x157 -> x183, local copies, waits for them, and re-layouts: 13.8 us -> 20.6 us
    slice x7 -> x6, local copies, waits for them, and re-layouts: 8.66 us -> 2.58 us  [the longest x1 0.76 us: body(): g_one = norms[0]]
    ppermute x41 -> x40, waiting for transfers between devices: 57 us -> 51.9 us  [swap_head(): return lax.ppermute(value, 'head', [(i, i ^ mask) for i in range(count)])]
    convert_element_type x6 -> x5, other arithmetic: 10.2 us -> 7.38 us  [the longest x2 5.5 us: sum_over_core(): return (keep.astype(F32) + taken.astype(F32)).astype(BF16)]
    ppermute x41 -> x40, starting transfers between devices: 24.9 us -> 24.9 us  [swap_head(): return lax.ppermute(value, 'head', [(i, i ^ mask) for i in range(count)])]
  transfers between devices with their start and end apart: 69 -> 68, of which waited for: 26 -> 28; matrix products, arithmetic and copies ran while one was open for 13% -> 9% of each run, Pallas kernels for 34% -> 37%
where the time goes in v4:
time: 473 us; the launch traced here: 465 us
  Pallas kernels  203 us (43%)
  waiting for transfers between devices  118 us (25%)
  starting transfers between devices  59.4 us (13%)
  local copies, waits for them, and re-layouts  37.6 us (8%)
  other arithmetic  36.8 us (8%)
  between operations  10.8 us (2%)
    pallas_call x4, Pallas kernels, attend_backward(): pl.pallas_call(partial(backward_kernel, plane, len(carry) > 1, last), out...  110 us
    ppermute x40, waiting for transfers between devices, swap_head(): return lax.ppermute(value, 'head', [(i, i ^ mask) for i in range(count)])  51.9 us
    pallas_call x4, Pallas kernels, attend_forward(): pl.pallas_call(partial(forward_kernel, plane, last), out_shape=tuple(outs...  51.8 us
    ppermute x21, waiting for transfers between devices, ring_send(): return lax.ppermute(value, 'ctx', ring_pairs(lax.axis_size('ctx'), step))  44.9 us
    ppermute x21, starting transfers between devices, ring_send(): return lax.ppermute(value, 'ctx', ring_pairs(lax.axis_size('ctx'), step))  27.6 us
    ppermute x40, starting transfers between devices, swap_head(): return lax.ppermute(value, 'head', [(i, i ^ mask) for i in range(count)])  24.9 us
    pallas_call x1, Pallas kernels, middle(): pl.pallas_call(partial(middle_kernel, len(pieces), pair, shard), out_shap...  24.8 us
    unnamed x183, local copies, waits for them, and re-layouts  20.6 us
  transfers between devices with their start and end apart: 68, of which 28 were waited for; matrix products, arithmetic and copies ran while one was open for 9% of the time, Pallas kernels for 37%

profile of v4, /device:TPU:0, one launch (start us, length us, event | category | flops | bytes accessed | tf_op | source)
XLA Modules:
  0.0 465.0 jit_solution(18353286793441435730)
XLA Ops:
  16.9 5.7 %collective-permute-done.3 = bf16[24,768]{1,0:T(8,128)(2,1)S(1)} collective-permute-done((bf16[24,768]{1,0:T(8,128)(2,1)S(1)}, bf16[24,768]{1,0:T(8,128)(2,1)S(1)}, u32[]{:S(2)}, u32[]{:S(2)}) %collective-permute-start.3) | collective-permute-done | bytes 36896 | tf_op jit(solution)/shard_map/ppermute | solution.py:54
  50.9 4.1 collective-permute-start.11
  56.3 5.3 %collective-permute-done.17 = bf16[1,1,4,4,24,768]{5,4,2,3,0,1:T(8,128)(2,1)S(1)} collective-permute-done((bf16[1,1,4,4,24,768]{5,4,2,3,0,1:T(8,128)(2,1)S(1)}, bf16[1,1,4,4,24,768]{5,4,2,3,0,1:T(8,128)(2,1)S(1)}, u32[]{:S(2)}, u32[]{:S(2)}) %collective-permute-start.17) | collective-permute-done | bytes 589856 | tf_op jit(solution)/shard_map/ppermute | solution.py:764
  66.3 15.6 %collective-permute-done.12 = bf16[216,768]{1,0:T(8,128)(2,1)} collective-permute-done((bf16[216,768]{1,0:T(8,128)(2,1)}, bf16[216,768]{1,0:T(8,128)(2,1)}, u32[]{:S(2)}, u32[]{:S(2)}) %collective-permute-start.12) | collective-permute-done | bytes 331808 | tf_op jit(solution)/shard_map/ppermute | solution.py:67
  86.3 16.0 %attend_forward.4 = (bf16[2048,384]{1,0:T(8,128)(2,1)S(1)}, bf16[2048,384]{1,0:T(8,128)(2,1)S(1)}, f32[3,80,2048]{2,1,0:T(8,128)S(1)}) custom-call(s32[4,4]{1,0:T(4,128)S(1)} %get-tuple-element.356.refs_0_, s32[4,4,4]{2,1,0:T(4,128)S(1)} %select_reduce_fusion.1.refs_1_, s32[16]{0:T(128)S(1)} %sub.57.refs_2_, bf16[512,768]{1,0:T(8,128)(2,1)S(1)} %copy-done, ...), custom_call_target="tpu_custom_call" | custom-call | flops 12000000000 | bytes 10485760 | tf_op jit(solution)/shard_map/attend_forward/pallas_call | solution.py:266
  103.5 9.3 %collective-permute-done.16 = bf16[216,768]{1,0:T(8,128)(2,1)S(1)} collective-permute-done((bf16[216,768]{1,0:T(8,128)(2,1)}, bf16[216,768]{1,0:T(8,128)(2,1)S(1)}, u32[]{:S(2)}, u32[]{:S(2)}) %collective-permute-start.16) | collective-permute-done | bytes 331808 | tf_op jit(solution)/shard_map/ppermute | solution.py:67
  117.9 10.4 %attend_forward.5 = (bf16[2048,384]{1,0:T(8,128)(2,1)S(1)}, f32[3,80,2048]{2,1,0:T(8,128)S(1)}) custom-call(s32[4,4]{1,0:T(4,128)S(1)} %get-tuple-element.356.refs_0_, s32[4,4,4]{2,1,0:T(4,128)S(1)} %select_reduce_fusion.1.refs_1_, s32[16]{0:T(128)S(1)} %sub.57.refs_2_, bf16[512,768]{1,0:T(8,128)(2,1)S(1)} %collective-permute-done.1.refs_3_.refs_9_, ...), custom_call_target="tpu_custom_call" | custom-call | flops 12000000000 | bytes 10485760 | tf_op jit(solution)/shard_map/attend_forward/pallas_call | solution.py:266
  128.3 5.4 %collective-permute-done.20.refs_11_ = bf16[432,768]{1,0:T(8,128)(2,1)} collective-permute-done((bf16[432,768]{1,0:T(8,128)(2,1)S(1)}, bf16[432,768]{1,0:T(8,128)(2,1)}, u32[]{:S(2)}, u32[]{:S(2)}) %collective-permute-start.20) | collective-permute-done | bytes 663584 | tf_op jit(solution)/shard_map/ppermute | solution.py:54
  133.7 16.0 %collective-permute-done.19.refs_4_.refs_10_ = bf16[512,768]{1,0:T(8,128)(2,1)S(1)} collective-permute-done((bf16[512,768]{1,0:T(8,128)(2,1)S(1)}, bf16[512,768]{1,0:T(8,128)(2,1)S(1)}, u32[]{:S(2)}, u32[]{:S(2)}) %collective-permute-start.19) | collective-permute-done | bytes 786464 | tf_op jit(solution)/shard_map/ppermute | solution.py:54
  153.2 10.6 %attend_forward.6 = (bf16[2048,384]{1,0:T(8,128)(2,1)S(1)}, f32[3,80,2048]{2,1,0:T(8,128)S(1)}) custom-call(s32[4,4]{1,0:T(4,128)S(1)} %get-tuple-element.356.refs_0_, s32[4,4,4]{2,1,0:T(4,128)S(1)} %select_reduce_fusion.1.refs_1_, s32[16]{0:T(128)S(1)} %sub.57.refs_2_, bf16[512,768]{1,0:T(8,128)(2,1)} %collective-permute-done.11.refs_3_.refs_9_, ...), custom_call_target="tpu_custom_call" | custom-call | flops 12000000000 | bytes 10485760 | tf_op jit(solution)/shard_map/attend_forward/pallas_call | solution.py:266
  170.7 14.8 %attend_forward.7 = (bf16[2048,384]{1,0:T(8,128)(2,1)S(1)}, bf16[3,64,2048]{2,1,0:T(8,128)(2,1)S(1)}, f32[3,1,2048]{2,1,0:T(1,128)S(1)}) custom-call(s32[4,4]{1,0:T(4,128)S(1)} %get-tuple-element.356.refs_0_, s32[4,4,4]{2,1,0:T(4,128)S(1)} %select_reduce_fusion.1.refs_1_, s32[16]{0:T(128)S(1)} %sub.57.refs_2_, ...), custom_call_target="tpu_custom_call" | custom-call | flops 12000000000 | bytes 10485760 | tf_op jit(solution)/shard_map/attend_forward/pallas_call | solution.py:266
  193.5 4.2 collective-permute-done.30.refs_4_.refs_7_
  201.0 24.8 %middle.1 = (bf16[512,768]{1,0:T(8,128)(2,1)}, f32[512,768]{1,0:T(8,128)}, bf16[512,768]{1,0:T(8,128)(2,1)}, bf16[512,768]{1,0:T(8,128)(2,1)}, bf16[512,3072]{1,...) custom-call(s32[16]{0:T(128)} %stack.170.refs_0_, ...), custom_call_target="tpu_custom_call" | custom-call | flops 12000000000 | bytes 25165824 | tf_op jit(solution)/shard_map/middle/pallas_call | solution.py:588
  225.8 7.0 %grad_down.1 = (bf16[1536,768]{1,0:T(8,128)(2,1)}, bf16[1536,768]{1,0:T(8,128)(2,1)}) custom-call(s32[1]{0:T(128)} %bitcast.82.core_ref.refs_0_, bf16[512,3072]{1,0:T(8,128)(2,1)} %get-tuple-element.236.hidden_ref, bf16[512,768]{1,0:T(8,128)(2,1)} %cot_ref.1), custom_call_target="tpu_custom_call" | custom-call | flops 3000000000 | bytes 10485760 | tf_op jit(solution)/shard_map/grad_down/pallas_call | solution.py:663
  235.3 9.3 %grad_wide.1 = (bf16[384,3840]{1,0:T(8,128)(2,1)}, bf16[384,3840]{1,0:T(8,128)(2,1)}) custom-call(s32[1]{0:T(128)} %bitcast.82.core_ref.refs_0_, s32[4]{0:T(128)} %copy-done.71, bf16[512,768]{1,0:T(8,128)(2,1)} %get-tuple-element.238.refs_2_, bf16[512,3072]{1,0:T(8,128)(2,1)} %get-tuple-element.239.refs_3_, bf16[512,768]{1,0:T(8,128)(2,1)} %get-tuple-element.240.refs_4_, ...), custom_call_target="tpu_custom_call" | custom-call | flops 4000000000 | bytes 12582912 | tf_op jit(solution)/shard_map/grad_wide/pallas_call | solution.py:686
  250.7 30.8 %attend_backward.4 = (bf16[2,512,768]{2,1,0:T(8,128)(2,1)S(1)}, bf16[2,512,768]{2,1,0:T(8,128)(2,1)}, f32[384,768]{1,0:T(8,128)S(1)}, f32[2048,384]{1,0:T(8,128)S(1)}, f32[8,768]{1,0:T(8,128)S(1)}) custom-call(s32[4,4]{1,0:T(4,128)S(1)} %get-tuple-element.356.refs_0_, s32[4,4,4]{2,1,0:T(4,128)S(1)} %select_reduce_fusion.1.refs_1_, s32[16]{0:T(128)S(1)} %sub.57.refs_2_, ...), custom_call_target="tpu_custom_call" | custom-call | flops 24999999488 | bytes 16777216 | tf_op jit(solution)/shard_map/attend_backward/pallas_call | solution.py:446
  298.3 23.8 %attend_backward.5 = (bf16[2,512,768]{2,1,0:T(8,128)(2,1)S(1)}, bf16[2,512,768]{2,1,0:T(8,128)(2,1)}, f32[384,768]{1,0:T(8,128)S(1)}, f32[2048,384]{1,0:T(8,128)S(1)}, f32[8,768]{1,0:T(8,128)S(1)}) custom-call(s32[4,4]{1,0:T(4,128)S(1)} %get-tuple-element.356.refs_0_, s32[4,4,4]{2,1,0:T(4,128)S(1)} %select_reduce_fusion.1.refs_1_, s32[16]{0:T(128)S(1)} %sub.57.refs_2_, ...), custom_call_target="tpu_custom_call" | custom-call | flops 24999999488 | bytes 16777216 | tf_op jit(solution)/shard_map/attend_backward/pallas_call | solution.py:446
  340.6 4.4 collective-permute-start.50
  345.1 22.4 %attend_backward.6 = (bf16[2,512,768]{2,1,0:T(8,128)(2,1)S(1)}, bf16[2,512,768]{2,1,0:T(8,128)(2,1)S(1)}, f32[384,768]{1,0:T(8,128)S(1)}, f32[2048,384]{1,0:T(8,128)S(1)}, f32[8,768]{1,0:T(8,128)S(1)}) custom-call(s32[4,4]{1,0:T(4,128)S(1)} %get-tuple-element.356.refs_0_, s32[4,4,4]{2,1,0:T(4,128)S(1)} %select_reduce_fusion.1.refs_1_, s32[16]{0:T(128)S(1)} %sub.57.refs_2_, ...), custom_call_target="tpu_custom_call" | custom-call | flops 24999999488 | bytes 16777216 | tf_op jit(solution)/shard_map/attend_backward/pallas_call | solution.py:446
  378.2 4.1 collective-permute-start.56
  386.0 32.9 %attend_backward.7 = (bf16[2,512,768]{2,1,0:T(8,128)(2,1)S(1)}, bf16[2,512,768]{2,1,0:T(8,128)(2,1)S(1)}, bf16[768,704]{1,0:T(8,128)(2,1)S(1)}) custom-call(s32[4,4]{1,0:T(4,128)S(1)} %get-tuple-element.356.refs_0_, s32[4,4,4]{2,1,0:T(4,128)S(1)} %select_reduce_fusion.1.refs_1_, s32[16]{0:T(128)S(1)} %sub.57.refs_2_, bf16[2048,384]{1,0:T(8,128)(2,1)S(1)} %copy-done.27, ...), custom_call_target="tpu_custom_call" | custom-call | flops 24999999488 | bytes 16777216 | tf_op jit(solution)/shard_map/attend_backward/pallas_call | solution.py:446
  425.9 12.4 %collective-permute-done.61 = bf16[1,4,4,24,704]{4,3,1,2,0:T(8,128)(2,1)S(1)} collective-permute-done((bf16[1,4,4,24,704]{4,3,1,2,0:T(8,128)(2,1)S(1)}, bf16[1,4,4,24,704]{4,3,1,2,0:T(8,128)(2,1)S(1)}, u32[]{:S(2)}, u32[]{:S(2)}) %collective-permute-start.61) | collective-permute-done | bytes 540704 | tf_op jit(solution)/shard_map/ppermute | solution.py:740
  438.4 4.3 collective-permute-done.59
  453.7 4.4 collective-permute-done.64
  (412 shorter events, 156.2 us)
Async XLA Ops:
  0.7 42.7 %collective-permute-start = (bf16[512,768]{1,0:T(8,128)(2,1)}, bf16[512,768]{1,0:T(8,128)(2,1)S(1)}, u32[]{:S(2)}, u32[]{:S(2)}) collective-permute-start(bf16[512,768]{1,0:T(8,128)(2,1)} %refs_9_.1), channel_id=1, source_target_pairs={{0,8},{4,12},{8,0},{12,4},{1,9},{5,13},{9,1},{13,5},{2,10},{6,14},... | collective-permute-start | bytes 2359304 | tf_op jit(solution)/shard_map/ppermute | solution.py:54
  3.7 40.3 %collective-permute-start.1 = (bf16[512,768]{1,0:T(8,128)(2,1)}, bf16[512,768]{1,0:T(8,128)(2,1)S(1)}, u32[]{:S(2)}, u32[]{:S(2)}) collective-permute-start(bf16[512,768]{1,0:T(8,128)(2,1)} %refs_9_.1), channel_id=1, source_target_pairs={{0,1},{1,3},{3,2},{2,0},{4,5},{5,7},{7,6},{6,4},{8,9},{9,11},{11,1... | collective-permute-start | bytes 2359304 | tf_op jit(solution)/shard_map/ppermute | solution.py:67
  49.4 32.5 %collective-permute-start.9 = (bf16[2,512,768]{2,1,0:T(8,128)(2,1)}, bf16[2,512,768]{2,1,0:T(8,128)(2,1)}, u32[]{:S(2)}, u32[]{:S(2)}) collective-permute-start(bf16[2,512,768]{2,1,0:T(8,128)(2,1)} %pad_maximum_fusion), channel_id=1, source_target_pairs={{0,4},{4,0},{8,12},{12,8},{1,5},{5,1},{9,13},{13,9},{2,6},{6,2},{1... | collective-permute-start | bytes 4718600 | tf_op jit(solution)/shard_map/ppermute | solution.py:54
  49.6 32.4 %collective-permute-start.10 = (bf16[512,768]{1,0:T(8,128)(2,1)S(1)}, bf16[512,768]{1,0:T(8,128)(2,1)}, u32[]{:S(2)}, u32[]{:S(2)}) collective-permute-start(bf16[512,768]{1,0:T(8,128)(2,1)S(1)} %collective-permute-done.1.refs_3_.refs_9_), channel_id=1, source_target_pairs={{0,8},{4,12},{8,0},{12,4},{1,9},{5,13},{9,1},{13,5},{2,10},{6,14},... | collective-permute-start | bytes 2359304 | tf_op jit(solution)/shard_map/ppermute | solution.py:54
  50.9 31.1 %collective-permute-start.11 = (bf16[512,768]{1,0:T(8,128)(2,1)S(1)}, bf16[512,768]{1,0:T(8,128)(2,1)}, u32[]{:S(2)}, u32[]{:S(2)}) collective-permute-start(bf16[512,768]{1,0:T(8,128)(2,1)S(1)} %collective-permute-done.1.refs_3_.refs_9_), channel_id=1, source_target_pairs={{0,1},{1,3},{3,2},{2,0},{4,5},{5,7},{7,6},{6,4},{8,9},{9,11},{11,1... | collective-permute-start | bytes 2359304 | tf_op jit(solution)/shard_map/ppermute | solution.py:67
  83.3 29.6 %collective-permute-start.13 = (bf16[2,512,768]{2,1,0:T(8,128)(2,1)S(1)}, bf16[2,512,768]{2,1,0:T(8,128)(2,1)S(1)}, u32[]{:S(2)}, u32[]{:S(2)}) collective-permute-start(bf16[2,512,768]{2,1,0:T(8,128)(2,1)S(1)} %pad_maximum_fusion.1), channel_id=1, source_target_pairs={{0,4},{4,0},{8,12},{12,8},{1,5},{5,1},{9,13},{13,9},{2,6},{6,2},{1... | collective-permute-start | bytes 4718600 | tf_op jit(solution)/shard_map/ppermute | solution.py:54
  84.1 28.8 %collective-permute-start.14 = (bf16[512,768]{1,0:T(8,128)(2,1)}, bf16[512,768]{1,0:T(8,128)(2,1)S(1)}, u32[]{:S(2)}, u32[]{:S(2)}) collective-permute-start(bf16[512,768]{1,0:T(8,128)(2,1)} %collective-permute-done.11.refs_3_.refs_9_), channel_id=1, source_target_pairs={{0,8},{4,12},{8,0},{12,4},{1,9},{5,13},{9,1},{13,5},{2,10},{6,14},... | collective-permute-start | bytes 2359304 | tf_op jit(solution)/shard_map/ppermute | solution.py:54
  114.9 34.8 %collective-permute-start.18 = (bf16[2,512,768]{2,1,0:T(8,128)(2,1)S(1)}, bf16[2,512,768]{2,1,0:T(8,128)(2,1)S(1)}, u32[]{:S(2)}, u32[]{:S(2)}) collective-permute-start(bf16[2,512,768]{2,1,0:T(8,128)(2,1)S(1)} %pad_maximum_fusion.2), channel_id=1, source_target_pairs={{0,4},{4,0},{8,12},{12,8},{1,5},{5,1},{9,13},{13,9},{2,6},{6,2},{1... | collective-permute-start | bytes 4718600 | tf_op jit(solution)/shard_map/ppermute | solution.py:54
  115.3 34.5 %collective-permute-start.21 = (bf16[864,768]{1,0:T(8,128)(2,1)S(1)}, bf16[864,768]{1,0:T(8,128)(2,1)S(1)}, u32[]{:S(2)}, u32[]{:S(2)}) collective-permute-start(bf16[864,768]{1,0:T(8,128)(2,1)S(1)} %get-tuple-element.394.refs_9_), channel_id=1, source_target_pairs={{0,16},{16,0},{1,17},{17,1},{2,18},{18,2},{3,19},{19,3},{4,20},{20... | collective-permute-start | bytes 3981320 | tf_op jit(solution)/shard_map/ppermute | solution.py:771
  117.1 32.7 %collective-permute-start.19 = (bf16[512,768]{1,0:T(8,128)(2,1)S(1)}, bf16[512,768]{1,0:T(8,128)(2,1)S(1)}, u32[]{:S(2)}, u32[]{:S(2)}) collective-permute-start(bf16[512,768]{1,0:T(8,128)(2,1)S(1)} %collective-permute-done.15.refs_3_.refs_9_), channel_id=1, source_target_pairs={{0,8},{4,12},{8,0},{12,4},{1,9},{5,13},{9,1},{13,5},{2,10},{6,14},... | collective-permute-start | bytes 2359304 | tf_op jit(solution)/shard_map/ppermute | solution.py:54
  153.2 35.3 %collective-permute-start.27 = (bf16[864,768]{1,0:T(8,128)(2,1)S(1)}, bf16[864,768]{1,0:T(8,128)(2,1)}, u32[]{:S(2)}, u32[]{:S(2)}) collective-permute-start(bf16[864,768]{1,0:T(8,128)(2,1)S(1)} %collective-permute-done.21.refs_10_), channel_id=1, source_target_pairs={{0,4},{4,0},{8,12},{12,8},{1,5},{5,1},{9,13},{13,9},{2,6},{6,2},{1... | collective-permute-start | bytes 3981320 | tf_op jit(solution)/shard_map/ppermute | solution.py:54
  244.7 41.2 %collective-permute-start.40 = (bf16[2,2,4,24,3840]{4,3,2,1,0:T(8,128)(2,1)}, bf16[2,2,4,24,3840]{4,3,2,1,0:T(8,128)(2,1)}, u32[]{:S(2)}, u32[]{:S(2)}) collective-permute-start(bf16[2,2,4,24,3840]{4,3,2,1,0:T(8,128)(2,1)} %bitcast.244), channel_id=1, source_target_pairs={{0,4},{4,0},{8,12},{12,8},{1,5},{5,1},{9,13},{13,9},{2,6},{6,2},{1... | collective-permute-start | bytes 8847368 | tf_op jit(solution)/shard_map/ppermute | solution.py:54
  247.8 37.1 %collective-permute-start.39 = (bf16[1,2,4,96,768]{4,3,2,1,0:T(8,128)(2,1)S(1)}, bf16[1,2,4,96,768]{4,3,2,1,0:T(8,128)(2,1)S(1)}, u32[]{:S(2)}, u32[]{:S(2)}) collective-permute-start(bf16[1,2,4,96,768]{4,3,2,1,0:T(8,128)(2,1)S(1)} %constant_dynamic-slice_fusion.7), channel_id=1, source_target_pairs={{0,16},{16,0},{1,17},{17,1},{2,18},{18,2},{3,19},{19,3},{4,20},{20... | collective-permute-start | bytes 3538952 | tf_op jit(solution)/shard_map/ppermute | solution.py:740
  295.6 34.6 %collective-permute-start.44 = (bf16[1,2,4,24,3840]{4,3,2,1,0:T(8,128)(2,1)S(1)}, bf16[1,2,4,24,3840]{4,3,2,1,0:T(8,128)(2,1)S(1)}, u32[]{:S(2)}, u32[]{:S(2)}) collective-permute-start(bf16[1,2,4,24,3840]{4,3,2,1,0:T(8,128)(2,1)S(1)} %constant_dynamic-slice_fusion.6), channel_id=1, source_target_pairs={{0,16},{16,0},{1,17},{17,1},{2,18},{18,2},{3,19},{19,3},{4,20},{20... | collective-permute-start | bytes 4423688 | tf_op jit(solution)/shard_map/ppermute | solution.py:740
  296.2 29.3 %collective-permute-start.43 = (bf16[4,96,768]{2,1,0:T(8,128)(2,1)S(1)}, bf16[4,96,768]{2,1,0:T(8,128)(2,1)S(1)}, u32[]{:S(2)}, u32[]{:S(2)}) collective-permute-start(bf16[4,96,768]{2,1,0:T(8,128)(2,1)S(1)} %dynamic-slice_bitcast_fusion.1), channel_id=1, source_target_pairs={{0,8},{4,12},{8,0},{12,4},{1,9},{5,13},{9,1},{13,5},{2,10},{6,14},... | collective-permute-start | bytes 1769480 | tf_op jit(solution)/shard_map/ppermute | solution.py:54
  297.1 31.1 %collective-permute-start.42 = (bf16[512,768]{1,0:T(8,128)(2,1)S(1)}, bf16[512,768]{1,0:T(8,128)(2,1)S(1)}, u32[]{:S(2)}, u32[]{:S(2)}) collective-permute-start(bf16[512,768]{1,0:T(8,128)(2,1)S(1)} %get-tuple-element.280), channel_id=1, source_target_pairs={{0,8},{4,12},{8,0},{12,4},{1,9},{5,13},{9,1},{13,5},{2,10},{6,14},... | collective-permute-start | bytes 2359304 | tf_op jit(solution)/shard_map/ppermute | solution.py:54
  338.5 32.1 %collective-permute-start.48 = (bf16[4,24,3840]{2,1,0:T(8,128)(2,1)S(1)}, bf16[4,24,3840]{2,1,0:T(8,128)(2,1)S(1)}, u32[]{:S(2)}, u32[]{:S(2)}) collective-permute-start(bf16[4,24,3840]{2,1,0:T(8,128)(2,1)S(1)} %dynamic-slice_bitcast_fusion), channel_id=1, source_target_pairs={{0,8},{4,12},{8,0},{12,4},{1,9},{5,13},{9,1},{13,5},{2,10},{6,14},... | collective-permute-start | bytes 2211848 | tf_op jit(solution)/shard_map/ppermute | solution.py:54
  339.4 34.9 %collective-permute-start.46 = (bf16[512,768]{1,0:T(8,128)(2,1)S(1)}, bf16[512,768]{1,0:T(8,128)(2,1)S(1)}, u32[]{:S(2)}, u32[]{:S(2)}) collective-permute-start(bf16[512,768]{1,0:T(8,128)(2,1)S(1)} %get-tuple-element.302), channel_id=1, source_target_pairs={{0,8},{4,12},{8,0},{12,4},{1,9},{5,13},{9,1},{13,5},{2,10},{6,14},... | collective-permute-start | bytes 2359304 | tf_op jit(solution)/shard_map/ppermute | solution.py:54
  340.6 33.7 %collective-permute-start.47 = (bf16[512,768]{1,0:T(8,128)(2,1)S(1)}, bf16[512,768]{1,0:T(8,128)(2,1)S(1)}, u32[]{:S(2)}, u32[]{:S(2)}) collective-permute-start(bf16[512,768]{1,0:T(8,128)(2,1)S(1)} %add_convert_fusion.8), channel_id=1, source_target_pairs={{0,2},{1,0},{3,1},{2,3},{4,6},{5,4},{7,5},{6,7},{8,10},{9,8},{11,9... | collective-permute-start | bytes 2359304 | tf_op jit(solution)/shard_map/ppermute | solution.py:67
  378.2 40.8 %collective-permute-start.55 = (bf16[24,3840]{1,0:T(8,128)(2,1)S(1)}, bf16[24,3840]{1,0:T(8,128)(2,1)S(1)}, u32[]{:S(2)}, u32[]{:S(2)}) collective-permute-start(bf16[24,3840]{1,0:T(8,128)(2,1)S(1)} %get-tuple-element.386), channel_id=1, source_target_pairs={{0,2},{1,0},{3,1},{2,3},{4,6},{5,4},{7,5},{6,7},{8,10},{9,8},{11,9... | collective-permute-start | bytes 552968 | tf_op jit(solution)/shard_map/ppermute | solution.py:67
  378.2 40.8 %collective-permute-start.56 = (bf16[24,3840]{1,0:T(8,128)(2,1)S(1)}, bf16[24,3840]{1,0:T(8,128)(2,1)S(1)}, u32[]{:S(2)}, u32[]{:S(2)}) collective-permute-start(bf16[24,3840]{1,0:T(8,128)(2,1)S(1)} %get-tuple-element.385), channel_id=1, source_target_pairs={{0,3},{1,2},{3,0},{2,1},{4,7},{5,6},{7,4},{6,5},{8,11},{9,10},{11,... | collective-permute-start | bytes 552968 | tf_op jit(solution)/shard_map/ppermute | solution.py:67
  382.3 36.7 %collective-permute-start.57 = (bf16[24,3840]{1,0:T(8,128)(2,1)S(1)}, bf16[24,3840]{1,0:T(8,128)(2,1)S(1)}, u32[]{:S(2)}, u32[]{:S(2)}) collective-permute-start(bf16[24,3840]{1,0:T(8,128)(2,1)S(1)} %get-tuple-element.384), channel_id=1, source_target_pairs={{0,1},{1,3},{3,2},{2,0},{4,5},{5,7},{7,6},{6,4},{8,9},{9,11},{11,1... | collective-permute-start | bytes 552968 | tf_op jit(solution)/shard_map/ppermute | solution.py:67
  382.3 36.7 %collective-permute-start.53 = (bf16[512,768]{1,0:T(8,128)(2,1)S(1)}, bf16[512,768]{1,0:T(8,128)(2,1)S(1)}, u32[]{:S(2)}, u32[]{:S(2)}) collective-permute-start(bf16[512,768]{1,0:T(8,128)(2,1)S(1)} %get-tuple-element.322), channel_id=1, source_target_pairs={{0,8},{4,12},{8,0},{12,4},{1,9},{5,13},{9,1},{13,5},{2,10},{6,14},... | collective-permute-start | bytes 2359304 | tf_op jit(solution)/shard_map/ppermute | solution.py:54
  383.1 35.9 %collective-permute-start.54 = (bf16[512,768]{1,0:T(8,128)(2,1)S(1)}, bf16[512,768]{1,0:T(8,128)(2,1)S(1)}, u32[]{:S(2)}, u32[]{:S(2)}) collective-permute-start(bf16[512,768]{1,0:T(8,128)(2,1)S(1)} %add_convert_fusion.5), channel_id=1, source_target_pairs={{0,2},{1,0},{3,1},{2,3},{4,6},{5,4},{7,5},{6,7},{8,10},{9,8},{11,9... | collective-permute-start | bytes 2359304 | tf_op jit(solution)/shard_map/ppermute | solution.py:67
  (126 other events, 1474.0 us)

commit v5 on v4

--- a/solution.py
+++ b/solution.py
@@ -14,8 +14,6 @@
 LANES = 128
 EPSILON = 1e-05
 MASKED = -1e30
-LOG2E = 1.4426950408889634
-LN2 = 0.6931471805599453
 ALL_AXES = ("seq", "head", "ctx")
 BF16 = jnp.bfloat16
 F32 = jnp.float32
@@ -130,7 +128,7 @@
     if plane == 0:
         q_ref = refs.pop(0)
     if last:
-        out_ref, lse_ref = refs.pop(0), refs.pop(0)
+        out_ref, exact_ref, lse_ref = refs.pop(0), refs.pop(0), refs.pop(0)
         keys, values_t, q_ext, acc, top, kv_copy, copied = refs
     else:
         acc = refs.pop(0)
@@ -143,7 +141,7 @@
         normed = normed.astype(BF16)
         kv_ref[rows, :] = dot_on(normed, w_ref[:, : 3 * LANES], 1, 0).astype(BF16)
         if plane == 0:
-            own = dot_on(normed, w_ref[:, 3 * LANES :], 1, 0) * (HDIM ** (-0.5) * LOG2E)
+            own = dot_on(normed, w_ref[:, 3 * LANES :], 1, 0) * HDIM ** (-0.5)
             q_ref[rows, :] = own.astype(BF16)
     fill_keys(4, kv_ref, valid_ref, keys, values_t=values_t, marks_first=4 * plane)
     if plane == 0:
@@ -177,7 +175,7 @@
             for head in range(3):
                 if head == 0:
                     ready.append(scores_of(slot, 2))
-                weights = jnp.exp2(ready.pop(0)).astype(BF16)
+                weights = jnp.exp(ready.pop(0)).astype(BF16)
                 acc[head, :, q_rows] += dot_on(values_t[head, :, rows], weights, 1, 0)
             return carry_in
 
@@ -214,9 +212,9 @@
                         scores = scores_of(slot, head)
                         old = top[head, :, q_rows]
                         now = jnp.maximum(old, jnp.max(scores, axis=0, keepdims=True))
-                        weights = jnp.exp2(scores - now).astype(BF16)
+                        weights = jnp.exp(scores - now).astype(BF16)
                         top[head, :, q_rows] = now
-                        acc[head, :, q_rows] = acc[head, :, q_rows] * jnp.exp2(
+                        acc[head, :, q_rows] = acc[head, :, q_rows] * jnp.exp(
                             old - now
                         ) + dot_on(values_t[head, :, rows], weights, 1, 0)
                     return carry_in
@@ -228,8 +226,10 @@
 
     for head in range(3):
         total = acc[head, 64:65, :]
-        out_ref[head] = (acc[head, 0:64, :] / total).astype(BF16)
-        lse_ref[head] = top[head] + jnp.log2(total)
+        result = acc[head, 0:64, :] / total
+        exact_ref[head] = result
+        out_ref[head] = result.astype(BF16)
+        lse_ref[head] = top[head] + jnp.log(total)
 
 
 def attend_forward(plane, last, counts, lists, valid, blocks, weights, queries, acc, before):
@@ -253,6 +253,7 @@
         in_specs += [anywhere] * len(before)
         outs += [
             jax.ShapeDtypeStruct((3, HDIM, kv_rows), BF16),
+            jax.ShapeDtypeStruct((3, HDIM, kv_rows), F32),
             jax.ShapeDtypeStruct((3, 1, kv_rows), F32),
         ]
         scratch += [
@@ -326,7 +327,7 @@
             lanes = slice(head * LANES, (head + 1) * LANES)
             turned = q_ref[q_rows, lanes].astype(F32).T[0:64]
             grad_t = grad_ref[head, :, q_rows].astype(F32)
-            delta = jnp.sum(grad_t * out_ref[head, :, q_rows].astype(F32), axis=0, keepdims=True)
+            delta = jnp.sum(grad_t * out_ref[head, :, q_rows], axis=0, keepdims=True)
             marks = split_three(-lse_ref[head, :, q_rows]) + query_marks(valid_ref[block], BLOCK)
             blank = jnp.zeros((64 - len(marks), BLOCK), F32)
             q_turned[head] = turned.astype(BF16)
@@ -351,7 +352,7 @@
                 if head < 2:
                     ready.append(products(head + 1))
                 scores, grad_probs = ready.pop(0)
-                probs = jnp.exp2(scores)
+                probs = jnp.exp(scores)
                 grad_scores = (probs * grad_probs).astype(BF16)
                 dkv_acc[head, 64:128, rows] += dot_on(
                     grad_ref[head, :, q_rows], probs.astype(BF16), 1, 0
@@ -383,7 +384,7 @@
         rows = pl.ds(pl.multiple_of(slot * BLOCK, BLOCK), BLOCK)
         pieces = []
         for head in range(3):
-            pieces.append(dkv_acc[head, 0:64, rows] * LN2)
+            pieces.append(dkv_acc[head, 0:64, rows])
             pieces.append(dkv_acc[head, 64:128, rows])
         turned = jnp.concatenate(pieces, axis=0)
         part = dot_on(turned.T.astype(BF16), w_ref[:, : 3 * LANES], 1, 1)
@@ -998,7 +999,7 @@
                 queries = tied.pop(0)
             acc = tied.pop(0)
     key_vals.append(results[0])
-    attended, lse = results[1:]
+    attended, exact, lse = results[1:]
     owns = [line, y_line, x_first, x_second, xy_first, xy_second]
     cores = [core_line, core_y, core_x_first]
     cores += [swap_head(v, 1) for v in (x_second, xy_first, xy_second)]
@@ -1075,7 +1076,7 @@
             slot_valid,
             queries,
             key_vals[r],
-            attended,
+            exact,
             lse,
             grad_local,
             weights,

time: 473 us -> 473 us (level)
    unnamed x183 -> x189, local copies, waits for them, and re-layouts: 20.6 us -> 20.4 us
  transfers between devices with their start and end apart: 68 -> 68, of which waited for: 28 -> 29; matrix products, arithmetic and copies ran while one was open for 9% -> 9% of each run, Pallas kernels for 37% -> 37%
where the time goes in v5:
time: 473 us; the launch traced here: 465 us
  Pallas kernels  203 us (43%)
  waiting for transfers between devices  118 us (25%)
  starting transfers between devices  60.4 us (13%)
  local copies, waits for them, and re-layouts  37.7 us (8%)
  other arithmetic  35 us (7%)
  between operations  10.8 us (2%)
    pallas_call x4, Pallas kernels, attend_backward(): pl.pallas_call(partial(backward_kernel, plane, len(carry) > 1, last), out...  110 us
    ppermute x40, waiting for transfers between devices, swap_head(): return lax.ppermute(value, 'head', [(i, i ^ mask) for i in range(count)])  53.7 us
    pallas_call x4, Pallas kernels, attend_forward(): pl.pallas_call(partial(forward_kernel, plane, last), out_shape=tuple(outs...  51.9 us
    ppermute x21, waiting for transfers between devices, ring_send(): return lax.ppermute(value, 'ctx', ring_pairs(lax.axis_size('ctx'), step))  44.8 us
    ppermute x21, starting transfers between devices, ring_send(): return lax.ppermute(value, 'ctx', ring_pairs(lax.axis_size('ctx'), step))  27.7 us
    pallas_call x1, Pallas kernels, middle(): pl.pallas_call(partial(middle_kernel, len(pieces), pair, shard), out_shap...  24.8 us
    ppermute x40, starting transfers between devices, swap_head(): return lax.ppermute(value, 'head', [(i, i ^ mask) for i in range(count)])  24.8 us
    unnamed x189, local copies, waits for them, and re-layouts  20.4 us
  transfers between devices with their start and end apart: 68, of which 29 were waited for; matrix products, arithmetic and copies ran while one was open for 9% of the time, Pallas kernels for 37%

profile of v5, /device:TPU:0, one launch (start us, length us, event | category | flops | bytes accessed | tf_op | source)
XLA Modules:
  0.0 465.1 jit_solution(14932190877301256811)
XLA Ops:
  17.0 5.6 %collective-permute-done.3 = bf16[24,768]{1,0:T(8,128)(2,1)S(1)} collective-permute-done((bf16[24,768]{1,0:T(8,128)(2,1)S(1)}, bf16[24,768]{1,0:T(8,128)(2,1)S(1)}, u32[]{:S(2)}, u32[]{:S(2)}) %collective-permute-start.3) | collective-permute-done | bytes 36896 | tf_op jit(solution)/shard_map/ppermute | solution.py:52
  50.8 4.1 collective-permute-start.11
  56.3 5.3 %collective-permute-done.17 = bf16[1,1,4,4,24,768]{5,4,2,3,0,1:T(8,128)(2,1)S(1)} collective-permute-done((bf16[1,1,4,4,24,768]{5,4,2,3,0,1:T(8,128)(2,1)S(1)}, bf16[1,1,4,4,24,768]{5,4,2,3,0,1:T(8,128)(2,1)S(1)}, u32[]{:S(2)}, u32[]{:S(2)}) %collective-permute-start.17) | collective-permute-done | bytes 589856 | tf_op jit(solution)/shard_map/ppermute | solution.py:765
  66.3 15.6 %collective-permute-done.12 = bf16[216,768]{1,0:T(8,128)(2,1)} collective-permute-done((bf16[216,768]{1,0:T(8,128)(2,1)}, bf16[216,768]{1,0:T(8,128)(2,1)}, u32[]{:S(2)}, u32[]{:S(2)}) %collective-permute-start.12) | collective-permute-done | bytes 331808 | tf_op jit(solution)/shard_map/ppermute | solution.py:65
  86.2 15.9 %attend_forward.4 = (bf16[2048,384]{1,0:T(8,128)(2,1)S(1)}, bf16[2048,384]{1,0:T(8,128)(2,1)S(1)}, f32[3,80,2048]{2,1,0:T(8,128)S(1)}) custom-call(s32[4,4]{1,0:T(4,128)S(1)} %get-tuple-element.360.refs_0_, s32[4,4,4]{2,1,0:T(4,128)S(1)} %select_reduce_fusion.1.refs_1_, s32[16]{0:T(128)S(1)} %sub.57.refs_2_, bf16[512,768]{1,0:T(8,128)(2,1)S(1)} %copy-done, ...), custom_call_target="tpu_custom_call" | custom-call | flops 12000000000 | bytes 10485760 | tf_op jit(solution)/shard_map/attend_forward/pallas_call | solution.py:267
  103.5 9.3 %collective-permute-done.16 = bf16[216,768]{1,0:T(8,128)(2,1)S(1)} collective-permute-done((bf16[216,768]{1,0:T(8,128)(2,1)}, bf16[216,768]{1,0:T(8,128)(2,1)S(1)}, u32[]{:S(2)}, u32[]{:S(2)}) %collective-permute-start.16) | collective-permute-done | bytes 331808 | tf_op jit(solution)/shard_map/ppermute | solution.py:65
  117.9 10.4 %attend_forward.5 = (bf16[2048,384]{1,0:T(8,128)(2,1)S(1)}, f32[3,80,2048]{2,1,0:T(8,128)S(1)}) custom-call(s32[4,4]{1,0:T(4,128)S(1)} %get-tuple-element.360.refs_0_, s32[4,4,4]{2,1,0:T(4,128)S(1)} %select_reduce_fusion.1.refs_1_, s32[16]{0:T(128)S(1)} %sub.57.refs_2_, bf16[512,768]{1,0:T(8,128)(2,1)S(1)} %collective-permute-done.1.refs_3_.refs_9_, ...), custom_call_target="tpu_custom_call" | custom-call | flops 12000000000 | bytes 10485760 | tf_op jit(solution)/shard_map/attend_forward/pallas_call | solution.py:267
  128.3 5.4 %collective-permute-done.20.refs_11_ = bf16[432,768]{1,0:T(8,128)(2,1)} collective-permute-done((bf16[432,768]{1,0:T(8,128)(2,1)S(1)}, bf16[432,768]{1,0:T(8,128)(2,1)}, u32[]{:S(2)}, u32[]{:S(2)}) %collective-permute-start.20) | collective-permute-done | bytes 663584 | tf_op jit(solution)/shard_map/ppermute | solution.py:52
  133.7 16.0 %collective-permute-done.19.refs_4_.refs_10_ = bf16[512,768]{1,0:T(8,128)(2,1)S(1)} collective-permute-done((bf16[512,768]{1,0:T(8,128)(2,1)S(1)}, bf16[512,768]{1,0:T(8,128)(2,1)S(1)}, u32[]{:S(2)}, u32[]{:S(2)}) %collective-permute-start.19) | collective-permute-done | bytes 786464 | tf_op jit(solution)/shard_map/ppermute | solution.py:52
  153.2 10.6 %attend_forward.6 = (bf16[2048,384]{1,0:T(8,128)(2,1)S(1)}, f32[3,80,2048]{2,1,0:T(8,128)S(1)}) custom-call(s32[4,4]{1,0:T(4,128)S(1)} %get-tuple-element.360.refs_0_, s32[4,4,4]{2,1,0:T(4,128)S(1)} %select_reduce_fusion.1.refs_1_, s32[16]{0:T(128)S(1)} %sub.57.refs_2_, bf16[512,768]{1,0:T(8,128)(2,1)} %collective-permute-done.11.refs_3_.refs_9_, ...), custom_call_target="tpu_custom_call" | custom-call | flops 12000000000 | bytes 10485760 | tf_op jit(solution)/shard_map/attend_forward/pallas_call | solution.py:267
  170.7 14.9 %attend_forward.7 = (bf16[2048,384]{1,0:T(8,128)(2,1)S(1)}, bf16[3,64,2048]{2,1,0:T(8,128)(2,1)S(1)}, f32[3,64,2048]{2,1,0:T(8,128)S(1)}, f32[3,1,2048]{2,1,0:T(1,128)S(1)}) custom-call(s32[4,4]{1,0:T(4,128)S(1)} %get-tuple-element.360.refs_0_, s32[4,4,4]{2,1,0:T(4,128)S(1)} %select_reduce_fusion.1.refs_1_, s32[16]{0:T(128)S(1)} %sub.57.refs_2_, ...), custom_call_target="tpu_custom_call" | custom-call | flops 12000000000 | bytes 10485760 | tf_op jit(solution)/shard_map/attend_forward/pallas_call | solution.py:267
  193.1 4.8 %collective-permute-done.30.refs_4_.refs_7_ = bf16[192,512]{1,0:T(8,128)(2,1)S(1)} collective-permute-done((bf16[192,512]{1,0:T(8,128)(2,1)S(1)}, bf16[192,512]{1,0:T(8,128)(2,1)S(1)}, u32[]{:S(2)}, u32[]{:S(2)}) %collective-permute-start.30) | collective-permute-done | bytes 196640 | tf_op jit(solution)/shard_map/ppermute | solution.py:52
  200.6 24.8 %middle.1 = (bf16[512,768]{1,0:T(8,128)(2,1)}, f32[512,768]{1,0:T(8,128)}, bf16[512,768]{1,0:T(8,128)(2,1)}, bf16[512,768]{1,0:T(8,128)(2,1)}, bf16[512,3072]{1,...) custom-call(s32[16]{0:T(128)} %stack.170.refs_0_, ...), custom_call_target="tpu_custom_call" | custom-call | flops 12000000000 | bytes 25165824 | tf_op jit(solution)/shard_map/middle/pallas_call | solution.py:589
  225.5 6.9 %grad_down.1 = (bf16[1536,768]{1,0:T(8,128)(2,1)}, bf16[1536,768]{1,0:T(8,128)(2,1)}) custom-call(s32[1]{0:T(128)} %bitcast.82.core_ref.refs_0_, bf16[512,3072]{1,0:T(8,128)(2,1)} %get-tuple-element.240.hidden_ref, bf16[512,768]{1,0:T(8,128)(2,1)} %cot_ref.1), custom_call_target="tpu_custom_call" | custom-call | flops 3000000000 | bytes 10485760 | tf_op jit(solution)/shard_map/grad_down/pallas_call | solution.py:664
  234.9 9.4 %grad_wide.1 = (bf16[384,3840]{1,0:T(8,128)(2,1)}, bf16[384,3840]{1,0:T(8,128)(2,1)}) custom-call(s32[1]{0:T(128)} %bitcast.82.core_ref.refs_0_, s32[4]{0:T(128)} %copy-done.76, bf16[512,768]{1,0:T(8,128)(2,1)} %get-tuple-element.242.refs_2_, bf16[512,3072]{1,0:T(8,128)(2,1)} %get-tuple-element.243.refs_3_, bf16[512,768]{1,0:T(8,128)(2,1)} %get-tuple-element.244.refs_4_, ...), custom_call_target="tpu_custom_call" | custom-call | flops 4000000000 | bytes 12582912 | tf_op jit(solution)/shard_map/grad_wide/pallas_call | solution.py:687
  249.9 30.8 %attend_backward.4 = (bf16[2,512,768]{2,1,0:T(8,128)(2,1)S(1)}, bf16[2,512,768]{2,1,0:T(8,128)(2,1)}, f32[384,768]{1,0:T(8,128)S(1)}, f32[2048,384]{1,0:T(8,128)S(1)}, f32[8,768]{1,0:T(8,128)S(1)}) custom-call(s32[4,4]{1,0:T(4,128)S(1)} %get-tuple-element.360.refs_0_, s32[4,4,4]{2,1,0:T(4,128)S(1)} %select_reduce_fusion.1.refs_1_, s32[16]{0:T(128)S(1)} %sub.57.refs_2_, ...), custom_call_target="tpu_custom_call" | custom-call | flops 24999999488 | bytes 16777216 | tf_op jit(solution)/shard_map/attend_backward/pallas_call | solution.py:447
  297.6 23.9 %attend_backward.5 = (bf16[2,512,768]{2,1,0:T(8,128)(2,1)S(1)}, bf16[2,512,768]{2,1,0:T(8,128)(2,1)}, f32[384,768]{1,0:T(8,128)S(1)}, f32[2048,384]{1,0:T(8,128)S(1)}, f32[8,768]{1,0:T(8,128)S(1)}) custom-call(s32[4,4]{1,0:T(4,128)S(1)} %get-tuple-element.360.refs_0_, s32[4,4,4]{2,1,0:T(4,128)S(1)} %select_reduce_fusion.1.refs_1_, s32[16]{0:T(128)S(1)} %sub.57.refs_2_, ...), custom_call_target="tpu_custom_call" | custom-call | flops 24999999488 | bytes 16777216 | tf_op jit(solution)/shard_map/attend_backward/pallas_call | solution.py:447
  339.8 4.4 collective-permute-start.50
  344.3 22.4 %attend_backward.6 = (bf16[2,512,768]{2,1,0:T(8,128)(2,1)S(1)}, bf16[2,512,768]{2,1,0:T(8,128)(2,1)S(1)}, f32[384,768]{1,0:T(8,128)S(1)}, f32[2048,384]{1,0:T(8,128)S(1)}, f32[8,768]{1,0:T(8,128)S(1)}) custom-call(s32[4,4]{1,0:T(4,128)S(1)} %get-tuple-element.360.refs_0_, s32[4,4,4]{2,1,0:T(4,128)S(1)} %select_reduce_fusion.1.refs_1_, s32[16]{0:T(128)S(1)} %sub.57.refs_2_, ...), custom_call_target="tpu_custom_call" | custom-call | flops 24999999488 | bytes 16777216 | tf_op jit(solution)/shard_map/attend_backward/pallas_call | solution.py:447
  377.4 4.1 collective-permute-start.56
  385.3 32.9 %attend_backward.7 = (bf16[2,512,768]{2,1,0:T(8,128)(2,1)S(1)}, bf16[2,512,768]{2,1,0:T(8,128)(2,1)S(1)}, bf16[768,704]{1,0:T(8,128)(2,1)S(1)}) custom-call(s32[4,4]{1,0:T(4,128)S(1)} %get-tuple-element.360.refs_0_, s32[4,4,4]{2,1,0:T(4,128)S(1)} %select_reduce_fusion.1.refs_1_, s32[16]{0:T(128)S(1)} %sub.57.refs_2_, bf16[2048,384]{1,0:T(8,128)(2,1)S(1)} %copy-done.24, ...), custom_call_target="tpu_custom_call" | custom-call | flops 24999999488 | bytes 16777216 | tf_op jit(solution)/shard_map/attend_backward/pallas_call | solution.py:447
  426.2 11.4 %collective-permute-done.61 = bf16[1,4,4,24,704]{4,3,1,2,0:T(8,128)(2,1)S(1)} collective-permute-done((bf16[1,4,4,24,704]{4,3,1,2,0:T(8,128)(2,1)S(1)}, bf16[1,4,4,24,704]{4,3,1,2,0:T(8,128)(2,1)S(1)}, u32[]{:S(2)}, u32[]{:S(2)}) %collective-permute-start.61) | collective-permute-done | bytes 540704 | tf_op jit(solution)/shard_map/ppermute | solution.py:741
  437.6 5.2 %collective-permute-done.59 = bf16[512,768]{1,0:T(8,128)(2,1)S(1)} collective-permute-done((bf16[512,768]{1,0:T(8,128)(2,1)S(1)}, bf16[512,768]{1,0:T(8,128)(2,1)S(1)}, u32[]{:S(2)}, u32[]{:S(2)}) %collective-permute-start.59) | collective-permute-done | bytes 786464 | tf_op jit(solution)/shard_map/ppermute | solution.py:52
  453.9 4.3 collective-permute-done.64
  (418 shorter events, 155.6 us)
Async XLA Ops:
  0.7 42.7 %collective-permute-start = (bf16[512,768]{1,0:T(8,128)(2,1)}, bf16[512,768]{1,0:T(8,128)(2,1)S(1)}, u32[]{:S(2)}, u32[]{:S(2)}) collective-permute-start(bf16[512,768]{1,0:T(8,128)(2,1)} %refs_9_.1), channel_id=1, source_target_pairs={{0,8},{4,12},{8,0},{12,4},{1,9},{5,13},{9,1},{13,5},{2,10},{6,14},... | collective-permute-start | bytes 2359304 | tf_op jit(solution)/shard_map/ppermute | solution.py:52
  3.7 40.3 %collective-permute-start.1 = (bf16[512,768]{1,0:T(8,128)(2,1)}, bf16[512,768]{1,0:T(8,128)(2,1)S(1)}, u32[]{:S(2)}, u32[]{:S(2)}) collective-permute-start(bf16[512,768]{1,0:T(8,128)(2,1)} %refs_9_.1), channel_id=1, source_target_pairs={{0,1},{1,3},{3,2},{2,0},{4,5},{5,7},{7,6},{6,4},{8,9},{9,11},{11,1... | collective-permute-start | bytes 2359304 | tf_op jit(solution)/shard_map/ppermute | solution.py:65
  49.4 32.5 %collective-permute-start.9 = (bf16[2,512,768]{2,1,0:T(8,128)(2,1)}, bf16[2,512,768]{2,1,0:T(8,128)(2,1)}, u32[]{:S(2)}, u32[]{:S(2)}) collective-permute-start(bf16[2,512,768]{2,1,0:T(8,128)(2,1)} %pad_maximum_fusion), channel_id=1, source_target_pairs={{0,4},{4,0},{8,12},{12,8},{1,5},{5,1},{9,13},{13,9},{2,6},{6,2},{1... | collective-permute-start | bytes 4718600 | tf_op jit(solution)/shard_map/ppermute | solution.py:52
  49.6 32.4 %collective-permute-start.10 = (bf16[512,768]{1,0:T(8,128)(2,1)S(1)}, bf16[512,768]{1,0:T(8,128)(2,1)}, u32[]{:S(2)}, u32[]{:S(2)}) collective-permute-start(bf16[512,768]{1,0:T(8,128)(2,1)S(1)} %collective-permute-done.1.refs_3_.refs_9_), channel_id=1, source_target_pairs={{0,8},{4,12},{8,0},{12,4},{1,9},{5,13},{9,1},{13,5},{2,10},{6,14},... | collective-permute-start | bytes 2359304 | tf_op jit(solution)/shard_map/ppermute | solution.py:52
  50.8 31.1 %collective-permute-start.11 = (bf16[512,768]{1,0:T(8,128)(2,1)S(1)}, bf16[512,768]{1,0:T(8,128)(2,1)}, u32[]{:S(2)}, u32[]{:S(2)}) collective-permute-start(bf16[512,768]{1,0:T(8,128)(2,1)S(1)} %collective-permute-done.1.refs_3_.refs_9_), channel_id=1, source_target_pairs={{0,1},{1,3},{3,2},{2,0},{4,5},{5,7},{7,6},{6,4},{8,9},{9,11},{11,1... | collective-permute-start | bytes 2359304 | tf_op jit(solution)/shard_map/ppermute | solution.py:65
  83.2 29.6 %collective-permute-start.13 = (bf16[2,512,768]{2,1,0:T(8,128)(2,1)S(1)}, bf16[2,512,768]{2,1,0:T(8,128)(2,1)S(1)}, u32[]{:S(2)}, u32[]{:S(2)}) collective-permute-start(bf16[2,512,768]{2,1,0:T(8,128)(2,1)S(1)} %pad_maximum_fusion.1), channel_id=1, source_target_pairs={{0,4},{4,0},{8,12},{12,8},{1,5},{5,1},{9,13},{13,9},{2,6},{6,2},{1... | collective-permute-start | bytes 4718600 | tf_op jit(solution)/shard_map/ppermute | solution.py:52
  84.1 28.8 %collective-permute-start.14 = (bf16[512,768]{1,0:T(8,128)(2,1)}, bf16[512,768]{1,0:T(8,128)(2,1)S(1)}, u32[]{:S(2)}, u32[]{:S(2)}) collective-permute-start(bf16[512,768]{1,0:T(8,128)(2,1)} %collective-permute-done.11.refs_3_.refs_9_), channel_id=1, source_target_pairs={{0,8},{4,12},{8,0},{12,4},{1,9},{5,13},{9,1},{13,5},{2,10},{6,14},... | collective-permute-start | bytes 2359304 | tf_op jit(solution)/shard_map/ppermute | solution.py:52
  114.9 34.8 %collective-permute-start.18 = (bf16[2,512,768]{2,1,0:T(8,128)(2,1)S(1)}, bf16[2,512,768]{2,1,0:T(8,128)(2,1)S(1)}, u32[]{:S(2)}, u32[]{:S(2)}) collective-permute-start(bf16[2,512,768]{2,1,0:T(8,128)(2,1)S(1)} %pad_maximum_fusion.2), channel_id=1, source_target_pairs={{0,4},{4,0},{8,12},{12,8},{1,5},{5,1},{9,13},{13,9},{2,6},{6,2},{1... | collective-permute-start | bytes 4718600 | tf_op jit(solution)/shard_map/ppermute | solution.py:52
  115.3 34.5 %collective-permute-start.21 = (bf16[864,768]{1,0:T(8,128)(2,1)S(1)}, bf16[864,768]{1,0:T(8,128)(2,1)S(1)}, u32[]{:S(2)}, u32[]{:S(2)}) collective-permute-start(bf16[864,768]{1,0:T(8,128)(2,1)S(1)} %get-tuple-element.398.refs_9_), channel_id=1, source_target_pairs={{0,16},{16,0},{1,17},{17,1},{2,18},{18,2},{3,19},{19,3},{4,20},{20... | collective-permute-start | bytes 3981320 | tf_op jit(solution)/shard_map/ppermute | solution.py:772
  117.0 32.7 %collective-permute-start.19 = (bf16[512,768]{1,0:T(8,128)(2,1)S(1)}, bf16[512,768]{1,0:T(8,128)(2,1)S(1)}, u32[]{:S(2)}, u32[]{:S(2)}) collective-permute-start(bf16[512,768]{1,0:T(8,128)(2,1)S(1)} %collective-permute-done.15.refs_3_.refs_9_), channel_id=1, source_target_pairs={{0,8},{4,12},{8,0},{12,4},{1,9},{5,13},{9,1},{13,5},{2,10},{6,14},... | collective-permute-start | bytes 2359304 | tf_op jit(solution)/shard_map/ppermute | solution.py:52
  153.2 35.3 %collective-permute-start.27 = (bf16[864,768]{1,0:T(8,128)(2,1)S(1)}, bf16[864,768]{1,0:T(8,128)(2,1)}, u32[]{:S(2)}, u32[]{:S(2)}) collective-permute-start(bf16[864,768]{1,0:T(8,128)(2,1)S(1)} %collective-permute-done.21.refs_10_), channel_id=1, source_target_pairs={{0,4},{4,0},{8,12},{12,8},{1,5},{5,1},{9,13},{13,9},{2,6},{6,2},{1... | collective-permute-start | bytes 3981320 | tf_op jit(solution)/shard_map/ppermute | solution.py:52
  245.1 40.1 %collective-permute-start.40 = (bf16[2,2,4,24,3840]{4,3,2,1,0:T(8,128)(2,1)}, bf16[2,2,4,24,3840]{4,3,2,1,0:T(8,128)(2,1)}, u32[]{:S(2)}, u32[]{:S(2)}) collective-permute-start(bf16[2,2,4,24,3840]{4,3,2,1,0:T(8,128)(2,1)} %bitcast.244), channel_id=1, source_target_pairs={{0,4},{4,0},{8,12},{12,8},{1,5},{5,1},{9,13},{13,9},{2,6},{6,2},{1... | collective-permute-start | bytes 8847368 | tf_op jit(solution)/shard_map/ppermute | solution.py:52
  246.2 37.9 %collective-permute-start.39 = (bf16[1,2,4,96,768]{4,3,2,1,0:T(8,128)(2,1)S(1)}, bf16[1,2,4,96,768]{4,3,2,1,0:T(8,128)(2,1)S(1)}, u32[]{:S(2)}, u32[]{:S(2)}) collective-permute-start(bf16[1,2,4,96,768]{4,3,2,1,0:T(8,128)(2,1)S(1)} %constant_dynamic-slice_fusion.7), channel_id=1, source_target_pairs={{0,16},{16,0},{1,17},{17,1},{2,18},{18,2},{3,19},{19,3},{4,20},{20... | collective-permute-start | bytes 3538952 | tf_op jit(solution)/shard_map/ppermute | solution.py:741
  294.8 34.5 %collective-permute-start.44 = (bf16[1,2,4,24,3840]{4,3,2,1,0:T(8,128)(2,1)S(1)}, bf16[1,2,4,24,3840]{4,3,2,1,0:T(8,128)(2,1)S(1)}, u32[]{:S(2)}, u32[]{:S(2)}) collective-permute-start(bf16[1,2,4,24,3840]{4,3,2,1,0:T(8,128)(2,1)S(1)} %constant_dynamic-slice_fusion.6), channel_id=1, source_target_pairs={{0,16},{16,0},{1,17},{17,1},{2,18},{18,2},{3,19},{19,3},{4,20},{20... | collective-permute-start | bytes 4423688 | tf_op jit(solution)/shard_map/ppermute | solution.py:741
  295.5 29.3 %collective-permute-start.43 = (bf16[4,96,768]{2,1,0:T(8,128)(2,1)S(1)}, bf16[4,96,768]{2,1,0:T(8,128)(2,1)S(1)}, u32[]{:S(2)}, u32[]{:S(2)}) collective-permute-start(bf16[4,96,768]{2,1,0:T(8,128)(2,1)S(1)} %dynamic-slice_bitcast_fusion.1), channel_id=1, source_target_pairs={{0,8},{4,12},{8,0},{12,4},{1,9},{5,13},{9,1},{13,5},{2,10},{6,14},... | collective-permute-start | bytes 1769480 | tf_op jit(solution)/shard_map/ppermute | solution.py:52
  296.3 31.3 %collective-permute-start.42 = (bf16[512,768]{1,0:T(8,128)(2,1)S(1)}, bf16[512,768]{1,0:T(8,128)(2,1)S(1)}, u32[]{:S(2)}, u32[]{:S(2)}) collective-permute-start(bf16[512,768]{1,0:T(8,128)(2,1)S(1)} %get-tuple-element.284), channel_id=1, source_target_pairs={{0,8},{4,12},{8,0},{12,4},{1,9},{5,13},{9,1},{13,5},{2,10},{6,14},... | collective-permute-start | bytes 2359304 | tf_op jit(solution)/shard_map/ppermute | solution.py:52
  337.7 32.1 %collective-permute-start.48 = (bf16[4,24,3840]{2,1,0:T(8,128)(2,1)S(1)}, bf16[4,24,3840]{2,1,0:T(8,128)(2,1)S(1)}, u32[]{:S(2)}, u32[]{:S(2)}) collective-permute-start(bf16[4,24,3840]{2,1,0:T(8,128)(2,1)S(1)} %dynamic-slice_bitcast_fusion), channel_id=1, source_target_pairs={{0,8},{4,12},{8,0},{12,4},{1,9},{5,13},{9,1},{13,5},{2,10},{6,14},... | collective-permute-start | bytes 2211848 | tf_op jit(solution)/shard_map/ppermute | solution.py:52
  338.6 34.9 %collective-permute-start.46 = (bf16[512,768]{1,0:T(8,128)(2,1)S(1)}, bf16[512,768]{1,0:T(8,128)(2,1)S(1)}, u32[]{:S(2)}, u32[]{:S(2)}) collective-permute-start(bf16[512,768]{1,0:T(8,128)(2,1)S(1)} %get-tuple-element.306), channel_id=1, source_target_pairs={{0,8},{4,12},{8,0},{12,4},{1,9},{5,13},{9,1},{13,5},{2,10},{6,14},... | collective-permute-start | bytes 2359304 | tf_op jit(solution)/shard_map/ppermute | solution.py:52
  339.8 33.7 %collective-permute-start.47 = (bf16[512,768]{1,0:T(8,128)(2,1)S(1)}, bf16[512,768]{1,0:T(8,128)(2,1)S(1)}, u32[]{:S(2)}, u32[]{:S(2)}) collective-permute-start(bf16[512,768]{1,0:T(8,128)(2,1)S(1)} %add_convert_fusion.8), channel_id=1, source_target_pairs={{0,2},{1,0},{3,1},{2,3},{4,6},{5,4},{7,5},{6,7},{8,10},{9,8},{11,9... | collective-permute-start | bytes 2359304 | tf_op jit(solution)/shard_map/ppermute | solution.py:65
  377.3 40.9 %collective-permute-start.55 = (bf16[24,3840]{1,0:T(8,128)(2,1)S(1)}, bf16[24,3840]{1,0:T(8,128)(2,1)S(1)}, u32[]{:S(2)}, u32[]{:S(2)}) collective-permute-start(bf16[24,3840]{1,0:T(8,128)(2,1)S(1)} %get-tuple-element.390), channel_id=1, source_target_pairs={{0,2},{1,0},{3,1},{2,3},{4,6},{5,4},{7,5},{6,7},{8,10},{9,8},{11,9... | collective-permute-start | bytes 552968 | tf_op jit(solution)/shard_map/ppermute | solution.py:65
  377.4 40.8 %collective-permute-start.56 = (bf16[24,3840]{1,0:T(8,128)(2,1)S(1)}, bf16[24,3840]{1,0:T(8,128)(2,1)S(1)}, u32[]{:S(2)}, u32[]{:S(2)}) collective-permute-start(bf16[24,3840]{1,0:T(8,128)(2,1)S(1)} %get-tuple-element.389), channel_id=1, source_target_pairs={{0,3},{1,2},{3,0},{2,1},{4,7},{5,6},{7,4},{6,5},{8,11},{9,10},{11,... | collective-permute-start | bytes 552968 | tf_op jit(solution)/shard_map/ppermute | solution.py:65
  381.5 36.7 %collective-permute-start.57 = (bf16[24,3840]{1,0:T(8,128)(2,1)S(1)}, bf16[24,3840]{1,0:T(8,128)(2,1)S(1)}, u32[]{:S(2)}, u32[]{:S(2)}) collective-permute-start(bf16[24,3840]{1,0:T(8,128)(2,1)S(1)} %get-tuple-element.388), channel_id=1, source_target_pairs={{0,1},{1,3},{3,2},{2,0},{4,5},{5,7},{7,6},{6,4},{8,9},{9,11},{11,1... | collective-permute-start | bytes 552968 | tf_op jit(solution)/shard_map/ppermute | solution.py:65
  381.5 36.7 %collective-permute-start.53 = (bf16[512,768]{1,0:T(8,128)(2,1)S(1)}, bf16[512,768]{1,0:T(8,128)(2,1)S(1)}, u32[]{:S(2)}, u32[]{:S(2)}) collective-permute-start(bf16[512,768]{1,0:T(8,128)(2,1)S(1)} %get-tuple-element.326), channel_id=1, source_target_pairs={{0,8},{4,12},{8,0},{12,4},{1,9},{5,13},{9,1},{13,5},{2,10},{6,14},... | collective-permute-start | bytes 2359304 | tf_op jit(solution)/shard_map/ppermute | solution.py:52
  382.4 35.9 %collective-permute-start.54 = (bf16[512,768]{1,0:T(8,128)(2,1)S(1)}, bf16[512,768]{1,0:T(8,128)(2,1)S(1)}, u32[]{:S(2)}, u32[]{:S(2)}) collective-permute-start(bf16[512,768]{1,0:T(8,128)(2,1)S(1)} %add_convert_fusion.5), channel_id=1, source_target_pairs={{0,2},{1,0},{3,1},{2,3},{4,6},{5,4},{7,5},{6,7},{8,10},{9,8},{11,9... | collective-permute-start | bytes 2359304 | tf_op jit(solution)/shard_map/ppermute | solution.py:65
  (129 other events, 1475.6 us)

commit v6 on v5

--- a/solution.py
+++ b/solution.py
@@ -117,9 +117,9 @@
 def forward_kernel(plane, last, *refs):
     refs = list(refs)
     count_ref, list_ref, valid_ref = refs[:3]
-    x_refs = [refs[3], refs[5].at[0], refs[4], refs[5].at[1]]
-    w_ref = refs[6]
-    refs = refs[7:]
+    x_refs = refs[3:7]
+    w_ref = refs[7]
+    refs = refs[8:]
     if plane:
         q_ref, acc_in = refs.pop(0), refs.pop(0)
     if last:
@@ -282,8 +282,7 @@
     refs = list(refs)
     count_ref, list_ref, valid_ref = refs[:3]
     q_ref, kv_ref, out_ref, lse_ref, grad_ref, w_ref = refs[3:9]
-    x_from = [refs[9], refs[11].at[0], refs[10], refs[11].at[1]]
-    refs = refs[12:]
+    x_from, refs = refs[9:13], refs[13:]
     sum_in, refs = refs[0], refs[1:]
     if carried:
         dq_in, dw_in = refs[:2]
@@ -447,7 +446,7 @@
     result = pl.pallas_call(
         partial(backward_kernel, plane, len(carry) > 1, last),
         out_shape=(half, half) + outs,
-        in_specs=[smem] * 3 + [vmem] * 6 + [anywhere] * 3 + [vmem, anywhere, vmem][: len(carry)],
+        in_specs=[smem] * 3 + [vmem] * 6 + [anywhere] * 4 + [vmem, anywhere, vmem][: len(carry)],
         out_specs=(vmem, vmem) + spaces,
         scratch_shapes=[
             pltpu.VMEM((3, q_rows, LANES), BF16),
@@ -941,7 +940,7 @@
     ready = None
     for r in range(ctx_ax + 1):
         if r < ctx_ax:
-            travelers = [swap_head(jnp.stack([block, near]), 1)]
+            travelers = [swap_head(block, 1), swap_head(near, 1)]
         else:
             travelers = []
         if r + 1 < ctx_ax:
@@ -986,7 +985,7 @@
             xy_second, core_y, core_x_first = extra
             results = tied
             break
-        planes.append([block, near, tied.pop(0)])
+        planes.append([block, tied.pop(0), near, tied.pop(0)])
         ready = planes[-1]
         if r + 1 < ctx_ax:
             block, near = ahead, tied.pop(0)
@@ -1115,9 +1114,7 @@
             if step >= 1:
                 traveling = tied[0]
         carry = (sums, fourth, dw)
-    near_half, far_half, traveling, dw, wide_sum = tie(
-        near_half, far_half, traveling, dw, wide_sum
-    )
+    near_half, far_half, traveling = tie(near_half, far_half, traveling)
     dw_mine = give_over_seq(dw.reshape(seq_ax, heads_ax, ctx_ax, shard, wide))
     taken, carried, *dw_mine = tie(
         swap_head(far_half, 2), ring_send(traveling, -1), *dw_mine

time: 473 us -> 471 us (level)
    ppermute x40 -> x44, waiting for transfers between devices: 53.7 us -> 61.2 us  [swap_head(): return lax.ppermute(value, 'head', [(i, i ^ mask) for i in range(count)])]
    unnamed x189 -> x195, local copies, waits for them, and re-layouts: 20.4 us -> 18.7 us
    ppermute x40 -> x44, starting transfers between devices: 24.8 us -> 26.1 us  [swap_head(): return lax.ppermute(value, 'head', [(i, i ^ mask) for i in range(count)])]
  transfers between devices with their start and end apart: 68 -> 72, of which waited for: 29 -> 26; matrix products, arithmetic and copies ran while one was open for 9% -> 9% of each run, Pallas kernels for 37% -> 37%
where the time goes in v6:
time: 471 us; the launch traced here: 463 us
  Pallas kernels  203 us (43%)
  waiting for transfers between devices  121 us (26%)
  starting transfers between devices  61.5 us (13%)
  local copies, waits for them, and re-layouts  36.5 us (8%)
  other arithmetic  30.5 us (6%)
  between operations  10.9 us (2%)
    pallas_call x4, Pallas kernels, attend_backward(): pl.pallas_call(partial(backward_kernel, plane, len(carry) > 1, last), out...  110 us
    ppermute x44, waiting for transfers between devices, swap_head(): return lax.ppermute(value, 'head', [(i, i ^ mask) for i in range(count)])  61.2 us
    pallas_call x4, Pallas kernels, attend_forward(): pl.pallas_call(partial(forward_kernel, plane, last), out_shape=tuple(outs...  51.9 us
    ppermute x21, waiting for transfers between devices, ring_send(): return lax.ppermute(value, 'ctx', ring_pairs(lax.axis_size('ctx'), step))  40.8 us
    ppermute x21, starting transfers between devices, ring_send(): return lax.ppermute(value, 'ctx', ring_pairs(lax.axis_size('ctx'), step))  27.4 us
    ppermute x44, starting transfers between devices, swap_head(): return lax.ppermute(value, 'head', [(i, i ^ mask) for i in range(count)])  26.1 us
    pallas_call x1, Pallas kernels, middle(): pl.pallas_call(partial(middle_kernel, len(pieces), pair, shard), out_shap...  24.8 us
    unnamed x195, local copies, waits for them, and re-layouts  18.7 us
  transfers between devices with their start and end apart: 72, of which 26 were waited for; matrix products, arithmetic and copies ran while one was open for 9% of the time, Pallas kernels for 37%

profile of v6, /device:TPU:0, one launch (start us, length us, event | category | flops | bytes accessed | tf_op | source)
XLA Modules:
  0.0 463.3 jit_solution(6412500594204527234)
XLA Ops:
  16.5 6.1 %collective-permute-done.3 = bf16[24,768]{1,0:T(8,128)(2,1)S(1)} collective-permute-done((bf16[24,768]{1,0:T(8,128)(2,1)S(1)}, bf16[24,768]{1,0:T(8,128)(2,1)S(1)}, u32[]{:S(2)}, u32[]{:S(2)}) %collective-permute-start.3) | collective-permute-done | bytes 36896 | tf_op jit(solution)/shard_map/ppermute | solution.py:52
  37.7 6.5 %collective-permute-done.7 = bf16[4,24,768]{2,1,0:T(8,128)(2,1)S(1)} collective-permute-done((bf16[4,24,768]{2,1,0:T(8,128)(2,1)S(1)}, bf16[4,24,768]{2,1,0:T(8,128)(2,1)S(1)}, u32[]{:S(2)}, u32[]{:S(2)}) %collective-permute-start.7) | collective-permute-done | bytes 147488 | tf_op jit(solution)/shard_map/ppermute | solution.py:65
  55.3 6.0 %collective-permute-done.19 = bf16[1,1,4,4,24,768]{5,4,2,3,0,1:T(8,128)(2,1)S(1)} collective-permute-done((bf16[1,1,4,4,24,768]{5,4,2,3,0,1:T(8,128)(2,1)S(1)}, bf16[1,1,4,4,24,768]{5,4,2,3,0,1:T(8,128)(2,1)S(1)}, u32[]{:S(2)}, u32[]{:S(2)}) %collective-permute-start.19) | collective-permute-done | bytes 589856 | tf_op jit(solution)/shard_map/ppermute | solution.py:764
  69.2 10.9 %collective-permute-done.14 = bf16[216,768]{1,0:T(8,128)(2,1)} collective-permute-done((bf16[216,768]{1,0:T(8,128)(2,1)}, bf16[216,768]{1,0:T(8,128)(2,1)}, u32[]{:S(2)}, u32[]{:S(2)}) %collective-permute-start.14) | collective-permute-done | bytes 331808 | tf_op jit(solution)/shard_map/ppermute | solution.py:65
  82.5 15.9 %attend_forward.4 = (bf16[2048,384]{1,0:T(8,128)(2,1)S(1)}, bf16[2048,384]{1,0:T(8,128)(2,1)S(1)}, f32[3,80,2048]{2,1,0:T(8,128)S(1)}) custom-call(s32[4,4]{1,0:T(4,128)S(1)} %get-tuple-element.364.refs_0_, s32[4,4,4]{2,1,0:T(4,128)S(1)} %select_reduce_fusion.1.refs_1_, s32[16]{0:T(128)S(1)} %sub.57.refs_2_, bf16[512,768]{1,0:T(8,128)(2,1)S(1)} %copy-done, ...), custom_call_target="tpu_custom_call" | custom-call | flops 12000000000 | bytes 10485760 | tf_op jit(solution)/shard_map/attend_forward/pallas_call | solution.py:267
  100.0 7.8 %collective-permute-done.18 = bf16[216,768]{1,0:T(8,128)(2,1)S(1)} collective-permute-done((bf16[216,768]{1,0:T(8,128)(2,1)}, bf16[216,768]{1,0:T(8,128)(2,1)S(1)}, u32[]{:S(2)}, u32[]{:S(2)}) %collective-permute-start.18) | collective-permute-done | bytes 331808 | tf_op jit(solution)/shard_map/ppermute | solution.py:65
  111.4 14.7 %collective-permute-done.24.refs_11_ = bf16[432,768]{1,0:T(8,128)(2,1)} collective-permute-done((bf16[432,768]{1,0:T(8,128)(2,1)S(1)}, bf16[432,768]{1,0:T(8,128)(2,1)}, u32[]{:S(2)}, u32[]{:S(2)}) %collective-permute-start.24) | collective-permute-done | bytes 663584 | tf_op jit(solution)/shard_map/ppermute | solution.py:52
  127.3 10.4 %attend_forward.5 = (bf16[2048,384]{1,0:T(8,128)(2,1)S(1)}, f32[3,80,2048]{2,1,0:T(8,128)S(1)}) custom-call(s32[4,4]{1,0:T(4,128)S(1)} %get-tuple-element.364.refs_0_, s32[4,4,4]{2,1,0:T(4,128)S(1)} %select_reduce_fusion.1.refs_1_, s32[16]{0:T(128)S(1)} %sub.57.refs_2_, bf16[512,768]{1,0:T(8,128)(2,1)S(1)} %collective-permute-done.1.refs_3_.refs_9_, ...), custom_call_target="tpu_custom_call" | custom-call | flops 12000000000 | bytes 10485760 | tf_op jit(solution)/shard_map/attend_forward/pallas_call | solution.py:267
  137.9 5.0 %collective-permute-done.23.refs_5_.refs_11_ = bf16[512,768]{1,0:T(8,128)(2,1)S(1)} collective-permute-done((bf16[512,768]{1,0:T(8,128)(2,1)S(1)}, bf16[512,768]{1,0:T(8,128)(2,1)S(1)}, u32[]{:S(2)}, u32[]{:S(2)}) %collective-permute-start.23) | collective-permute-done | bytes 786464 | tf_op jit(solution)/shard_map/ppermute | solution.py:52
  143.5 10.8 %collective-permute-done.27.refs_12_ = bf16[432,768]{1,0:T(8,128)(2,1)} collective-permute-done((bf16[432,768]{1,0:T(8,128)(2,1)S(1)}, bf16[432,768]{1,0:T(8,128)(2,1)}, u32[]{:S(2)}, u32[]{:S(2)}) %collective-permute-start.27) | collective-permute-done | bytes 663584 | tf_op jit(solution)/shard_map/ppermute | solution.py:52
  154.4 10.6 %attend_forward.6 = (bf16[2048,384]{1,0:T(8,128)(2,1)S(1)}, f32[3,80,2048]{2,1,0:T(8,128)S(1)}) custom-call(s32[4,4]{1,0:T(4,128)S(1)} %get-tuple-element.364.refs_0_, s32[4,4,4]{2,1,0:T(4,128)S(1)} %select_reduce_fusion.1.refs_1_, s32[16]{0:T(128)S(1)} %sub.57.refs_2_, bf16[512,768]{1,0:T(8,128)(2,1)} %collective-permute-done.13.refs_3_.refs_9_, ...), custom_call_target="tpu_custom_call" | custom-call | flops 12000000000 | bytes 10485760 | tf_op jit(solution)/shard_map/attend_forward/pallas_call | solution.py:267
  169.6 14.9 %attend_forward.7 = (bf16[2048,384]{1,0:T(8,128)(2,1)S(1)}, bf16[3,64,2048]{2,1,0:T(8,128)(2,1)S(1)}, f32[3,64,2048]{2,1,0:T(8,128)S(1)}, f32[3,1,2048]{2,1,0:T(1,128)S(1)}) custom-call(s32[4,4]{1,0:T(4,128)S(1)} %get-tuple-element.364.refs_0_, s32[4,4,4]{2,1,0:T(4,128)S(1)} %select_reduce_fusion.1.refs_1_, s32[16]{0:T(128)S(1)} %sub.57.refs_2_, ...), custom_call_target="tpu_custom_call" | custom-call | flops 12000000000 | bytes 10485760 | tf_op jit(solution)/shard_map/attend_forward/pallas_call | solution.py:267
  191.2 4.8 %collective-permute-done.34.refs_4_.refs_7_ = bf16[192,512]{1,0:T(8,128)(2,1)S(1)} collective-permute-done((bf16[192,512]{1,0:T(8,128)(2,1)S(1)}, bf16[192,512]{1,0:T(8,128)(2,1)S(1)}, u32[]{:S(2)}, u32[]{:S(2)}) %collective-permute-start.34) | collective-permute-done | bytes 196640 | tf_op jit(solution)/shard_map/ppermute | solution.py:52
  198.9 24.8 %middle.1 = (bf16[512,768]{1,0:T(8,128)(2,1)}, f32[512,768]{1,0:T(8,128)}, bf16[512,768]{1,0:T(8,128)(2,1)}, bf16[512,768]{1,0:T(8,128)(2,1)}, bf16[512,3072]{1,...) custom-call(s32[16]{0:T(128)} %stack.134.refs_0_, ...), custom_call_target="tpu_custom_call" | custom-call | flops 12000000000 | bytes 25165824 | tf_op jit(solution)/shard_map/middle/pallas_call | solution.py:588
  223.7 6.9 %grad_down.1 = (bf16[1536,768]{1,0:T(8,128)(2,1)}, bf16[1536,768]{1,0:T(8,128)(2,1)}) custom-call(s32[1]{0:T(128)} %bitcast.74.core_ref.refs_0_, bf16[512,3072]{1,0:T(8,128)(2,1)} %get-tuple-element.246.hidden_ref, bf16[512,768]{1,0:T(8,128)(2,1)} %cot_ref.1), custom_call_target="tpu_custom_call" | custom-call | flops 3000000000 | bytes 10485760 | tf_op jit(solution)/shard_map/grad_down/pallas_call | solution.py:663
  233.0 9.4 %grad_wide.1 = (bf16[384,3840]{1,0:T(8,128)(2,1)}, bf16[384,3840]{1,0:T(8,128)(2,1)}) custom-call(s32[1]{0:T(128)} %bitcast.74.core_ref.refs_0_, s32[4]{0:T(128)} %copy-done.79, bf16[512,768]{1,0:T(8,128)(2,1)} %get-tuple-element.248.refs_2_, bf16[512,3072]{1,0:T(8,128)(2,1)} %get-tuple-element.249.refs_3_, bf16[512,768]{1,0:T(8,128)(2,1)} %get-tuple-element.250.refs_4_, ...), custom_call_target="tpu_custom_call" | custom-call | flops 4000000000 | bytes 12582912 | tf_op jit(solution)/shard_map/grad_wide/pallas_call | solution.py:686
  248.0 30.9 %attend_backward.4 = (bf16[2,512,768]{2,1,0:T(8,128)(2,1)S(1)}, bf16[2,512,768]{2,1,0:T(8,128)(2,1)}, f32[384,768]{1,0:T(8,128)S(1)}, f32[2048,384]{1,0:T(8,128)S(1)}, f32[8,768]{1,0:T(8,128)S(1)}) custom-call(s32[4,4]{1,0:T(4,128)S(1)} %get-tuple-element.364.refs_0_, s32[4,4,4]{2,1,0:T(4,128)S(1)} %select_reduce_fusion.1.refs_1_, s32[16]{0:T(128)S(1)} %sub.57.refs_2_, ...), custom_call_target="tpu_custom_call" | custom-call | flops 24999999488 | bytes 16777216 | tf_op jit(solution)/shard_map/attend_backward/pallas_call | solution.py:446
  296.0 23.8 %attend_backward.5 = (bf16[2,512,768]{2,1,0:T(8,128)(2,1)S(1)}, bf16[2,512,768]{2,1,0:T(8,128)(2,1)}, f32[384,768]{1,0:T(8,128)S(1)}, f32[2048,384]{1,0:T(8,128)S(1)}, f32[8,768]{1,0:T(8,128)S(1)}) custom-call(s32[4,4]{1,0:T(4,128)S(1)} %get-tuple-element.364.refs_0_, s32[4,4,4]{2,1,0:T(4,128)S(1)} %select_reduce_fusion.1.refs_1_, s32[16]{0:T(128)S(1)} %sub.57.refs_2_, ...), custom_call_target="tpu_custom_call" | custom-call | flops 24999999488 | bytes 16777216 | tf_op jit(solution)/shard_map/attend_backward/pallas_call | solution.py:446
  337.9 4.4 collective-permute-start.54
  342.4 22.4 %attend_backward.6 = (bf16[2,512,768]{2,1,0:T(8,128)(2,1)S(1)}, bf16[2,512,768]{2,1,0:T(8,128)(2,1)S(1)}, f32[384,768]{1,0:T(8,128)S(1)}, f32[2048,384]{1,0:T(8,128)S(1)}, f32[8,768]{1,0:T(8,128)S(1)}) custom-call(s32[4,4]{1,0:T(4,128)S(1)} %get-tuple-element.364.refs_0_, s32[4,4,4]{2,1,0:T(4,128)S(1)} %select_reduce_fusion.1.refs_1_, s32[16]{0:T(128)S(1)} %sub.57.refs_2_, ...), custom_call_target="tpu_custom_call" | custom-call | flops 24999999488 | bytes 16777216 | tf_op jit(solution)/shard_map/attend_backward/pallas_call | solution.py:446
  383.8 32.9 %attend_backward.7 = (bf16[2,512,768]{2,1,0:T(8,128)(2,1)S(1)}, bf16[2,512,768]{2,1,0:T(8,128)(2,1)S(1)}, bf16[768,704]{1,0:T(8,128)(2,1)S(1)}) custom-call(s32[4,4]{1,0:T(4,128)S(1)} %get-tuple-element.364.refs_0_, s32[4,4,4]{2,1,0:T(4,128)S(1)} %select_reduce_fusion.1.refs_1_, s32[16]{0:T(128)S(1)} %sub.57.refs_2_, bf16[2048,384]{1,0:T(8,128)(2,1)S(1)} %copy-done.30, ...), custom_call_target="tpu_custom_call" | custom-call | flops 24999999488 | bytes 16777216 | tf_op jit(solution)/shard_map/attend_backward/pallas_call | solution.py:446
  423.5 11.3 %collective-permute-done.65 = bf16[1,4,4,24,704]{4,3,1,2,0:T(8,128)(2,1)S(1)} collective-permute-done((bf16[1,4,4,24,704]{4,3,1,2,0:T(8,128)(2,1)S(1)}, bf16[1,4,4,24,704]{4,3,1,2,0:T(8,128)(2,1)S(1)}, u32[]{:S(2)}, u32[]{:S(2)}) %collective-permute-start.65) | collective-permute-done | bytes 540704 | tf_op jit(solution)/shard_map/ppermute | solution.py:740
  434.8 6.1 %collective-permute-done.63 = bf16[512,768]{1,0:T(8,128)(2,1)S(1)} collective-permute-done((bf16[512,768]{1,0:T(8,128)(2,1)S(1)}, bf16[512,768]{1,0:T(8,128)(2,1)S(1)}, u32[]{:S(2)}, u32[]{:S(2)}) %collective-permute-start.63) | collective-permute-done | bytes 786464 | tf_op jit(solution)/shard_map/ppermute | solution.py:52
  451.4 4.9 %collective-permute-done.68 = bf16[4,24,704]{2,1,0:T(8,128)(2,1)S(1)} collective-permute-done((bf16[4,24,704]{2,1,0:T(8,128)(2,1)S(1)}, bf16[4,24,704]{2,1,0:T(8,128)(2,1)S(1)}, u32[]{:S(2)}, u32[]{:S(2)}) %collective-permute-start.68) | collective-permute-done | bytes 135200 | tf_op jit(solution)/shard_map/ppermute | solution.py:65
  (428 shorter events, 150.1 us)
Async XLA Ops:
  0.7 44.0 %collective-permute-start = (bf16[512,768]{1,0:T(8,128)(2,1)}, bf16[512,768]{1,0:T(8,128)(2,1)S(1)}, u32[]{:S(2)}, u32[]{:S(2)}) collective-permute-start(bf16[512,768]{1,0:T(8,128)(2,1)} %refs_9_.1), channel_id=1, source_target_pairs={{0,8},{4,12},{8,0},{12,4},{1,9},{5,13},{9,1},{13,5},{2,10},{6,14},... | collective-permute-start | bytes 2359304 | tf_op jit(solution)/shard_map/ppermute | solution.py:52
  3.7 41.0 %collective-permute-start.1 = (bf16[512,768]{1,0:T(8,128)(2,1)}, bf16[512,768]{1,0:T(8,128)(2,1)S(1)}, u32[]{:S(2)}, u32[]{:S(2)}) collective-permute-start(bf16[512,768]{1,0:T(8,128)(2,1)} %refs_9_.1), channel_id=1, source_target_pairs={{0,1},{1,3},{3,2},{2,0},{4,5},{5,7},{7,6},{6,4},{8,9},{9,11},{11,1... | collective-permute-start | bytes 2359304 | tf_op jit(solution)/shard_map/ppermute | solution.py:65
  49.1 31.0 %collective-permute-start.12 = (bf16[512,768]{1,0:T(8,128)(2,1)S(1)}, bf16[512,768]{1,0:T(8,128)(2,1)}, u32[]{:S(2)}, u32[]{:S(2)}) collective-permute-start(bf16[512,768]{1,0:T(8,128)(2,1)S(1)} %collective-permute-done.1.refs_3_.refs_9_), channel_id=1, source_target_pairs={{0,8},{4,12},{8,0},{12,4},{1,9},{5,13},{9,1},{13,5},{2,10},{6,14},... | collective-permute-start | bytes 2359304 | tf_op jit(solution)/shard_map/ppermute | solution.py:52
  50.4 29.7 %collective-permute-start.13 = (bf16[512,768]{1,0:T(8,128)(2,1)S(1)}, bf16[512,768]{1,0:T(8,128)(2,1)}, u32[]{:S(2)}, u32[]{:S(2)}) collective-permute-start(bf16[512,768]{1,0:T(8,128)(2,1)S(1)} %collective-permute-done.1.refs_3_.refs_9_), channel_id=1, source_target_pairs={{0,1},{1,3},{3,2},{2,0},{4,5},{5,7},{7,6},{6,4},{8,9},{9,11},{11,1... | collective-permute-start | bytes 2359304 | tf_op jit(solution)/shard_map/ppermute | solution.py:65
  68.6 31.1 %collective-permute-start.9 = (bf16[512,768]{1,0:T(8,128)(2,1)S(1)}, bf16[512,768]{1,0:T(8,128)(2,1)S(1)}, u32[]{:S(2)}, u32[]{:S(2)}) collective-permute-start(bf16[512,768]{1,0:T(8,128)(2,1)S(1)} %collective-permute-done.1.refs_3_.refs_9_), channel_id=1, source_target_pairs={{0,4},{4,0},{8,12},{12,8},{1,5},{5,1},{9,13},{13,9},{2,6},{6,2},{1... | collective-permute-start | bytes 2359304 | tf_op jit(solution)/shard_map/ppermute | solution.py:52
  109.5 33.4 %collective-permute-start.25 = (bf16[864,768]{1,0:T(8,128)(2,1)S(1)}, bf16[864,768]{1,0:T(8,128)(2,1)S(1)}, u32[]{:S(2)}, u32[]{:S(2)}) collective-permute-start(bf16[864,768]{1,0:T(8,128)(2,1)S(1)} %get-tuple-element.402.refs_9_), channel_id=1, source_target_pairs={{0,16},{16,0},{1,17},{17,1},{2,18},{18,2},{3,19},{19,3},{4,20},{20... | collective-permute-start | bytes 3981320 | tf_op jit(solution)/shard_map/ppermute | solution.py:771
  110.1 56.7 %collective-permute-start.29 = (bf16[864,768]{1,0:T(8,128)(2,1)S(1)}, bf16[864,768]{1,0:T(8,128)(2,1)S(1)}, u32[]{:S(2)}, u32[]{:S(2)}) collective-permute-start(bf16[864,768]{1,0:T(8,128)(2,1)S(1)} %get-tuple-element.402.refs_9_), channel_id=1, source_target_pairs={{0,4},{4,0},{8,12},{12,8},{1,5},{5,1},{9,13},{13,9},{2,6},{6,2},{1... | collective-permute-start | bytes 3981320 | tf_op jit(solution)/shard_map/ppermute | solution.py:52
  110.6 32.3 %collective-permute-start.23 = (bf16[512,768]{1,0:T(8,128)(2,1)S(1)}, bf16[512,768]{1,0:T(8,128)(2,1)S(1)}, u32[]{:S(2)}, u32[]{:S(2)}) collective-permute-start(bf16[512,768]{1,0:T(8,128)(2,1)S(1)} %collective-permute-done.17.refs_3_.refs_9_), channel_id=1, source_target_pairs={{0,8},{4,12},{8,0},{12,4},{1,9},{5,13},{9,1},{13,5},{2,10},{6,14},... | collective-permute-start | bytes 2359304 | tf_op jit(solution)/shard_map/ppermute | solution.py:52
  126.1 28.2 %collective-permute-start.27 = (bf16[432,768]{1,0:T(8,128)(2,1)S(1)}, bf16[432,768]{1,0:T(8,128)(2,1)}, u32[]{:S(2)}, u32[]{:S(2)}) collective-permute-start(bf16[432,768]{1,0:T(8,128)(2,1)S(1)} %get-tuple-element.401), channel_id=1, source_target_pairs={{0,8},{4,12},{8,0},{12,4},{1,9},{5,13},{9,1},{13,5},{2,10},{6,14},... | collective-permute-start | bytes 1990664 | tf_op jit(solution)/shard_map/ppermute | solution.py:52
  137.8 28.5 %collective-permute-start.20 = (bf16[512,768]{1,0:T(8,128)(2,1)S(1)}, bf16[512,768]{1,0:T(8,128)(2,1)S(1)}, u32[]{:S(2)}, u32[]{:S(2)}) collective-permute-start(bf16[512,768]{1,0:T(8,128)(2,1)S(1)} %collective-permute-done.17.refs_3_.refs_9_), channel_id=1, source_target_pairs={{0,4},{4,0},{8,12},{12,8},{1,5},{5,1},{9,13},{13,9},{2,6},{6,2},{1... | collective-permute-start | bytes 2359304 | tf_op jit(solution)/shard_map/ppermute | solution.py:52
  154.3 32.0 %collective-permute-start.31 = (bf16[864,768]{1,0:T(8,128)(2,1)S(1)}, bf16[864,768]{1,0:T(8,128)(2,1)S(1)}, u32[]{:S(2)}, u32[]{:S(2)}) collective-permute-start(bf16[864,768]{1,0:T(8,128)(2,1)S(1)} %collective-permute-done.25.refs_10_), channel_id=1, source_target_pairs={{0,4},{4,0},{8,12},{12,8},{1,5},{5,1},{9,13},{13,9},{2,6},{6,2},{1... | collective-permute-start | bytes 3981320 | tf_op jit(solution)/shard_map/ppermute | solution.py:52
  243.2 40.1 %collective-permute-start.44 = (bf16[2,2,4,24,3840]{4,3,2,1,0:T(8,128)(2,1)}, bf16[2,2,4,24,3840]{4,3,2,1,0:T(8,128)(2,1)}, u32[]{:S(2)}, u32[]{:S(2)}) collective-permute-start(bf16[2,2,4,24,3840]{4,3,2,1,0:T(8,128)(2,1)} %bitcast.230), channel_id=1, source_target_pairs={{0,4},{4,0},{8,12},{12,8},{1,5},{5,1},{9,13},{13,9},{2,6},{6,2},{1... | collective-permute-start | bytes 8847368 | tf_op jit(solution)/shard_map/ppermute | solution.py:52
  244.4 37.8 %collective-permute-start.43 = (bf16[1,2,4,96,768]{4,3,2,1,0:T(8,128)(2,1)S(1)}, bf16[1,2,4,96,768]{4,3,2,1,0:T(8,128)(2,1)S(1)}, u32[]{:S(2)}, u32[]{:S(2)}) collective-permute-start(bf16[1,2,4,96,768]{4,3,2,1,0:T(8,128)(2,1)S(1)} %constant_dynamic-slice_fusion.7), channel_id=1, source_target_pairs={{0,16},{16,0},{1,17},{17,1},{2,18},{18,2},{3,19},{19,3},{4,20},{20... | collective-permute-start | bytes 3538952 | tf_op jit(solution)/shard_map/ppermute | solution.py:740
  293.0 34.5 %collective-permute-start.48 = (bf16[1,2,4,24,3840]{4,3,2,1,0:T(8,128)(2,1)S(1)}, bf16[1,2,4,24,3840]{4,3,2,1,0:T(8,128)(2,1)S(1)}, u32[]{:S(2)}, u32[]{:S(2)}) collective-permute-start(bf16[1,2,4,24,3840]{4,3,2,1,0:T(8,128)(2,1)S(1)} %constant_dynamic-slice_fusion.6), channel_id=1, source_target_pairs={{0,16},{16,0},{1,17},{17,1},{2,18},{18,2},{3,19},{19,3},{4,20},{20... | collective-permute-start | bytes 4423688 | tf_op jit(solution)/shard_map/ppermute | solution.py:740
  293.8 29.3 %collective-permute-start.47 = (bf16[4,96,768]{2,1,0:T(8,128)(2,1)S(1)}, bf16[4,96,768]{2,1,0:T(8,128)(2,1)S(1)}, u32[]{:S(2)}, u32[]{:S(2)}) collective-permute-start(bf16[4,96,768]{2,1,0:T(8,128)(2,1)S(1)} %dynamic-slice_bitcast_fusion.1), channel_id=1, source_target_pairs={{0,8},{4,12},{8,0},{12,4},{1,9},{5,13},{9,1},{13,5},{2,10},{6,14},... | collective-permute-start | bytes 1769480 | tf_op jit(solution)/shard_map/ppermute | solution.py:52
  295.1 30.9 %collective-permute-start.46 = (bf16[512,768]{1,0:T(8,128)(2,1)S(1)}, bf16[512,768]{1,0:T(8,128)(2,1)S(1)}, u32[]{:S(2)}, u32[]{:S(2)}) collective-permute-start(bf16[512,768]{1,0:T(8,128)(2,1)S(1)} %get-tuple-element.290), channel_id=1, source_target_pairs={{0,8},{4,12},{8,0},{12,4},{1,9},{5,13},{9,1},{13,5},{2,10},{6,14},... | collective-permute-start | bytes 2359304 | tf_op jit(solution)/shard_map/ppermute | solution.py:52
  335.8 32.1 %collective-permute-start.52 = (bf16[4,24,3840]{2,1,0:T(8,128)(2,1)S(1)}, bf16[4,24,3840]{2,1,0:T(8,128)(2,1)S(1)}, u32[]{:S(2)}, u32[]{:S(2)}) collective-permute-start(bf16[4,24,3840]{2,1,0:T(8,128)(2,1)S(1)} %dynamic-slice_bitcast_fusion), channel_id=1, source_target_pairs={{0,8},{4,12},{8,0},{12,4},{1,9},{5,13},{9,1},{13,5},{2,10},{6,14},... | collective-permute-start | bytes 2211848 | tf_op jit(solution)/shard_map/ppermute | solution.py:52
  337.1 34.5 %collective-permute-start.50 = (bf16[512,768]{1,0:T(8,128)(2,1)S(1)}, bf16[512,768]{1,0:T(8,128)(2,1)S(1)}, u32[]{:S(2)}, u32[]{:S(2)}) collective-permute-start(bf16[512,768]{1,0:T(8,128)(2,1)S(1)} %get-tuple-element.312), channel_id=1, source_target_pairs={{0,8},{4,12},{8,0},{12,4},{1,9},{5,13},{9,1},{13,5},{2,10},{6,14},... | collective-permute-start | bytes 2359304 | tf_op jit(solution)/shard_map/ppermute | solution.py:52
  337.9 33.7 %collective-permute-start.51 = (bf16[512,768]{1,0:T(8,128)(2,1)S(1)}, bf16[512,768]{1,0:T(8,128)(2,1)S(1)}, u32[]{:S(2)}, u32[]{:S(2)}) collective-permute-start(bf16[512,768]{1,0:T(8,128)(2,1)S(1)} %add_convert_fusion.8), channel_id=1, source_target_pairs={{0,2},{1,0},{3,1},{2,3},{4,6},{5,4},{7,5},{6,7},{8,10},{9,8},{11,9... | collective-permute-start | bytes 2359304 | tf_op jit(solution)/shard_map/ppermute | solution.py:65
  375.4 41.3 %collective-permute-start.59 = (bf16[24,3840]{1,0:T(8,128)(2,1)S(1)}, bf16[24,3840]{1,0:T(8,128)(2,1)S(1)}, u32[]{:S(2)}, u32[]{:S(2)}) collective-permute-start(bf16[24,3840]{1,0:T(8,128)(2,1)S(1)} %get-tuple-element.394), channel_id=1, source_target_pairs={{0,2},{1,0},{3,1},{2,3},{4,6},{5,4},{7,5},{6,7},{8,10},{9,8},{11,9... | collective-permute-start | bytes 552968 | tf_op jit(solution)/shard_map/ppermute | solution.py:65
  375.5 41.2 %collective-permute-start.60 = (bf16[24,3840]{1,0:T(8,128)(2,1)S(1)}, bf16[24,3840]{1,0:T(8,128)(2,1)S(1)}, u32[]{:S(2)}, u32[]{:S(2)}) collective-permute-start(bf16[24,3840]{1,0:T(8,128)(2,1)S(1)} %get-tuple-element.393), channel_id=1, source_target_pairs={{0,3},{1,2},{3,0},{2,1},{4,7},{5,6},{7,4},{6,5},{8,11},{9,10},{11,... | collective-permute-start | bytes 552968 | tf_op jit(solution)/shard_map/ppermute | solution.py:65
  379.7 37.1 %collective-permute-start.61 = (bf16[24,3840]{1,0:T(8,128)(2,1)S(1)}, bf16[24,3840]{1,0:T(8,128)(2,1)S(1)}, u32[]{:S(2)}, u32[]{:S(2)}) collective-permute-start(bf16[24,3840]{1,0:T(8,128)(2,1)S(1)} %get-tuple-element.392), channel_id=1, source_target_pairs={{0,1},{1,3},{3,2},{2,0},{4,5},{5,7},{7,6},{6,4},{8,9},{9,11},{11,1... | collective-permute-start | bytes 552968 | tf_op jit(solution)/shard_map/ppermute | solution.py:65
  379.7 37.1 %collective-permute-start.57 = (bf16[512,768]{1,0:T(8,128)(2,1)S(1)}, bf16[512,768]{1,0:T(8,128)(2,1)S(1)}, u32[]{:S(2)}, u32[]{:S(2)}) collective-permute-start(bf16[512,768]{1,0:T(8,128)(2,1)S(1)} %get-tuple-element.332), channel_id=1, source_target_pairs={{0,8},{4,12},{8,0},{12,4},{1,9},{5,13},{9,1},{13,5},{2,10},{6,14},... | collective-permute-start | bytes 2359304 | tf_op jit(solution)/shard_map/ppermute | solution.py:52
  380.9 35.9 %collective-permute-start.58 = (bf16[512,768]{1,0:T(8,128)(2,1)S(1)}, bf16[512,768]{1,0:T(8,128)(2,1)S(1)}, u32[]{:S(2)}, u32[]{:S(2)}) collective-permute-start(bf16[512,768]{1,0:T(8,128)(2,1)S(1)} %add_convert_fusion.5), channel_id=1, source_target_pairs={{0,2},{1,0},{3,1},{2,3},{4,6},{5,4},{7,5},{6,7},{8,10},{9,8},{11,9... | collective-permute-start | bytes 2359304 | tf_op jit(solution)/shard_map/ppermute | solution.py:65
  (136 other events, 1776.6 us)

commit v7 on v6

--- a/solution.py
+++ b/solution.py
@@ -270,7 +270,7 @@
         in_specs=in_specs,
         out_specs=(vmem,) * len(outs),
         scratch_shapes=scratch,
-        compiler_params=pltpu.CompilerParams(vmem_limit_bytes=40 << 20),
+        compiler_params=pltpu.CompilerParams(vmem_limit_bytes=34 << 20),
         cost_estimate=pl.CostEstimate(
             flops=12 * 1000 * 1000 * 1000, bytes_accessed=10 << 20, transcendentals=7 << 20
         ),
@@ -460,7 +460,7 @@
             pltpu.SemaphoreType.DMA((5,)),
         ]
         + [pltpu.VMEM(k.shape, k.dtype) for k in kept],
-        compiler_params=pltpu.CompilerParams(vmem_limit_bytes=34 << 20),
+        compiler_params=pltpu.CompilerParams(vmem_limit_bytes=32 << 20),
         cost_estimate=pl.CostEstimate(
             flops=25 * 1000 * 1000 * 1000, bytes_accessed=16 << 20, transcendentals=7 << 20
         ),
@@ -605,7 +605,7 @@
             pltpu.VMEM((4 * D, D), BF16),
             pltpu.SemaphoreType.DMA((6, number)),
         ],
-        compiler_params=pltpu.CompilerParams(vmem_limit_bytes=58 << 20),
+        compiler_params=pltpu.CompilerParams(vmem_limit_bytes=59 << 20),
         cost_estimate=pl.CostEstimate(
             flops=12 * 1000 * 1000 * 1000, bytes_accessed=24 << 20, transcendentals=3 << 20
         ),
@@ -670,7 +670,7 @@
             pl.BlockSpec((rows, D), lambda j: (0, 0)),
         ],
         out_specs=(half, half),
-        compiler_params=pltpu.CompilerParams(vmem_limit_bytes=54 << 20),
+        compiler_params=pltpu.CompilerParams(vmem_limit_bytes=56 << 20),
         cost_estimate=pl.CostEstimate(
             flops=3 * 10**9, bytes_accessed=10 << 20, transcendentals=0
         ),
@@ -691,7 +691,7 @@
         + [pl.BlockSpec((rows, D), lambda j: (0, jnp.minimum(j, 3))), whole]
         + [pl.BlockSpec((D // 4, rows), lambda j: (0, 0))] * 4,
         out_specs=(half, half),
-        compiler_params=pltpu.CompilerParams(vmem_limit_bytes=54 << 20),
+        compiler_params=pltpu.CompilerParams(vmem_limit_bytes=56 << 20),
         cost_estimate=pl.CostEstimate(
             flops=4 * 10**9, bytes_accessed=12 << 20, transcendentals=0
         ),

time: 471 us -> 468 us (level)
    unnamed x195 -> x205, local copies, waits for them, and re-layouts: 18.7 us -> 17.6 us
  transfers between devices with their start and end apart: 72 -> 72, of which waited for: 26 -> 27; matrix products, arithmetic and copies ran while one was open for 9% -> 9% of each run, Pallas kernels for 37% -> 37%
where the time goes in v7:
time: 468 us; the launch traced here: 460 us
  Pallas kernels  201 us (43%)
  waiting for transfers between devices  122 us (26%)
  starting transfers between devices  59.7 us (13%)
  local copies, waits for them, and re-layouts  35.4 us (8%)
  other arithmetic  30.6 us (7%)
  between operations  11 us (2%)
    pallas_call x4, Pallas kernels, attend_backward(): pl.pallas_call(partial(backward_kernel, plane, len(carry) > 1, last), out...  109 us
    ppermute x44, waiting for transfers between devices, swap_head(): return lax.ppermute(value, 'head', [(i, i ^ mask) for i in range(count)])  61.2 us
    pallas_call x4, Pallas kernels, attend_forward(): pl.pallas_call(partial(forward_kernel, plane, last), out_shape=tuple(outs...  51.2 us
    ppermute x21, waiting for transfers between devices, ring_send(): return lax.ppermute(value, 'ctx', ring_pairs(lax.axis_size('ctx'), step))  41.4 us
    ppermute x21, starting transfers between devices, ring_send(): return lax.ppermute(value, 'ctx', ring_pairs(lax.axis_size('ctx'), step))  27.3 us
    ppermute x44, starting transfers between devices, swap_head(): return lax.ppermute(value, 'head', [(i, i ^ mask) for i in range(count)])  26 us
    pallas_call x1, Pallas kernels, middle(): pl.pallas_call(partial(middle_kernel, len(pieces), pair, shard), out_shap...  24.9 us
    unnamed x205, local copies, waits for them, and re-layouts  17.6 us
  transfers between devices with their start and end apart: 72, of which 27 were waited for; matrix products, arithmetic and copies ran while one was open for 9% of the time, Pallas kernels for 37%

profile of v7, /device:TPU:0, one launch (start us, length us, event | category | flops | bytes accessed | tf_op | source)
XLA Modules:
  0.0 459.7 jit_solution(8522569433976836527)
XLA Ops:
  16.5 6.1 %collective-permute-done.3 = bf16[24,768]{1,0:T(8,128)(2,1)S(1)} collective-permute-done((bf16[24,768]{1,0:T(8,128)(2,1)S(1)}, bf16[24,768]{1,0:T(8,128)(2,1)S(1)}, u32[]{:S(2)}, u32[]{:S(2)}) %collective-permute-start.3) | collective-permute-done | bytes 36896 | tf_op jit(solution)/shard_map/ppermute | solution.py:52
  37.7 6.5 %collective-permute-done.7 = bf16[4,24,768]{2,1,0:T(8,128)(2,1)S(1)} collective-permute-done((bf16[4,24,768]{2,1,0:T(8,128)(2,1)S(1)}, bf16[4,24,768]{2,1,0:T(8,128)(2,1)S(1)}, u32[]{:S(2)}, u32[]{:S(2)}) %collective-permute-start.7) | collective-permute-done | bytes 147488 | tf_op jit(solution)/shard_map/ppermute | solution.py:65
  55.3 6.0 %collective-permute-done.19 = bf16[1,1,4,4,24,768]{5,4,2,3,0,1:T(8,128)(2,1)S(1)} collective-permute-done((bf16[1,1,4,4,24,768]{5,4,2,3,0,1:T(8,128)(2,1)S(1)}, bf16[1,1,4,4,24,768]{5,4,2,3,0,1:T(8,128)(2,1)S(1)}, u32[]{:S(2)}, u32[]{:S(2)}) %collective-permute-start.19) | collective-permute-done | bytes 589856 | tf_op jit(solution)/shard_map/ppermute | solution.py:764
  69.2 10.9 %collective-permute-done.14 = bf16[216,768]{1,0:T(8,128)(2,1)} collective-permute-done((bf16[216,768]{1,0:T(8,128)(2,1)}, bf16[216,768]{1,0:T(8,128)(2,1)}, u32[]{:S(2)}, u32[]{:S(2)}) %collective-permute-start.14) | collective-permute-done | bytes 331808 | tf_op jit(solution)/shard_map/ppermute | solution.py:65
  82.5 15.9 %attend_forward.4 = (bf16[2048,384]{1,0:T(8,128)(2,1)S(1)}, bf16[2048,384]{1,0:T(8,128)(2,1)S(1)}, f32[3,80,2048]{2,1,0:T(8,128)S(1)}) custom-call(s32[4,4]{1,0:T(4,128)S(1)} %get-tuple-element.364.refs_0_, s32[4,4,4]{2,1,0:T(4,128)S(1)} %select_reduce_fusion.1.refs_1_, s32[16]{0:T(128)S(1)} %sub.57.refs_2_, bf16[512,768]{1,0:T(8,128)(2,1)S(1)} %copy-done, ...), custom_call_target="tpu_custom_call" | custom-call | flops 12000000000 | bytes 10485760 | tf_op jit(solution)/shard_map/attend_forward/pallas_call | solution.py:267
  100.0 7.8 %collective-permute-done.18 = bf16[216,768]{1,0:T(8,128)(2,1)S(1)} collective-permute-done((bf16[216,768]{1,0:T(8,128)(2,1)}, bf16[216,768]{1,0:T(8,128)(2,1)S(1)}, u32[]{:S(2)}, u32[]{:S(2)}) %collective-permute-start.18) | collective-permute-done | bytes 331808 | tf_op jit(solution)/shard_map/ppermute | solution.py:65
  111.4 14.6 %collective-permute-done.24.refs_11_ = bf16[432,768]{1,0:T(8,128)(2,1)S(1)} collective-permute-done((bf16[432,768]{1,0:T(8,128)(2,1)S(1)}, bf16[432,768]{1,0:T(8,128)(2,1)S(1)}, u32[]{:S(2)}, u32[]{:S(2)}) %collective-permute-start.24) | collective-permute-done | bytes 663584 | tf_op jit(solution)/shard_map/ppermute | solution.py:52
  127.2 10.4 %attend_forward.5 = (bf16[2048,384]{1,0:T(8,128)(2,1)S(1)}, f32[3,80,2048]{2,1,0:T(8,128)S(1)}) custom-call(s32[4,4]{1,0:T(4,128)S(1)} %get-tuple-element.364.refs_0_, s32[4,4,4]{2,1,0:T(4,128)S(1)} %select_reduce_fusion.1.refs_1_, s32[16]{0:T(128)S(1)} %sub.57.refs_2_, bf16[512,768]{1,0:T(8,128)(2,1)S(1)} %collective-permute-done.1.refs_3_.refs_9_, ...), custom_call_target="tpu_custom_call" | custom-call | flops 12000000000 | bytes 10485760 | tf_op jit(solution)/shard_map/attend_forward/pallas_call | solution.py:267
  137.7 5.1 %collective-permute-done.23.refs_5_.refs_11_ = bf16[512,768]{1,0:T(8,128)(2,1)S(1)} collective-permute-done((bf16[512,768]{1,0:T(8,128)(2,1)S(1)}, bf16[512,768]{1,0:T(8,128)(2,1)S(1)}, u32[]{:S(2)}, u32[]{:S(2)}) %collective-permute-start.23) | collective-permute-done | bytes 786464 | tf_op jit(solution)/shard_map/ppermute | solution.py:52
  143.5 10.7 %collective-permute-done.27.refs_12_ = bf16[432,768]{1,0:T(8,128)(2,1)S(1)} collective-permute-done((bf16[432,768]{1,0:T(8,128)(2,1)S(1)}, bf16[432,768]{1,0:T(8,128)(2,1)S(1)}, u32[]{:S(2)}, u32[]{:S(2)}) %collective-permute-start.27) | collective-permute-done | bytes 663584 | tf_op jit(solution)/shard_map/ppermute | solution.py:52
  154.3 10.8 %attend_forward.6 = (bf16[2048,384]{1,0:T(8,128)(2,1)S(1)}, f32[3,80,2048]{2,1,0:T(8,128)S(1)}) custom-call(s32[4,4]{1,0:T(4,128)S(1)} %get-tuple-element.364.refs_0_, s32[4,4,4]{2,1,0:T(4,128)S(1)} %select_reduce_fusion.1.refs_1_, s32[16]{0:T(128)S(1)} %sub.57.refs_2_, bf16[512,768]{1,0:T(8,128)(2,1)} %collective-permute-done.13.refs_3_.refs_9_, ...), custom_call_target="tpu_custom_call" | custom-call | flops 12000000000 | bytes 10485760 | tf_op jit(solution)/shard_map/attend_forward/pallas_call | solution.py:267
  167.4 14.1 %attend_forward.7 = (bf16[2048,384]{1,0:T(8,128)(2,1)S(1)}, bf16[3,64,2048]{2,1,0:T(8,128)(2,1)S(1)}, f32[3,64,2048]{2,1,0:T(8,128)S(1)}, f32[3,1,2048]{2,1,0:T(1,128)S(1)}) custom-call(s32[4,4]{1,0:T(4,128)S(1)} %get-tuple-element.364.refs_0_, s32[4,4,4]{2,1,0:T(4,128)S(1)} %select_reduce_fusion.1.refs_1_, s32[16]{0:T(128)S(1)} %sub.57.refs_2_, ...), custom_call_target="tpu_custom_call" | custom-call | flops 12000000000 | bytes 10485760 | tf_op jit(solution)/shard_map/attend_forward/pallas_call | solution.py:267
  188.2 4.7 %collective-permute-done.34.refs_4_.refs_7_ = bf16[192,512]{1,0:T(8,128)(2,1)S(1)} collective-permute-done((bf16[192,512]{1,0:T(8,128)(2,1)S(1)}, bf16[192,512]{1,0:T(8,128)(2,1)S(1)}, u32[]{:S(2)}, u32[]{:S(2)}) %collective-permute-start.34) | collective-permute-done | bytes 196640 | tf_op jit(solution)/shard_map/ppermute | solution.py:52
  195.9 24.9 %middle.1 = (bf16[512,768]{1,0:T(8,128)(2,1)}, f32[512,768]{1,0:T(8,128)}, bf16[512,768]{1,0:T(8,128)(2,1)}, bf16[512,768]{1,0:T(8,128)(2,1)}, bf16[512,3072]{1,...) custom-call(s32[16]{0:T(128)} %stack.134.refs_0_, ...), custom_call_target="tpu_custom_call" | custom-call | flops 12000000000 | bytes 25165824 | tf_op jit(solution)/shard_map/middle/pallas_call | solution.py:588
  220.8 6.9 %grad_down.1 = (bf16[1536,768]{1,0:T(8,128)(2,1)}, bf16[1536,768]{1,0:T(8,128)(2,1)}) custom-call(s32[1]{0:T(128)} %bitcast.74.core_ref.refs_0_, bf16[512,3072]{1,0:T(8,128)(2,1)} %get-tuple-element.246.hidden_ref, bf16[512,768]{1,0:T(8,128)(2,1)} %cot_ref.1), custom_call_target="tpu_custom_call" | custom-call | flops 3000000000 | bytes 10485760 | tf_op jit(solution)/shard_map/grad_down/pallas_call | solution.py:663
  230.1 9.4 %grad_wide.1 = (bf16[384,3840]{1,0:T(8,128)(2,1)}, bf16[384,3840]{1,0:T(8,128)(2,1)}) custom-call(s32[1]{0:T(128)} %bitcast.74.core_ref.refs_0_, s32[4]{0:T(128)} %copy-done.82, bf16[512,768]{1,0:T(8,128)(2,1)} %get-tuple-element.248.refs_2_, bf16[512,3072]{1,0:T(8,128)(2,1)} %get-tuple-element.249.refs_3_, bf16[512,768]{1,0:T(8,128)(2,1)} %get-tuple-element.250.refs_4_, ...), custom_call_target="tpu_custom_call" | custom-call | flops 4000000000 | bytes 12582912 | tf_op jit(solution)/shard_map/grad_wide/pallas_call | solution.py:686
  245.1 30.9 %attend_backward.4 = (bf16[2,512,768]{2,1,0:T(8,128)(2,1)S(1)}, bf16[2,512,768]{2,1,0:T(8,128)(2,1)}, f32[384,768]{1,0:T(8,128)S(1)}, f32[2048,384]{1,0:T(8,128)S(1)}, f32[8,768]{1,0:T(8,128)S(1)}) custom-call(s32[4,4]{1,0:T(4,128)S(1)} %get-tuple-element.364.refs_0_, s32[4,4,4]{2,1,0:T(4,128)S(1)} %select_reduce_fusion.1.refs_1_, s32[16]{0:T(128)S(1)} %sub.57.refs_2_, ...), custom_call_target="tpu_custom_call" | custom-call | flops 24999999488 | bytes 16777216 | tf_op jit(solution)/shard_map/attend_backward/pallas_call | solution.py:446
  293.0 23.2 %attend_backward.5 = (bf16[2,512,768]{2,1,0:T(8,128)(2,1)S(1)}, bf16[2,512,768]{2,1,0:T(8,128)(2,1)}, f32[384,768]{1,0:T(8,128)S(1)}, f32[2048,384]{1,0:T(8,128)S(1)}, f32[8,768]{1,0:T(8,128)S(1)}) custom-call(s32[4,4]{1,0:T(4,128)S(1)} %get-tuple-element.364.refs_0_, s32[4,4,4]{2,1,0:T(4,128)S(1)} %select_reduce_fusion.1.refs_1_, s32[16]{0:T(128)S(1)} %sub.57.refs_2_, ...), custom_call_target="tpu_custom_call" | custom-call | flops 24999999488 | bytes 16777216 | tf_op jit(solution)/shard_map/attend_backward/pallas_call | solution.py:446
  335.0 4.4 collective-permute-start.54
  339.6 21.7 %attend_backward.6 = (bf16[2,512,768]{2,1,0:T(8,128)(2,1)S(1)}, bf16[2,512,768]{2,1,0:T(8,128)(2,1)S(1)}, f32[384,768]{1,0:T(8,128)S(1)}, f32[2048,384]{1,0:T(8,128)S(1)}, f32[8,768]{1,0:T(8,128)S(1)}) custom-call(s32[4,4]{1,0:T(4,128)S(1)} %get-tuple-element.364.refs_0_, s32[4,4,4]{2,1,0:T(4,128)S(1)} %select_reduce_fusion.1.refs_1_, s32[16]{0:T(128)S(1)} %sub.57.refs_2_, ...), custom_call_target="tpu_custom_call" | custom-call | flops 24999999488 | bytes 16777216 | tf_op jit(solution)/shard_map/attend_backward/pallas_call | solution.py:446
  380.9 32.9 %attend_backward.7 = (bf16[2,512,768]{2,1,0:T(8,128)(2,1)S(1)}, bf16[2,512,768]{2,1,0:T(8,128)(2,1)S(1)}, bf16[768,704]{1,0:T(8,128)(2,1)S(1)}) custom-call(s32[4,4]{1,0:T(4,128)S(1)} %get-tuple-element.364.refs_0_, s32[4,4,4]{2,1,0:T(4,128)S(1)} %select_reduce_fusion.1.refs_1_, s32[16]{0:T(128)S(1)} %sub.57.refs_2_, bf16[2048,384]{1,0:T(8,128)(2,1)S(1)} %copy-done.29, ...), custom_call_target="tpu_custom_call" | custom-call | flops 24999999488 | bytes 16777216 | tf_op jit(solution)/shard_map/attend_backward/pallas_call | solution.py:446
  420.0 11.8 %collective-permute-done.65 = bf16[1,4,4,24,704]{4,3,1,2,0:T(8,128)(2,1)S(1)} collective-permute-done((bf16[1,4,4,24,704]{4,3,1,2,0:T(8,128)(2,1)S(1)}, bf16[1,4,4,24,704]{4,3,1,2,0:T(8,128)(2,1)S(1)}, u32[]{:S(2)}, u32[]{:S(2)}) %collective-permute-start.65) | collective-permute-done | bytes 540704 | tf_op jit(solution)/shard_map/ppermute | solution.py:740
  431.9 5.5 %collective-permute-done.63 = bf16[512,768]{1,0:T(8,128)(2,1)S(1)} collective-permute-done((bf16[512,768]{1,0:T(8,128)(2,1)S(1)}, bf16[512,768]{1,0:T(8,128)(2,1)S(1)}, u32[]{:S(2)}, u32[]{:S(2)}) %collective-permute-start.63) | collective-permute-done | bytes 786464 | tf_op jit(solution)/shard_map/ppermute | solution.py:52
  447.9 4.8 %collective-permute-done.68 = bf16[4,24,704]{2,1,0:T(8,128)(2,1)S(1)} collective-permute-done((bf16[4,24,704]{2,1,0:T(8,128)(2,1)S(1)}, bf16[4,24,704]{2,1,0:T(8,128)(2,1)S(1)}, u32[]{:S(2)}, u32[]{:S(2)}) %collective-permute-start.68) | collective-permute-done | bytes 135200 | tf_op jit(solution)/shard_map/ppermute | solution.py:65
  (438 shorter events, 148.7 us)
Async XLA Ops:
  0.7 44.0 %collective-permute-start = (bf16[512,768]{1,0:T(8,128)(2,1)}, bf16[512,768]{1,0:T(8,128)(2,1)S(1)}, u32[]{:S(2)}, u32[]{:S(2)}) collective-permute-start(bf16[512,768]{1,0:T(8,128)(2,1)} %refs_9_.1), channel_id=1, source_target_pairs={{0,8},{4,12},{8,0},{12,4},{1,9},{5,13},{9,1},{13,5},{2,10},{6,14},... | collective-permute-start | bytes 2359304 | tf_op jit(solution)/shard_map/ppermute | solution.py:52
  3.7 41.0 %collective-permute-start.1 = (bf16[512,768]{1,0:T(8,128)(2,1)}, bf16[512,768]{1,0:T(8,128)(2,1)S(1)}, u32[]{:S(2)}, u32[]{:S(2)}) collective-permute-start(bf16[512,768]{1,0:T(8,128)(2,1)} %refs_9_.1), channel_id=1, source_target_pairs={{0,1},{1,3},{3,2},{2,0},{4,5},{5,7},{7,6},{6,4},{8,9},{9,11},{11,1... | collective-permute-start | bytes 2359304 | tf_op jit(solution)/shard_map/ppermute | solution.py:65
  49.1 31.0 %collective-permute-start.12 = (bf16[512,768]{1,0:T(8,128)(2,1)S(1)}, bf16[512,768]{1,0:T(8,128)(2,1)}, u32[]{:S(2)}, u32[]{:S(2)}) collective-permute-start(bf16[512,768]{1,0:T(8,128)(2,1)S(1)} %collective-permute-done.1.refs_3_.refs_9_), channel_id=1, source_target_pairs={{0,8},{4,12},{8,0},{12,4},{1,9},{5,13},{9,1},{13,5},{2,10},{6,14},... | collective-permute-start | bytes 2359304 | tf_op jit(solution)/shard_map/ppermute | solution.py:52
  50.4 29.7 %collective-permute-start.13 = (bf16[512,768]{1,0:T(8,128)(2,1)S(1)}, bf16[512,768]{1,0:T(8,128)(2,1)}, u32[]{:S(2)}, u32[]{:S(2)}) collective-permute-start(bf16[512,768]{1,0:T(8,128)(2,1)S(1)} %collective-permute-done.1.refs_3_.refs_9_), channel_id=1, source_target_pairs={{0,1},{1,3},{3,2},{2,0},{4,5},{5,7},{7,6},{6,4},{8,9},{9,11},{11,1... | collective-permute-start | bytes 2359304 | tf_op jit(solution)/shard_map/ppermute | solution.py:65
  68.6 31.1 %collective-permute-start.9 = (bf16[512,768]{1,0:T(8,128)(2,1)S(1)}, bf16[512,768]{1,0:T(8,128)(2,1)S(1)}, u32[]{:S(2)}, u32[]{:S(2)}) collective-permute-start(bf16[512,768]{1,0:T(8,128)(2,1)S(1)} %collective-permute-done.1.refs_3_.refs_9_), channel_id=1, source_target_pairs={{0,4},{4,0},{8,12},{12,8},{1,5},{5,1},{9,13},{13,9},{2,6},{6,2},{1... | collective-permute-start | bytes 2359304 | tf_op jit(solution)/shard_map/ppermute | solution.py:52
  80.1 27.7 %collective-permute-start.16 = (bf16[512,768]{1,0:T(8,128)(2,1)}, bf16[512,768]{1,0:T(8,128)(2,1)S(1)}, u32[]{:S(2)}, u32[]{:S(2)}) collective-permute-start(bf16[512,768]{1,0:T(8,128)(2,1)} %collective-permute-done.13.refs_3_.refs_9_), channel_id=1, source_target_pairs={{0,8},{4,12},{8,0},{12,4},{1,9},{5,13},{9,1},{13,5},{2,10},{6,14},... | collective-permute-start | bytes 2359304 | tf_op jit(solution)/shard_map/ppermute | solution.py:52
  109.5 33.4 %collective-permute-start.25 = (bf16[864,768]{1,0:T(8,128)(2,1)S(1)}, bf16[864,768]{1,0:T(8,128)(2,1)S(1)}, u32[]{:S(2)}, u32[]{:S(2)}) collective-permute-start(bf16[864,768]{1,0:T(8,128)(2,1)S(1)} %get-tuple-element.402.refs_9_), channel_id=1, source_target_pairs={{0,16},{16,0},{1,17},{17,1},{2,18},{18,2},{3,19},{19,3},{4,20},{20... | collective-permute-start | bytes 3981320 | tf_op jit(solution)/shard_map/ppermute | solution.py:771
  110.1 55.4 %collective-permute-start.29 = (bf16[864,768]{1,0:T(8,128)(2,1)S(1)}, bf16[864,768]{1,0:T(8,128)(2,1)S(1)}, u32[]{:S(2)}, u32[]{:S(2)}) collective-permute-start(bf16[864,768]{1,0:T(8,128)(2,1)S(1)} %get-tuple-element.402.refs_9_), channel_id=1, source_target_pairs={{0,4},{4,0},{8,12},{12,8},{1,5},{5,1},{9,13},{13,9},{2,6},{6,2},{1... | collective-permute-start | bytes 3981320 | tf_op jit(solution)/shard_map/ppermute | solution.py:52
  110.6 32.3 %collective-permute-start.23 = (bf16[512,768]{1,0:T(8,128)(2,1)S(1)}, bf16[512,768]{1,0:T(8,128)(2,1)S(1)}, u32[]{:S(2)}, u32[]{:S(2)}) collective-permute-start(bf16[512,768]{1,0:T(8,128)(2,1)S(1)} %collective-permute-done.17.refs_3_.refs_9_), channel_id=1, source_target_pairs={{0,8},{4,12},{8,0},{12,4},{1,9},{5,13},{9,1},{13,5},{2,10},{6,14},... | collective-permute-start | bytes 2359304 | tf_op jit(solution)/shard_map/ppermute | solution.py:52
  126.0 28.2 %collective-permute-start.27 = (bf16[432,768]{1,0:T(8,128)(2,1)S(1)}, bf16[432,768]{1,0:T(8,128)(2,1)S(1)}, u32[]{:S(2)}, u32[]{:S(2)}) collective-permute-start(bf16[432,768]{1,0:T(8,128)(2,1)S(1)} %get-tuple-element.401), channel_id=1, source_target_pairs={{0,8},{4,12},{8,0},{12,4},{1,9},{5,13},{9,1},{13,5},{2,10},{6,14},... | collective-permute-start | bytes 1990664 | tf_op jit(solution)/shard_map/ppermute | solution.py:52
  154.2 29.1 %collective-permute-start.31 = (bf16[864,768]{1,0:T(8,128)(2,1)S(1)}, bf16[864,768]{1,0:T(8,128)(2,1)S(1)}, u32[]{:S(2)}, u32[]{:S(2)}) collective-permute-start(bf16[864,768]{1,0:T(8,128)(2,1)S(1)} %collective-permute-done.25.refs_10_), channel_id=1, source_target_pairs={{0,4},{4,0},{8,12},{12,8},{1,5},{5,1},{9,13},{13,9},{2,6},{6,2},{1... | collective-permute-start | bytes 3981320 | tf_op jit(solution)/shard_map/ppermute | solution.py:52
  240.2 40.2 %collective-permute-start.44 = (bf16[2,2,4,24,3840]{4,3,2,1,0:T(8,128)(2,1)}, bf16[2,2,4,24,3840]{4,3,2,1,0:T(8,128)(2,1)}, u32[]{:S(2)}, u32[]{:S(2)}) collective-permute-start(bf16[2,2,4,24,3840]{4,3,2,1,0:T(8,128)(2,1)} %bitcast.230), channel_id=1, source_target_pairs={{0,4},{4,0},{8,12},{12,8},{1,5},{5,1},{9,13},{13,9},{2,6},{6,2},{1... | collective-permute-start | bytes 8847368 | tf_op jit(solution)/shard_map/ppermute | solution.py:52
  241.4 37.9 %collective-permute-start.43 = (bf16[1,2,4,96,768]{4,3,2,1,0:T(8,128)(2,1)S(1)}, bf16[1,2,4,96,768]{4,3,2,1,0:T(8,128)(2,1)S(1)}, u32[]{:S(2)}, u32[]{:S(2)}) collective-permute-start(bf16[1,2,4,96,768]{4,3,2,1,0:T(8,128)(2,1)S(1)} %constant_dynamic-slice_fusion.7), channel_id=1, source_target_pairs={{0,16},{16,0},{1,17},{17,1},{2,18},{18,2},{3,19},{19,3},{4,20},{20... | collective-permute-start | bytes 3538952 | tf_op jit(solution)/shard_map/ppermute | solution.py:740
  290.1 34.5 %collective-permute-start.48 = (bf16[1,2,4,24,3840]{4,3,2,1,0:T(8,128)(2,1)S(1)}, bf16[1,2,4,24,3840]{4,3,2,1,0:T(8,128)(2,1)S(1)}, u32[]{:S(2)}, u32[]{:S(2)}) collective-permute-start(bf16[1,2,4,24,3840]{4,3,2,1,0:T(8,128)(2,1)S(1)} %constant_dynamic-slice_fusion.6), channel_id=1, source_target_pairs={{0,16},{16,0},{1,17},{17,1},{2,18},{18,2},{3,19},{19,3},{4,20},{20... | collective-permute-start | bytes 4423688 | tf_op jit(solution)/shard_map/ppermute | solution.py:740
  290.9 28.7 %collective-permute-start.47 = (bf16[4,96,768]{2,1,0:T(8,128)(2,1)S(1)}, bf16[4,96,768]{2,1,0:T(8,128)(2,1)S(1)}, u32[]{:S(2)}, u32[]{:S(2)}) collective-permute-start(bf16[4,96,768]{2,1,0:T(8,128)(2,1)S(1)} %dynamic-slice_bitcast_fusion.1), channel_id=1, source_target_pairs={{0,8},{4,12},{8,0},{12,4},{1,9},{5,13},{9,1},{13,5},{2,10},{6,14},... | collective-permute-start | bytes 1769480 | tf_op jit(solution)/shard_map/ppermute | solution.py:52
  292.1 30.9 %collective-permute-start.46 = (bf16[512,768]{1,0:T(8,128)(2,1)S(1)}, bf16[512,768]{1,0:T(8,128)(2,1)S(1)}, u32[]{:S(2)}, u32[]{:S(2)}) collective-permute-start(bf16[512,768]{1,0:T(8,128)(2,1)S(1)} %get-tuple-element.290), channel_id=1, source_target_pairs={{0,8},{4,12},{8,0},{12,4},{1,9},{5,13},{9,1},{13,5},{2,10},{6,14},... | collective-permute-start | bytes 2359304 | tf_op jit(solution)/shard_map/ppermute | solution.py:52
  332.9 32.1 %collective-permute-start.52 = (bf16[4,24,3840]{2,1,0:T(8,128)(2,1)S(1)}, bf16[4,24,3840]{2,1,0:T(8,128)(2,1)S(1)}, u32[]{:S(2)}, u32[]{:S(2)}) collective-permute-start(bf16[4,24,3840]{2,1,0:T(8,128)(2,1)S(1)} %dynamic-slice_bitcast_fusion), channel_id=1, source_target_pairs={{0,8},{4,12},{8,0},{12,4},{1,9},{5,13},{9,1},{13,5},{2,10},{6,14},... | collective-permute-start | bytes 2211848 | tf_op jit(solution)/shard_map/ppermute | solution.py:52
  334.2 34.5 %collective-permute-start.50 = (bf16[512,768]{1,0:T(8,128)(2,1)S(1)}, bf16[512,768]{1,0:T(8,128)(2,1)S(1)}, u32[]{:S(2)}, u32[]{:S(2)}) collective-permute-start(bf16[512,768]{1,0:T(8,128)(2,1)S(1)} %get-tuple-element.312), channel_id=1, source_target_pairs={{0,8},{4,12},{8,0},{12,4},{1,9},{5,13},{9,1},{13,5},{2,10},{6,14},... | collective-permute-start | bytes 2359304 | tf_op jit(solution)/shard_map/ppermute | solution.py:52
  335.0 33.7 %collective-permute-start.51 = (bf16[512,768]{1,0:T(8,128)(2,1)S(1)}, bf16[512,768]{1,0:T(8,128)(2,1)S(1)}, u32[]{:S(2)}, u32[]{:S(2)}) collective-permute-start(bf16[512,768]{1,0:T(8,128)(2,1)S(1)} %add_convert_fusion.8), channel_id=1, source_target_pairs={{0,2},{1,0},{3,1},{2,3},{4,6},{5,4},{7,5},{6,7},{8,10},{9,8},{11,9... | collective-permute-start | bytes 2359304 | tf_op jit(solution)/shard_map/ppermute | solution.py:65
  372.6 41.2 %collective-permute-start.59 = (bf16[24,3840]{1,0:T(8,128)(2,1)S(1)}, bf16[24,3840]{1,0:T(8,128)(2,1)S(1)}, u32[]{:S(2)}, u32[]{:S(2)}) collective-permute-start(bf16[24,3840]{1,0:T(8,128)(2,1)S(1)} %get-tuple-element.394), channel_id=1, source_target_pairs={{0,2},{1,0},{3,1},{2,3},{4,6},{5,4},{7,5},{6,7},{8,10},{9,8},{11,9... | collective-permute-start | bytes 552968 | tf_op jit(solution)/shard_map/ppermute | solution.py:65
  372.7 41.1 %collective-permute-start.60 = (bf16[24,3840]{1,0:T(8,128)(2,1)S(1)}, bf16[24,3840]{1,0:T(8,128)(2,1)S(1)}, u32[]{:S(2)}, u32[]{:S(2)}) collective-permute-start(bf16[24,3840]{1,0:T(8,128)(2,1)S(1)} %get-tuple-element.393), channel_id=1, source_target_pairs={{0,3},{1,2},{3,0},{2,1},{4,7},{5,6},{7,4},{6,5},{8,11},{9,10},{11,... | collective-permute-start | bytes 552968 | tf_op jit(solution)/shard_map/ppermute | solution.py:65
  376.7 37.1 %collective-permute-start.61 = (bf16[24,3840]{1,0:T(8,128)(2,1)S(1)}, bf16[24,3840]{1,0:T(8,128)(2,1)S(1)}, u32[]{:S(2)}, u32[]{:S(2)}) collective-permute-start(bf16[24,3840]{1,0:T(8,128)(2,1)S(1)} %get-tuple-element.392), channel_id=1, source_target_pairs={{0,1},{1,3},{3,2},{2,0},{4,5},{5,7},{7,6},{6,4},{8,9},{9,11},{11,1... | collective-permute-start | bytes 552968 | tf_op jit(solution)/shard_map/ppermute | solution.py:65
  376.7 37.1 %collective-permute-start.57 = (bf16[512,768]{1,0:T(8,128)(2,1)S(1)}, bf16[512,768]{1,0:T(8,128)(2,1)S(1)}, u32[]{:S(2)}, u32[]{:S(2)}) collective-permute-start(bf16[512,768]{1,0:T(8,128)(2,1)S(1)} %get-tuple-element.332), channel_id=1, source_target_pairs={{0,8},{4,12},{8,0},{12,4},{1,9},{5,13},{9,1},{13,5},{2,10},{6,14},... | collective-permute-start | bytes 2359304 | tf_op jit(solution)/shard_map/ppermute | solution.py:52
  377.9 35.9 %collective-permute-start.58 = (bf16[512,768]{1,0:T(8,128)(2,1)S(1)}, bf16[512,768]{1,0:T(8,128)(2,1)S(1)}, u32[]{:S(2)}, u32[]{:S(2)}) collective-permute-start(bf16[512,768]{1,0:T(8,128)(2,1)S(1)} %add_convert_fusion.5), channel_id=1, source_target_pairs={{0,2},{1,0},{3,1},{2,3},{4,6},{5,4},{7,5},{6,7},{8,10},{9,8},{11,9... | collective-permute-start | bytes 2359304 | tf_op jit(solution)/shard_map/ppermute | solution.py:65
  (141 other events, 1823.3 us)
